TPU v7x, 256 devices: a whole 4x4x8 slice. The times are simulated.
256 devices in a mesh: row: 32 (over y, z_hi, core), col: 8 (over z_lo, x).
Axes of the slice: x: 4, y: 4, z: 8 (z_hi: 4, z_lo: 2; z = z_hi * 2 + z_lo), core: 2. Of those that a mesh axis runs over, the one named last changes fastest.
Arguments:
- c_matrix: bfloat16 [8, 768, 6144], P(None, 'row', 'col'), may hold values from -6 to 6
- beta_values: bfloat16 [1, 48, 6, 128, 128], P(None, 'col'), may hold values from -0.21875 to 0.21875
- beta_rows: int32 [1, 48, 6], P(None, 'col'), may hold values from 0 to 47, as said below
- alpha_values: bfloat16 [1, 8, 32, 32, 24, 24], P(None, None, 'row'), may hold values from -0.21875 to 0.21875
- alpha_rows: int32 [1, 8, 32, 32], P(None, None, 'row'), may hold values from 0 to 255, as said below
- gaps: float32 [8, 768, 6144], P(None, 'row', 'col'), may hold values from 0.5 to 4
Outputs:
- update: float32 [8, 768, 6144], P(None, 'row', 'col')
Inputs may be any that keep to these rules, and one draw needn't show every extreme that they name: For every k and tile column j, beta_rows[k, j] lists 6 distinct tile rows and its first entry is j. For every k, g, r, alpha_rows[k, g, r] lists 32 distinct tile rows and its first entry is the tile column g * 32 + r.
All inputs are finite; a program needn't handle non-finite values.
Results may differ from a plain program's by a relative error of at most 0.0029.
Values may be sent and summed in bfloat16 or wider, within the bound.
No kernel may reach another device: no remote copies, remote signals or barrier semaphores. Data moves between devices by JAX's collectives and lax.ppermute only.
A program may use at most 128 MiB of HBM per device.

v0:
```python
import jax
import jax.numpy as jnp
from jax import lax
from jax.sharding import PartitionSpec as P


def beta_products(gathered, beta_values, beta_rows):
    groups, stretch_rows, columns = gathered.shape
    local_rows = groups * stretch_rows
    tile_width = beta_values.shape[-1]
    tiled = gathered.reshape(local_rows, columns // tile_width, tile_width)
    picked = tiled[:, beta_rows]
    product = jnp.einsum(
        "rkjzt,kjzts->krjs", picked, beta_values, preferred_element_type=jnp.float32
    )
    return product.astype(jnp.bfloat16).reshape(beta_values.shape[0] * local_rows, -1)


def alpha_blocks(alpha_values, alpha_rows, row_devices, pattern):
    alpha_tiles = alpha_values[:, :, 0]
    alpha_lists = alpha_rows[:, :, 0]
    groups = alpha_lists.shape[1]
    tile_count = groups * row_devices
    onehot = (alpha_lists[..., None] == jnp.arange(tile_count, dtype=jnp.int32)).astype(
        jnp.bfloat16
    )
    onehot = onehot.reshape(onehot.shape[:3] + (groups, row_devices))
    spread = jnp.einsum(pattern, onehot, alpha_tiles, preferred_element_type=jnp.float32)
    return spread.astype(jnp.bfloat16).reshape(tile_count * alpha_tiles.shape[-1], -1)


def per_device(c_matrix, beta_values, beta_rows, alpha_values, alpha_rows, gaps):
    row_devices = lax.axis_size("row")
    groups, stretch_rows, columns = c_matrix.shape
    gathered = lax.all_gather(c_matrix, "col", axis=2, tiled=True)
    x_stack = beta_products(gathered, beta_values, beta_rows)
    spread = alpha_blocks(alpha_values, alpha_rows, row_devices, "kgzab,kgzuv->baukgv")
    own_part = lax.psum_scatter(
        jnp.dot(spread, x_stack, preferred_element_type=jnp.float32),
        "row",
        scatter_dimension=0,
        tiled=True,
    )
    own_part = own_part.reshape(groups, stretch_rows, columns)
    first_section = lax.all_to_all(own_part, "col", split_axis=0, concat_axis=0, tiled=True)
    second_section = lax.all_to_all(first_section, "row", split_axis=2, concat_axis=1, tiled=True)
    mirrored = jnp.transpose(second_section, (0, 2, 1))
    return (own_part + mirrored) / gaps


def solution(mesh):
    placed = (
        P(None, "row", "col"),
        P(None, "col", None, None, None),
        P(None, "col", None),
        P(None, None, "row", None, None, None),
        P(None, None, "row", None),
        P(None, "row", "col"),
    )
    return jax.shard_map(
        per_device, mesh=mesh, in_specs=placed, out_specs=P(None, "row", "col"), check_vma=False
    )
```

profile of v0, /device:TPU:1, one launch (start us, length us, event | category | flops | bytes accessed | tf_op | source)
XLA Modules:
  0.0 325.7 jit_solution(8095739388453561755)
XLA Ops:
  6.5 0.0 copy-start
  6.5 0.0 all-gather.2.cloned.1.call-start
  6.5 0.7 all-gather.2.cloned.1.call-update
  7.3 0.0 reduce-scatter.2.cloned.1.call-start
  7.3 0.5 copy-done
  7.8 5.7 %convert_bitcast_fusion = bf16[32,8,24,1,8,24]{0,5,2,1,4,3:T(8,128)(2,1)} fusion(bf16[1,8,1,32,24,24]{3,5,4,2,1,0:T(8,128)(2,1)S(1)} %copy-done, s32[8,32]{1,0:T(8,128)S(1)} %multiply_add_fusion, s32[8,32]{1,0:T(8,128)} %bitcast.77), kind=kOutput, calls=%fused_computation.1 | convolution fusion | flops 76742656 | bytes 2656256 | tf_op jit(solution)/shard_map/kgzab,kgzuv->baukgv/dot_general | solution.py:28
  13.5 21.3 %copy.16 = bf16[32,8,24,1,8,24]{2,1,0,5,4,3:T(8,128)(2,1)} copy(bf16[32,8,24,1,8,24]{0,5,2,1,4,3:T(8,128)(2,1)} %convert_bitcast_fusion) | data formatting | bytes 4718592 | tf_op jit(solution)/shard_map/convert_element_type | solution.py:29
  34.8 0.0 copy-start.5
  34.8 19.3 %reshape.35 = bf16[6144,192]{0,1:T(8,128)(2,1)S(1)} reshape(bf16[32,8,24,1,8,24]{2,1,0,5,4,3:T(8,128)(2,1)} %copy.16) | data formatting | bytes 4718592 | tf_op jit(solution)/shard_map/reshape | solution.py:29
  54.1 0.0 copy-done.5
  54.1 0.1 reshape.43
  54.2 0.0 all-gather.2.cloned.1.call-done
  54.3 2.2 copy.27
  56.4 2.0 copy.17
  58.5 0.0 copy-start.3
  58.5 3.9 %gather_fusion = bf16[36,192,128]{2,1,0:T(8,128)(2,1)} fusion(bf16[192,48,128]{2,0,1:T(8,128)(2,1)} %copy.17, s32[1024]{0:T(1024)S(1)} %pad_clamp_fusion), kind=kCustom, calls=%fused_computation | custom fusion | bytes 3539088 | tf_op jit(solution)/shard_map/gather | solution.py:12
  62.3 0.0 copy-done.3
  62.3 2.1 fusion.3
  64.4 0.2 copy.18
  64.6 7.9 %fusion.11 = f32[6144,768]{1,0:T(8,128)} fusion(bf16[6144,192]{0,1:T(8,128)(2,1)S(1)} %reshape.35, bf16[24,8,6,128]{3,2,1,0:T(8,128)(2,1)S(1)} %bitcast.76), kind=kOutput, calls=%fused_computation.13 | convolution fusion | flops 1811939328 | bytes 21528576 | tf_op jit(solution)/shard_map/dot_general | solution.py:39
  72.6 0.0 reduce-scatter.2.cloned.1.call-update
  72.6 181.7 %reduce-scatter.2.cloned.1.call-done = f32[192,768]{1,0:T(8,128)} async-done(((f32[6144,768]{1,0:T(8,128)}), f32[192,768]{1,0:T(8,128)}) %reduce-scatter.2.cloned.1.call-update) | async-done | bytes 589840 | tf_op jit(solution)/shard_map/reduce_scatter | solution.py:38
  254.3 13.1 %all_to_all.23 = f32[8,24,768]{2,1,0:T(8,128)S(1)} all-to-all(f32[8,24,768]{2,1,0:T(8,128)} %bitcast.74), channel_id=1, replica_groups=mesh['row'=32,'col'=8] {'col'}, dimensions={0} | all-to-all | bytes 1179648 | tf_op jit(solution)/shard_map/all_to_all | solution.py:45
  267.4 2.2 copy.19
  269.6 3.9 %reshape.56 = f32[32,1,4608]{2,1,0:T(1,128)S(1)} reshape(f32[768,8,24]{2,1,0:T(8,128)} %bitcast.69) | data formatting | bytes 1179648
  273.4 29.2 %all_to_all.24 = f32[32,1,4608]{2,1,0:T(1,128)S(1)} all-to-all(f32[32,1,4608]{2,1,0:T(1,128)S(1)} %reshape.56), channel_id=1, replica_groups=mesh['row'=32,'col'=8] {'row'}, dimensions={0} | all-to-all | bytes 1179648 | tf_op jit(solution)/shard_map/all_to_all | solution.py:46
  302.6 0.5 broadcast.16
  303.1 2.0 reduce.2
  305.2 3.9 %reshape.57 = f32[768,8,24]{2,1,0:T(8,128)} reshape(f32[32,4608]{1,0:T(8,128)S(1)} %reduce.2) | data formatting | bytes 1179648
  309.1 0.0 copy-start.1
  309.1 5.5 %copy.21 = f32[8,32,24,24]{2,1,3,0:T(8,128)} copy(f32[8,32,24,24]{2,0,3,1:T(8,128)} %bitcast.70) | data formatting | bytes 1179648 | tf_op jit(solution)/shard_map/all_to_all | solution.py:46
  314.6 0.0 copy-start.2
  314.6 0.0 copy-start.4
  314.6 3.3 %all_to_all.20 = f32[8,768,24]{1,2,0:T(8,128)S(1)} reshape(f32[8,32,24,24]{2,1,3,0:T(8,128)} %copy.21) | data formatting | bytes 1179648 | tf_op jit(solution)/shard_map/all_to_all | solution.py:46
  317.9 0.0 copy-done.2
  317.9 0.0 copy-done.4
  317.9 0.9 fusion.8
  318.8 0.0 copy-done.1
  (3 shorter events, 0.0 us)
Async XLA Ops:
  6.5 1.3 copy-start
  6.5 47.7 %all-gather.2.cloned.1.call-start = ((), (), s32[]{:S(2)}) async-start(), calls=%async_computation.3 | async-start | bytes 2654208 | tf_op jit(solution)/shard_map/all_gather | solution.py:35
  7.3 247.1 %reduce-scatter.2.cloned.1.call-start = ((), (), s32[]{:S(2)}) async-start(), calls=%async_computation.4 | async-start | bytes 19464192 | tf_op jit(solution)/shard_map/reduce_scatter | solution.py:38
  34.8 19.3 %copy-start.5 = (s32[1,6,6]{2,0,1:T(1,128)S(1)}, s32[1,6,6]{2,0,1:T(1,128)}, u32[]{:S(2)}) copy-start(s32[1,6,6]{2,0,1:T(1,128)} %param.8) | copy-start | bytes 436
  58.5 3.9 %copy-start.3 = (bf16[1,6,6,128,128]{4,3,2,1,0:T(8,128)(2,1)S(1)}, bf16[1,6,6,128,128]{4,3,2,1,0:T(8,128)(2,1)}, u32[]{:S(2)}) copy-start(bf16[1,6,6,128,128]{4,3,2,1,0:T(8,128)(2,1)} %param.7) | copy-start | bytes 3538948
  309.1 9.8 %copy-start.1 = (bf16[1,8,1,32,24,24]{3,5,4,2,1,0:T(8,128)(2,1)S(1)}, bf16[1,8,1,32,24,24]{3,5,4,2,1,0:T(8,128)(2,1)}, u32[]{:S(2)}) copy-start(bf16[1,8,1,32,24,24]{3,5,4,2,1,0:T(8,128)(2,1)} %param.9) | copy-start | bytes 884740
  314.6 3.4 %copy-start.2 = (f32[192,768]{1,0:T(8,128)S(1)}, f32[192,768]{1,0:T(8,128)}, u32[]{:S(2)}) copy-start(f32[192,768]{1,0:T(8,128)} %reduce-scatter.2.cloned.1.call-done) | copy-start | bytes 1769476
  314.6 3.4 %copy-start.4 = (f32[8,24,768]{2,1,0:T(8,128)S(1)}, f32[8,24,768]{2,1,0:T(8,128)}, u32[]{:S(2)}) copy-start(f32[8,24,768]{2,1,0:T(8,128)} %param.11) | copy-start | bytes 1769476
Sparse Core Ops, SparseCore 0:
  9.2 43.8 all-gather.1
  72.7 181.5 reduce-scatter.1
where the time goes:
time: 327 us; the launch traced here: 326 us
  waiting for transfers between devices  182 us (56%)
  local copies, waits for them, and re-layouts  68.7 us (21%)
  blocking collectives  42.2 us (13%)
  matrix products  15.7 us (5%)
  between operations  13.5 us (4%)
    reduce_scatter x1, waiting for transfers between devices, per_device(): lax.psum_scatter(jnp.dot(spread, x_stack, preferred_element_type=jnp.floa...  182 us
    all_to_all x1, blocking collectives, per_device(): lax.all_to_all(first_section, 'row', split_axis=2, concat_axis=1, tiled=T...  29.2 us
    convert_element_type x1, local copies, waits for them, and re-layouts, alpha_blocks(): spread.astype(jnp.bfloat16).reshape(tile_count * alpha_tiles.shape[-1], -1)  21.3 us
    reshape x1, local copies, waits for them, and re-layouts, alpha_blocks(): spread.astype(jnp.bfloat16).reshape(tile_count * alpha_tiles.shape[-1], -1)  19.3 us
    all_to_all x1, blocking collectives, per_device(): lax.all_to_all(own_part, 'col', split_axis=0, concat_axis=0, tiled=True)  13.1 us
    unnamed x15, local copies, waits for them, and re-layouts  10.4 us
    all_to_all x3, local copies, waits for them, and re-layouts, per_device(): lax.all_to_all(first_section, 'row', split_axis=2, concat_axis=1, tiled=T...  9.32 us
    dot_general x1, matrix products, per_device(): jnp.dot(spread, x_stack, preferred_element_type=jnp.float32)  7.93 us
  transfers between devices with their start and end apart: 2, of which 1 were waited for; matrix products, arithmetic and copies ran while one was open for 14% of the time, Pallas kernels for 0%

commit v1 on v0

v1 whole, which is shorter than its diff:
```python
import jax
import jax.numpy as jnp
from jax import lax
from jax.experimental import pallas as pl
from jax.experimental.pallas import tpu as pltpu
from jax.sharding import Mesh, PartitionSpec as P

BF = jnp.bfloat16
F32 = jnp.float32
NY, NZ, NC, NL, NX = 4, 4, 2, 2, 4
NH = NZ * NC
G, U, RT = 8, 24, 32
ROWS = G * U
COLS = 768
PART = COLS // NH
STEPS = (0, 1, -1, 2)
HBM = pl.BlockSpec(memory_space=pltpu.HBM)
VM = pl.BlockSpec(memory_space=pltpu.VMEM)
SM = pl.BlockSpec(memory_space=pltpu.SMEM)


def shift_x(a, k):
    return lax.ppermute(a, "x", [(i, (i + k) % NX) for i in range(NX)])


def flip_zl(a):
    return lax.ppermute(a, "zl", [(0, 1), (1, 0)])


def flip_core(a):
    return lax.ppermute(a, "core", [(0, 1), (1, 0)])


def shift_y(a, k):
    return lax.ppermute(a, "y", [(i, (i + k) % NY) for i in range(NY)])


def cross_z(a):
    moves = []
    for zh in range(NZ):
        moves.append((zh * 2, (zh - 1) % NZ * 2 + 1))
        moves.append((zh * 2 + 1, (zh + 1) % NZ * 2))
    return lax.ppermute(a, ("zh", "zl"), moves)


def send_step(a, label):
    moves = []
    for zh in range(NZ):
        for zl in range(NL):
            to = (zh + (1 - 2 * zl) * STEPS[label]) % NZ
            moves.append((zh * 2 + zl, to * 2 + zl))
    return lax.ppermute(a, ("zh", "zl"), moves)


def exchange(payloads):
    direct = [payloads[0]] + [send_step(payloads[k], k) for k in range(1, NZ)]
    return direct + [flip_core(a) for a in direct]


def pack(pieces):
    lane = lax.broadcasted_iota(jnp.int32, pieces[0].shape, 1)
    p0, r1, r2, r3 = pieces[0], *(pltpu.roll(pieces[i], 128 - 32 * i, 1) for i in (1, 2, 3))
    return jnp.concatenate(
        [
            jnp.where(lane < 96, p0, r1),
            jnp.where(lane < 64, r1, r2),
            jnp.where(lane < 32, r2, r3),
        ],
        axis=1,
    )


def unpack(packed):
    t0, t1, t2 = (packed[:, i * 128 : (i + 1) * 128] for i in range(3))
    lane = lax.broadcasted_iota(jnp.int32, t0.shape, 1)
    return [
        t0,
        pltpu.roll(jnp.where(lane < 96, t1, t0), 32, 1),
        pltpu.roll(jnp.where(lane < 64, t2, t1), 64, 1),
        pltpu.roll(t2, 96, 1),
    ]


def gather_c(own):
    over, left, right = flip_zl(own), shift_x(own, 1), shift_x(own, -1)
    over_right, far, over_left = shift_x(over, -1), shift_x(left, 1), flip_zl(left)
    over_far = shift_x(over_right, -1)
    return [own, right, far, left, over, over_right, over_far, over_left]


def x_kernel(slots, *refs):
    blocks, (b_ref, perm_ref), outs = refs[:8], refs[8:10], refs[10 : 10 + NZ]
    cbuf, xs, sems = refs[10 + NZ :]
    copies = [pltpu.make_async_copy(blocks[k], cbuf.at[k], sems.at[k]) for k in range(8)]
    for cp in copies:
        cp.start()
    for cp in copies:
        cp.wait()
    for j in range(6):
        picked = []
        for z in range(6):
            slot = slots[j * 6 + z]
            k, t = slot // 6, slot % 6
            picked.append(cbuf[k, :, pl.ds(pl.multiple_of(t * 128, 128), 128)])
        lhs = jnp.concatenate(picked, axis=1)
        xs[:, j * 128 : (j + 1) * 128] = jnp.dot(
            lhs, b_ref[j], preferred_element_type=F32
        ).astype(BF)
    for label in range(NH):
        piece = jnp.dot(
            xs[...], perm_ref[:, label * 128 : (label + 1) * 128], preferred_element_type=F32
        )
        outs[label // 2][label % 2] = pack([piece[i * 48 : (i + 1) * 48] for i in range(4)]).astype(BF)


def a_kernel(lists, *refs):
    ps, xs, (own_ref, s1, s2, s3) = refs[:8], refs[8:16], refs[16:20]
    acc, pbuf, xbuf, res, psem, xsem = refs[20:]
    pc, xc = [], []
    for i in range(NH):
        pc.append(pltpu.make_async_copy(ps[i].at[pl.ds(0, ROWS)], pbuf.at[i], psem.at[i]))
        xc.append(pltpu.make_async_copy(xs[i % 2 * NZ + i // 2].at[i % 2], xbuf.at[i], xsem.at[i]))
    for cp in pc + xc:
        cp.start()
    acc[...] = jnp.zeros_like(acc)
    for cp in pc + xc:
        cp.wait()
    rows = lax.broadcasted_iota(jnp.int32, (ROWS, 128), 0)
    blank = jnp.zeros((64, 256), F32)

    @pl.loop(0, NH)
    def _(label):
        x = jnp.concatenate(unpack(xbuf[label].astype(F32)), axis=0)
        for pair in range(4):
            sides = []
            for g in (2 * pair, 2 * pair + 1):
                keep = (rows >= g * U) & (rows < (g + 1) * U)
                sides.append(jnp.where(keep, x, 0.0))
            diag = jnp.concatenate(sides, axis=1)
            even = jnp.concatenate([diag, blank], axis=0).astype(BF)
            odd = jnp.concatenate([blank, diag], axis=0).astype(BF)
            for q in range(4):
                first = q * ROWS - q % 2 * 64
                res[pair % 2, q * ROWS : (q + 1) * ROWS] = jnp.dot(
                    pbuf[label, :, first : first + 256],
                    odd if q % 2 else even,
                    preferred_element_type=F32,
                )
            for side in range(2):
                g = 2 * pair + side
                for batch in range(4):
                    spots, sums = [], []
                    for z in range(batch * 8, batch * 8 + 8):
                        t = lists[label * (G * RT) + g * RT + z]
                        spot = pl.ds(pl.multiple_of(t * U, 8), U)
                        spots.append(spot)
                        sums.append(
                            acc[spot, :]
                            + res[pair % 2, z * U : (z + 1) * U, side * 128 : (side + 1) * 128]
                        )
                    for spot, total in zip(spots, sums):
                        acc[spot, :] = total

    size = ROWS * NH
    own_ref[...] = acc[0:size]
    quarter = size // 4
    for k, ref in enumerate((s1, s2, s3)):
        first = (k + 1) * size
        ref[...] = pack(
            [acc[first + i * quarter : first + (i + 1) * quarter] for i in range(4)]
        ).astype(BF)


def y_kernel(dests, own, r1, r2, r3, ident, *refs):
    ds, m_ref, y = refs[:NZ], refs[NZ], refs[NZ + 1]
    quarter = ROWS * NH // 4
    parts = [unpack(r[...].astype(F32)) for r in (r1, r2, r3)]
    for i in range(4):
        span = slice(i * quarter, (i + 1) * quarter)
        y[span, :] = own[span, :] + parts[0][i] + parts[1][i] + parts[2][i]
    for label in range(NH):
        h = dests[label]
        pieces = []
        for g in range(G):
            pieces.append(y[pl.ds(pl.multiple_of((g * NH + h) * U, 8), U), :])
        pairs = [jnp.concatenate(pieces[2 * i : 2 * i + 2], axis=0) for i in range(4)]
        ds[label // 2][label % 2] = pack(pairs).astype(BF)
    for g in range(G):
        block = y[g * ROWS : (g + 1) * ROWS, :].astype(BF)
        turned = lax.dot_general(
            ident[...], block, (((1,), (1,)), ((), ())), preferred_element_type=F32
        )
        for ys in range(NY):
            m_ref[ys * G + g] = turned[ys * U : (ys + 1) * U, :].astype(BF)


def out_kernel(*refs):
    ds, (m_ref, perm_ref, gaps, out_ref) = refs[:NH], refs[NH:]
    total = jnp.zeros((ROWS, COLS), F32)
    for label in range(NH):
        packed = ds[label % 2 * NZ + label // 2][label % 2].astype(F32)
        piece = jnp.concatenate(unpack(packed), axis=0).astype(BF)
        total = total + jnp.dot(piece, perm_ref[label], preferred_element_type=F32)
    row = lax.broadcasted_iota(jnp.int32, (ROWS, COLS), 0)
    col = lax.broadcasted_iota(jnp.int32, (ROWS, COLS), 1)
    for ys in range(NY):
        place = jnp.where(col == row + ys * ROWS, 1.0, 0.0).astype(BF)
        total = total + jnp.dot(m_ref[ys], place, preferred_element_type=F32)
    out_ref[...] = total / gaps[...]


def params():
    return pltpu.CompilerParams(vmem_limit_bytes=50 * 1024 * 1024)


def per_device(c_matrix, beta_values, beta_rows, alpha_values, alpha_rows, gaps):
    y, zh, core = lax.axis_index("y"), lax.axis_index("zh"), lax.axis_index("core")
    zl, x = lax.axis_index("zl"), lax.axis_index("x")
    sign = 1 - 2 * zl
    steps = jnp.array([s for s in STEPS for _ in range(NC)], jnp.int32)
    flips = jnp.array([0, 1] * NZ, jnp.int32)
    h_to = (zh + sign * steps) % NZ * NC + (core ^ flips)
    h_from = (zh - sign * steps) % NZ * NC + (core ^ flips)

    tiles = alpha_values[0, :, 0].reshape(G, 4, 8, U, U)
    tiles = jnp.transpose(tiles, (2, 3, 1, 0, 4)).reshape(ROWS, COLS)
    listed = jnp.pad(alpha_rows[0, :, 0].astype(BF).reshape(1, G * RT), ((0, 7), (0, COLS - G * RT)))
    tiles = jnp.concatenate([tiles, listed], axis=0)
    near = cross_z(tiles)
    next_ = flip_zl(near)
    far = cross_z(next_)
    a_parts = []
    for part in (tiles, near, next_, far):
        a_parts += [part, flip_core(part)]
    lists = jnp.stack([a[ROWS, : G * RT] for a in a_parts]).astype(jnp.int32)
    tile_row = lists % RT
    lists = ((tile_row // NH - y) % NY) * (G * NH) + lists // RT * NH + tile_row % NH

    blocks = gather_c(c_matrix.reshape(ROWS, COLS))
    col_block = beta_rows[0] // 6
    slots = (((col_block // NX) ^ zl) * NX + (col_block % NX - x) % NX) * 6 + beta_rows[0] % 6
    lane = jnp.arange(128, dtype=jnp.int32)
    place = jnp.where(lane < PART, lane // U * (NH * U) + lane % U, -COLS)
    cols = jnp.arange(COLS, dtype=jnp.int32)
    spread_to = (place[None, :] + h_to[:, None] * U).reshape(-1)
    perm_to = (cols[:, None] == spread_to[None, :]).astype(BF)
    perm_from = (cols[None, None, :] == (place[None, :] + h_from[:, None] * U)[:, :, None]).astype(BF)
    piece = jax.ShapeDtypeStruct((NC, ROWS // 4, 384), BF)
    x_out = pl.pallas_call(
        x_kernel,
        out_shape=[piece] * NZ,
        in_specs=[SM] + [HBM] * 8 + [VM] * 2,
        out_specs=[VM] * NZ,
        scratch_shapes=[
            pltpu.VMEM((8, ROWS, COLS), BF),
            pltpu.VMEM((ROWS, COLS), BF),
            pltpu.SemaphoreType.DMA((8,)),
        ],
        compiler_params=params(),
        name="beta_product",
    )(slots.reshape(-1), *blocks, beta_values[0].reshape(6, 768, 128), perm_to)
    x_parts = exchange(x_out)

    size = ROWS * NH
    part = jax.ShapeDtypeStruct((size // 4, 384), BF)
    own, s1, s2, s3 = pl.pallas_call(
        a_kernel,
        out_shape=[jax.ShapeDtypeStruct((size, 128), F32), part, part, part],
        in_specs=[SM] + [HBM] * 16,
        out_specs=[VM] * 4,
        scratch_shapes=[
            pltpu.VMEM((size * NY, 128), F32),
            pltpu.VMEM((NH, ROWS, COLS), BF),
            pltpu.VMEM((NH, ROWS // 4, 384), BF),
            pltpu.VMEM((2, RT * U, 256), F32),
            pltpu.SemaphoreType.DMA((NH,)),
            pltpu.SemaphoreType.DMA((NH,)),
        ],
        compiler_params=params(),
        name="alpha_product",
    )(lists.reshape(-1), *a_parts, *x_parts)
    r1, r2, r3 = shift_y(s1, 1), shift_y(s2, 2), shift_y(s3, 3)

    y_out = pl.pallas_call(
        y_kernel,
        out_shape=[piece] * NZ + [jax.ShapeDtypeStruct((NY * G, U, ROWS), BF)],
        in_specs=[SM] + [VM] * 5,
        out_specs=[VM] * (NZ + 1),
        scratch_shapes=[pltpu.VMEM((size, 128), F32)],
        compiler_params=params(),
        name="y_sum",
    )(h_to, own, r1, r2, r3, jnp.eye(128, dtype=BF))
    mirrored = lax.all_to_all(y_out[NZ], ("y", "zl", "x"), split_axis=0, concat_axis=0, tiled=True)
    d_parts = exchange(y_out[:NZ])
    out = pl.pallas_call(
        out_kernel,
        out_shape=jax.ShapeDtypeStruct((ROWS, COLS), F32),
        in_specs=[VM] * (NH + 3),
        out_specs=VM,
        compiler_params=params(),
        name="combine",
    )(*d_parts, mirrored.reshape(NY, ROWS, ROWS), perm_from, gaps.reshape(ROWS, COLS))
    return out.reshape(gaps.shape)


def solution(mesh):
    fine = Mesh(mesh.devices.reshape(NY, NZ, NC, NL, NX), ("y", "zh", "core", "zl", "x"))
    row, col = ("y", "zh", "core"), ("zl", "x")
    placed = (
        P(None, row, col),
        P(None, col, None, None, None),
        P(None, col, None),
        P(None, None, row, None, None, None),
        P(None, None, row, None),
        P(None, row, col),
    )
    return jax.shard_map(
        per_device, mesh=fine, in_specs=placed, out_specs=P(None, row, col), check_vma=False
    )
```

time: 327 us -> 127 us (0.39)
  waiting for transfers between devices: 182 us -> 29.4 us
  starting transfers between devices: 0.04 us -> 60.2 us
  local copies, waits for them, and re-layouts: 68.7 us -> 15 us
  blocking collectives: 42.2 us -> 0 us
  Pallas kernels: 0 us -> 17.8 us
  matrix products: 15.7 us -> 0 us
  between operations: 13.5 us -> 0.29 us
    reduce_scatter x1 -> x0, waiting for transfers between devices: 182 us -> none  [per_device(): lax.psum_scatter(jnp.dot(spread, x_stack, preferred_element_type=jnp.floa...]
    ppermute x0 -> x31, starting transfers between devices: none -> 52.8 us  [the longest x12 21.4 us: flip_core(): return lax.ppermute(a, 'core', [(0, 1), (1, 0)])]
    all_to_all x2 -> x0, blocking collectives: 42.2 us -> none  [the longest x1 29.2 us: per_device(): lax.all_to_all(first_section, 'row', split_axis=2, concat_axis=1, tiled=T...]
    ppermute x0 -> x31, waiting for transfers between devices: none -> 29.4 us  [the longest x3 12.4 us: shift_y(): return lax.ppermute(a, 'y', [(i, (i + k) % NY) for i in range(NY)])]
    convert_element_type x2 -> x1, local copies, waits for them, and re-layouts: 21.5 us -> 0.09 us  [per_device(): alpha_rows[0, :, 0].astype(BF).reshape(1, G * RT)]
    reshape x2 -> x1, local copies, waits for them, and re-layouts: 21.3 us -> 2.81 us  [per_device(): tiles = jnp.transpose(tiles, (2, 3, 1, 0, 4)).reshape(ROWS, COLS)]
    pallas_call x0 -> x4, Pallas kernels: none -> 17.8 us  [the longest x1 9.21 us: per_device(): pl.pallas_call(a_kernel, out_shape=[jax.ShapeDtypeStruct((size, 128), F32...]
    dot_general x3 -> x0, matrix products: 15.7 us -> none  [the longest x1 7.93 us: per_device(): jnp.dot(spread, x_stack, preferred_element_type=jnp.float32)]
  transfers between devices with their start and end apart: 2 -> 32, of which waited for: 1 -> 9; matrix products, arithmetic and copies ran while one was open for 14% -> 4% of each run, Pallas kernels for 0% -> 4%
where the time goes in v1:
time: 127 us; the launch traced here: 126 us
  starting transfers between devices  60.2 us (47%)
  waiting for transfers between devices  29.4 us (23%)
  Pallas kernels  17.8 us (14%)
  local copies, waits for them, and re-layouts  15 us (12%)
  other arithmetic  3.63 us (3%)
    ppermute x12, starting transfers between devices, flip_core(): return lax.ppermute(a, 'core', [(0, 1), (1, 0)])  21.4 us
    ppermute x3, waiting for transfers between devices, shift_y(): return lax.ppermute(a, 'y', [(i, (i + k) % NY) for i in range(NY)])  12.4 us
    unnamed x38, local copies, waits for them, and re-layouts  9.42 us
    pallas_call x1, Pallas kernels, per_device(): pl.pallas_call(a_kernel, out_shape=[jax.ShapeDtypeStruct((size, 128), F32...  9.21 us
    ppermute x6, starting transfers between devices, send_step(): return lax.ppermute(a, ('zh', 'zl'), moves)  8.85 us
    ppermute x2, starting transfers between devices, cross_z(): return lax.ppermute(a, ('zh', 'zl'), moves)  8.53 us
    ppermute x5, starting transfers between devices, shift_x(): return lax.ppermute(a, 'x', [(i, (i + k) % NX) for i in range(NX)])  7.91 us
    all_to_all x1, starting transfers between devices, per_device(): lax.all_to_all(y_out[NZ], ('y', 'zl', 'x'), split_axis=0, concat_axis=0,...  7.34 us
  transfers between devices with their start and end apart: 32, of which 9 were waited for; matrix products, arithmetic and copies ran while one was open for 4% of the time, Pallas kernels for 4%

profile of v1, /device:TPU:1, one launch (start us, length us, event | category | flops | bytes accessed | tf_op | source)
XLA Modules:
  0.0 126.3 jit_solution(5146710315282597083)
XLA Ops:
  0.0 0.7 convert_reduce_fusion
  0.7 0.1 convert_element_type.32
  0.8 2.0 %copy.10 = bf16[1,8,1,32,24,24]{5,4,3,1,2,0:T(8,128)(2,1)S(1)} copy(bf16[1,8,1,32,24,24]{3,5,4,2,1,0:T(8,128)(2,1)} %param.11) | data formatting | bytes 589824 | tf_op args[3]
  2.8 1.0 copy.11
  3.9 0.0 copy-start.16
  3.9 0.0 copy-start.17
  3.9 0.0 copy-start.14
  3.9 2.8 %reshape.107 = bf16[192,768]{1,0:T(8,128)(2,1)S(1)} reshape(bf16[8,24,4,8,24]{4,3,2,1,0:T(8,128)(2,1)S(1)} %copy.11) | data formatting | bytes 589824 | tf_op jit(solution)/shard_map/reshape | solution.py:226
  6.7 6.5 %collective-permute-start.1 = (bf16[200,768]{1,0:T(8,128)(2,1)S(1)}, bf16[200,768]{1,0:T(8,128)(2,1)S(1)}, u32[]{:S(2)}, u32[]{:S(2)}) collective-permute-start(bf16[200,768]{1,0:T(8,128)(2,1)S(1)} %fusion.3.refs_0_), channel_id=1, source_target_pairs={{0,52},{4,16},{16,4},{20,32},{32,20},{36,48},{48,36},{52,0},{1,53}... | collective-permute-start | bytes 921608 | tf_op jit(solution)/shard_map/ppermute | solution.py:43
  13.2 1.3 %collective-permute-start.8 = (bf16[192,768]{1,0:T(8,128)(2,1)S(1)}, bf16[192,768]{1,0:T(8,128)(2,1)S(1)}, u32[]{:S(2)}, u32[]{:S(2)}) collective-permute-start(bf16[192,768]{1,0:T(8,128)(2,1)S(1)} %bitcast.19), channel_id=1, source_target_pairs={{0,1},{1,2},{2,3},{3,0},{4,5},{5,6},{6,7},{7,4},{8,9},{9,10},{10,1... | collective-permute-start | bytes 884744 | tf_op jit(solution)/shard_map/ppermute | solution.py:23
  14.5 1.5 %collective-permute-start.7 = (bf16[192,768]{1,0:T(8,128)(2,1)S(1)}, bf16[192,768]{1,0:T(8,128)(2,1)}, u32[]{:S(2)}, u32[]{:S(2)}) collective-permute-start(bf16[192,768]{1,0:T(8,128)(2,1)S(1)} %bitcast.20), channel_id=1, source_target_pairs={{0,3},{1,0},{2,1},{3,2},{4,7},{5,4},{6,5},{7,6},{8,11},{9,8},{10,9... | collective-permute-start | bytes 884744 | tf_op jit(solution)/shard_map/ppermute | solution.py:23
  16.0 4.2 %collective-permute-done.1.refs_2_ = bf16[200,768]{1,0:T(8,128)(2,1)S(1)} collective-permute-done((bf16[200,768]{1,0:T(8,128)(2,1)S(1)}, bf16[200,768]{1,0:T(8,128)(2,1)S(1)}, u32[]{:S(2)}, u32[]{:S(2)}) %collective-permute-start.1) | collective-permute-done | bytes 307232 | tf_op jit(solution)/shard_map/ppermute | solution.py:43
  20.2 0.7 broadcast_add_fusion
  20.9 1.2 collective-permute-done.8.refs_3_
  22.1 1.1 collective-permute-start.13
  23.2 0.4 collective-permute-start.9
  23.6 2.3 %collective-permute-start.11 = (bf16[192,768]{1,0:T(8,128)(2,1)S(1)}, bf16[192,768]{1,0:T(8,128)(2,1)}, u32[]{:S(2)}, u32[]{:S(2)}) collective-permute-start(bf16[192,768]{1,0:T(8,128)(2,1)S(1)} %collective-permute-done.10.refs_4_), channel_id=1, source_target_pairs={{0,3},{1,0},{2,1},{3,2},{4,7},{5,4},{6,5},{7,6},{8,11},{9,8},{10,9... | collective-permute-start | bytes 884744 | tf_op jit(solution)/shard_map/ppermute | solution.py:23
  25.9 1.9 %collective-permute-done.3.refs_4_ = bf16[200,768]{1,0:T(8,128)(2,1)S(1)} collective-permute-done((bf16[200,768]{1,0:T(8,128)(2,1)S(1)}, bf16[200,768]{1,0:T(8,128)(2,1)S(1)}, u32[]{:S(2)}, u32[]{:S(2)}) %collective-permute-start.3) | collective-permute-done | bytes 307232 | tf_op jit(solution)/shard_map/ppermute | solution.py:27
  27.8 2.0 %collective-permute-start.5 = (bf16[200,768]{1,0:T(8,128)(2,1)S(1)}, bf16[200,768]{1,0:T(8,128)(2,1)S(1)}, u32[]{:S(2)}, u32[]{:S(2)}) collective-permute-start(bf16[200,768]{1,0:T(8,128)(2,1)S(1)} %collective-permute-done.3.refs_4_), channel_id=1, source_target_pairs={{0,52},{4,16},{16,4},{20,32},{32,20},{36,48},{48,36},{52,0},{1,53}... | collective-permute-start | bytes 921608 | tf_op jit(solution)/shard_map/ppermute | solution.py:43
  29.8 1.8 %fusion.refs_9_ = bf16[768,1024]{1,0:T(8,128)(2,1)} fusion(s32[1024]{0:T(1024)S(1)} %get-tuple-element.37), kind=kLoop, calls=%fused_computation.2 | loop fusion | flops 1572864 | bytes 1576960 | tf_op jit(solution)/shard_map/convert_element_type | solution.py:246
  31.6 4.8 %collective-permute-start = (bf16[200,768]{1,0:T(8,128)(2,1)S(1)}, bf16[200,768]{1,0:T(8,128)(2,1)S(1)}, u32[]{:S(2)}, u32[]{:S(2)}) collective-permute-start(bf16[200,768]{1,0:T(8,128)(2,1)S(1)} %fusion.3.refs_0_), channel_id=1, source_target_pairs={{0,8},{8,0},{1,9},{9,1},{2,10},{10,2},{3,11},{11,3},{4,12},{12,4},... | collective-permute-start | bytes 921608 | tf_op jit(solution)/shard_map/ppermute | solution.py:31
  36.4 0.1 collective-permute-start.2
  36.5 0.7 copy-done.9
  37.2 2.5 %collective-permute-start.12 = (bf16[192,768]{1,0:T(8,128)(2,1)}, bf16[192,768]{1,0:T(8,128)(2,1)}, u32[]{:S(2)}, u32[]{:S(2)}) collective-permute-start(bf16[192,768]{1,0:T(8,128)(2,1)} %collective-permute-done.11.refs_5_), channel_id=1, source_target_pairs={{0,3},{1,0},{2,1},{3,2},{4,7},{5,4},{6,5},{7,6},{8,11},{9,8},{10,9... | collective-permute-start | bytes 884744 | tf_op jit(solution)/shard_map/ppermute | solution.py:23
  39.7 0.7 copy-done.11
  40.4 0.7 collective-permute-start.4
  41.2 0.1 div.63
  41.2 0.1 rem.204
  41.3 0.1 ne.160
  41.4 4.6 %collective-permute-done.12.refs_6_ = bf16[192,768]{1,0:T(8,128)(2,1)} collective-permute-done((bf16[192,768]{1,0:T(8,128)(2,1)}, bf16[192,768]{1,0:T(8,128)(2,1)}, u32[]{:S(2)}, u32[]{:S(2)}) %collective-permute-start.12) | collective-permute-done | bytes 294944 | tf_op jit(solution)/shard_map/ppermute | solution.py:23
  46.0 1.0 copy-done.4
  47.0 1.0 copy-done.6
  47.9 1.0 copy-done.8
  48.9 1.0 copy-done.10
  49.9 1.0 copy-done.12
  50.8 4.8 %beta_product.1 = (bf16[2,48,384]{2,1,0:T(8,128)(2,1)S(1)}, bf16[2,48,384]{2,1,0:T(8,128)(2,1)}, bf16[2,48,384]{2,1,0:T(8,128)(2,1)S(1)}, bf16[2,48,384]{2,1,0:T(8,128)(2,1)S(1)}) custom-call(s32[36]{0:T(128)S(1)} %fusion.16.slots, bf16[192,768]{1,0:T(8,128)(2,1)S(1)} %bitcast.21, bf16[192,768]{1,0:T(8,128)(2,1)} %collective-permute-done.7.refs_1_, ...), custom_call_target="tpu_custom_call" | custom-call | tf_op jit(solution)/shard_map/beta_product/pallas_call | solution.py:249
  55.6 0.1 collective-permute-start.14
  55.7 3.6 %collective-permute-start.15 = (bf16[2,48,384]{2,1,0:T(8,128)(2,1)S(1)}, bf16[2,48,384]{2,1,0:T(8,128)(2,1)S(1)}, u32[]{:S(2)}, u32[]{:S(2)}) collective-permute-start(bf16[2,48,384]{2,1,0:T(8,128)(2,1)S(1)} %get-tuple-element.20), channel_id=1, source_target_pairs={{0,48},{4,20},{16,0},{20,36},{32,16},{36,52},{48,32},{52,4},{1,49}... | collective-permute-start | bytes 221192 | tf_op jit(solution)/shard_map/ppermute | solution.py:52
  59.3 3.5 %collective-permute-start.17 = (bf16[2,48,384]{2,1,0:T(8,128)(2,1)S(1)}, bf16[2,48,384]{2,1,0:T(8,128)(2,1)S(1)}, u32[]{:S(2)}, u32[]{:S(2)}) collective-permute-start(bf16[2,48,384]{2,1,0:T(8,128)(2,1)S(1)} %get-tuple-element.18.refs_8_), channel_id=1, source_target_pairs={{0,8},{8,0},{1,9},{9,1},{2,10},{10,2},{3,11},{11,3},{4,12},{12,4},... | collective-permute-start | bytes 221192 | tf_op jit(solution)/shard_map/ppermute | solution.py:31
  62.8 2.3 %collective-permute-start.18 = (bf16[2,48,384]{2,1,0:T(8,128)(2,1)S(1)}, bf16[2,48,384]{2,1,0:T(8,128)(2,1)S(1)}, u32[]{:S(2)}, u32[]{:S(2)}) collective-permute-start(bf16[2,48,384]{2,1,0:T(8,128)(2,1)S(1)} %collective-permute-done.14.refs_9_), channel_id=1, source_target_pairs={{0,8},{8,0},{1,9},{9,1},{2,10},{10,2},{3,11},{11,3},{4,12},{12,4},... | collective-permute-start | bytes 221192 | tf_op jit(solution)/shard_map/ppermute | solution.py:31
  65.1 3.6 %collective-permute-done.16.refs_11_ = bf16[2,48,384]{2,1,0:T(8,128)(2,1)S(1)} collective-permute-done((bf16[2,48,384]{2,1,0:T(8,128)(2,1)S(1)}, bf16[2,48,384]{2,1,0:T(8,128)(2,1)S(1)}, u32[]{:S(2)}, u32[]{:S(2)}) %collective-permute-start.16) | collective-permute-done | bytes 73760 | tf_op jit(solution)/shard_map/ppermute | solution.py:52
  68.7 1.5 %collective-permute-start.20 = (bf16[2,48,384]{2,1,0:T(8,128)(2,1)S(1)}, bf16[2,48,384]{2,1,0:T(8,128)(2,1)S(1)}, u32[]{:S(2)}, u32[]{:S(2)}) collective-permute-start(bf16[2,48,384]{2,1,0:T(8,128)(2,1)S(1)} %collective-permute-done.16.refs_11_), channel_id=1, source_target_pairs={{0,8},{8,0},{1,9},{9,1},{2,10},{10,2},{3,11},{11,3},{4,12},{12,4},... | collective-permute-start | bytes 221192 | tf_op jit(solution)/shard_map/ppermute | solution.py:31
  70.2 0.7 slice.35
  70.9 0.7 stack.3
  71.7 9.2 %alpha_product.1 = (f32[1536,128]{1,0:T(8,128)}, bf16[384,384]{1,0:T(8,128)(2,1)S(1)}, bf16[384,384]{1,0:T(8,128)(2,1)S(1)}, bf16[384,384]{1,0:T(8,128)(2,1)S(1)}) custom-call(s32[2048]{0:T(1024)S(1)} %fusion.9.lists, bf16[200,768]{1,0:T(8,128)(2,1)S(1)} %fusion.3.refs_0_, bf16[200,768]{1,0:T(8,128)(2,1)S(1)} %collective-permute-done.refs_1_, ...), custom_call_target="tpu_custom_call" | custom-call | tf_op jit(solution)/shard_map/alpha_product/pallas_call | solution.py:266
  80.9 1.4 %collective-permute-start.21 = (bf16[384,384]{1,0:T(8,128)(2,1)S(1)}, bf16[384,384]{1,0:T(8,128)(2,1)S(1)}, u32[]{:S(2)}, u32[]{:S(2)}) collective-permute-start(bf16[384,384]{1,0:T(8,128)(2,1)S(1)} %get-tuple-element.23), channel_id=1, source_target_pairs={{0,64},{64,128},{128,192},{192,0},{1,65},{65,129},{129,193},{193,1... | collective-permute-start | bytes 884744 | tf_op jit(solution)/shard_map/ppermute | solution.py:35
  82.2 2.6 %collective-permute-start.22 = (bf16[384,384]{1,0:T(8,128)(2,1)S(1)}, bf16[384,384]{1,0:T(8,128)(2,1)S(1)}, u32[]{:S(2)}, u32[]{:S(2)}) collective-permute-start(bf16[384,384]{1,0:T(8,128)(2,1)S(1)} %get-tuple-element.24), channel_id=1, source_target_pairs={{0,128},{64,192},{128,0},{192,64},{1,129},{65,193},{129,1},{193,65... | collective-permute-start | bytes 884744 | tf_op jit(solution)/shard_map/ppermute | solution.py:35
  84.9 1.1 collective-permute-start.23
  85.9 5.0 %collective-permute-done.21.r1 = bf16[384,384]{1,0:T(8,128)(2,1)S(1)} collective-permute-done((bf16[384,384]{1,0:T(8,128)(2,1)S(1)}, bf16[384,384]{1,0:T(8,128)(2,1)S(1)}, u32[]{:S(2)}, u32[]{:S(2)}) %collective-permute-start.21) | collective-permute-done | bytes 294944 | tf_op jit(solution)/shard_map/ppermute | solution.py:35
  90.9 7.4 %collective-permute-done.22.r2 = bf16[384,384]{1,0:T(8,128)(2,1)S(1)} collective-permute-done((bf16[384,384]{1,0:T(8,128)(2,1)S(1)}, bf16[384,384]{1,0:T(8,128)(2,1)S(1)}, u32[]{:S(2)}, u32[]{:S(2)}) %collective-permute-start.22) | collective-permute-done | bytes 294944 | tf_op jit(solution)/shard_map/ppermute | solution.py:35
  98.3 1.1 copy-done.1
  99.5 1.9 %y_sum.1 = (bf16[2,48,384]{2,1,0:T(8,128)(2,1)S(1)}, bf16[2,48,384]{2,1,0:T(8,128)(2,1)S(1)}, bf16[2,48,384]{2,1,0:T(8,128)(2,1)S(1)}, bf16[2,48,384]{2,1,0:T(8,128)(2,1)S(1)}, bf16[32,24,192]{2,1,0:T(8,128)(2,1)}) custom-call(s32[8]{0:T(128)S(1)} %get-tuple-element.34.dests, f32[1536,128]{1,0:T(8,128)S(1)} %copy-done.1, ...), custom_call_target="tpu_custom_call" | custom-call | tf_op jit(solution)/shard_map/y_sum/pallas_call | solution.py:284
  101.4 7.3 %all-to-all-start = ((bf16[32,24,192]{2,1,0:T(8,128)(2,1)}), bf16[32,24,192]{2,1,0:T(8,128)(2,1)S(1)}, u32[]{:S(2)}, u32[]{:S(2)}) async-start(bf16[32,24,192]{2,1,0:T(8,128)(2,1)} %get-tuple-element.30), calls=%async_computation | async-start | bytes 786432 | tf_op jit(solution)/shard_map/all_to_all | solution.py:293
  108.7 1.7 %collective-permute-start.24 = (bf16[2,48,384]{2,1,0:T(8,128)(2,1)S(1)}, bf16[2,48,384]{2,1,0:T(8,128)(2,1)S(1)}, u32[]{:S(2)}, u32[]{:S(2)}) collective-permute-start(bf16[2,48,384]{2,1,0:T(8,128)(2,1)S(1)} %get-tuple-element.27), channel_id=1, source_target_pairs={{0,16},{4,52},{16,32},{20,4},{32,48},{36,20},{48,0},{52,36},{1,17}... | collective-permute-start | bytes 221192 | tf_op jit(solution)/shard_map/ppermute | solution.py:52
  110.4 2.0 %collective-permute-start.25 = (bf16[2,48,384]{2,1,0:T(8,128)(2,1)S(1)}, bf16[2,48,384]{2,1,0:T(8,128)(2,1)S(1)}, u32[]{:S(2)}, u32[]{:S(2)}) collective-permute-start(bf16[2,48,384]{2,1,0:T(8,128)(2,1)S(1)} %get-tuple-element.28), channel_id=1, source_target_pairs={{0,48},{4,20},{16,0},{20,36},{32,16},{36,52},{48,32},{52,4},{1,49}... | collective-permute-start | bytes 221192 | tf_op jit(solution)/shard_map/ppermute | solution.py:52
  112.4 1.6 %collective-permute-start.26 = (bf16[2,48,384]{2,1,0:T(8,128)(2,1)S(1)}, bf16[2,48,384]{2,1,0:T(8,128)(2,1)S(1)}, u32[]{:S(2)}, u32[]{:S(2)}) collective-permute-start(bf16[2,48,384]{2,1,0:T(8,128)(2,1)S(1)} %get-tuple-element.29), channel_id=1, source_target_pairs={{0,32},{4,36},{16,48},{20,52},{32,0},{36,4},{48,16},{52,20},{1,33}... | collective-permute-start | bytes 221192 | tf_op jit(solution)/shard_map/ppermute | solution.py:52
  114.0 2.0 %collective-permute-start.27 = (bf16[2,48,384]{2,1,0:T(8,128)(2,1)S(1)}, bf16[2,48,384]{2,1,0:T(8,128)(2,1)S(1)}, u32[]{:S(2)}, u32[]{:S(2)}) collective-permute-start(bf16[2,48,384]{2,1,0:T(8,128)(2,1)S(1)} %get-tuple-element.26.refs_0_), channel_id=1, source_target_pairs={{0,8},{8,0},{1,9},{9,1},{2,10},{10,2},{3,11},{11,3},{4,12},{12,4},... | collective-permute-start | bytes 221192 | tf_op jit(solution)/shard_map/ppermute | solution.py:31
  116.0 0.0 collective-permute-done.24.refs_1_
  116.0 3.1 %collective-permute-start.28 = (bf16[2,48,384]{2,1,0:T(8,128)(2,1)S(1)}, bf16[2,48,384]{2,1,0:T(8,128)(2,1)S(1)}, u32[]{:S(2)}, u32[]{:S(2)}) collective-permute-start(bf16[2,48,384]{2,1,0:T(8,128)(2,1)S(1)} %collective-permute-done.24.refs_1_), channel_id=1, source_target_pairs={{0,8},{8,0},{1,9},{9,1},{2,10},{10,2},{3,11},{11,3},{4,12},{12,4},... | collective-permute-start | bytes 221192 | tf_op jit(solution)/shard_map/ppermute | solution.py:31
  119.1 0.9 collective-permute-done.26.refs_3_
  120.0 3.4 %collective-permute-start.30 = (bf16[2,48,384]{2,1,0:T(8,128)(2,1)S(1)}, bf16[2,48,384]{2,1,0:T(8,128)(2,1)S(1)}, u32[]{:S(2)}, u32[]{:S(2)}) collective-permute-start(bf16[2,48,384]{2,1,0:T(8,128)(2,1)S(1)} %collective-permute-done.26.refs_3_), channel_id=1, source_target_pairs={{0,8},{8,0},{1,9},{9,1},{2,10},{10,2},{3,11},{11,3},{4,12},{12,4},... | collective-permute-start | bytes 221192 | tf_op jit(solution)/shard_map/ppermute | solution.py:31
  123.4 0.3 fusion.1.refs_9_
  123.8 0.6 collective-permute-done.30.refs_7_
  124.3 1.9 %combine.1 = f32[192,768]{1,0:T(8,128)} custom-call(bf16[2,48,384]{2,1,0:T(8,128)(2,1)S(1)} %get-tuple-element.26.refs_0_, bf16[2,48,384]{2,1,0:T(8,128)(2,1)S(1)} %collective-permute-done.24.refs_1_, bf16[2,48,384]{2,1,0:T(8,128)(2,1)S(1)} %collective-permute-done.25.refs_2_, bf16[2,48,384]{2,1,0:T(8,128)(2,1)S(1)} %collective-permute-done.26.refs_3_, ...), custom_call_target="tpu_custom_call" | custom-call | tf_op jit(solution)/shard_map/combine/pallas_call | solution.py:295
  (69 shorter events, 0.3 us)
Async XLA Ops:
  0.8 12.4 %copy-start.15 = (bf16[1,256]{1,0:T(2,128)(2,1)}, bf16[1,256]{1,0:T(2,128)(2,1)S(1)}, u32[]{:S(2)}) copy-start(bf16[1,256]{1,0:T(2,128)(2,1)S(1)} %convert_element_type.32) | copy-start | bytes 1540
  3.8 9.4 %copy-start.3 = (bf16[8,24,768]{2,1,0:T(8,128)(2,1)S(1)}, bf16[8,24,768]{2,1,0:T(8,128)(2,1)}, u32[]{:S(2)}) copy-start(bf16[8,24,768]{2,1,0:T(8,128)(2,1)} %param.8) | copy-start | bytes 884740
  3.9 12.2 %copy-start.16 = (s32[8]{0:T(128)S(1)}, s32[8]{0:T(128)}, u32[]{:S(2)}) copy-start(s32[8]{0:T(128)} %constant.166.clone) | copy-start | bytes 100
  3.9 12.1 %copy-start.17 = (s32[8]{0:T(128)S(1)}, s32[8]{0:T(128)}, u32[]{:S(2)}) copy-start(s32[8]{0:T(128)} %constant.167.clone) | copy-start | bytes 100
  3.9 25.9 %copy-start.14 = (s32[1,6,6]{2,0,1:T(1,128)S(1)}, s32[1,6,6]{2,0,1:T(1,128)}, u32[]{:S(2)}) copy-start(s32[1,6,6]{2,0,1:T(1,128)} %param.10) | copy-start | bytes 436
  6.7 39.3 %copy-start = (bf16[1,6,6,128,128]{4,3,2,1,0:T(8,128)(2,1)S(1)}, bf16[1,6,6,128,128]{4,3,2,1,0:T(8,128)(2,1)}, u32[]{:S(2)}) copy-start(bf16[1,6,6,128,128]{4,3,2,1,0:T(8,128)(2,1)} %param.9) | copy-start | bytes 3538948
  6.7 13.5 %collective-permute-start.1 = (bf16[200,768]{1,0:T(8,128)(2,1)S(1)}, bf16[200,768]{1,0:T(8,128)(2,1)S(1)}, u32[]{:S(2)}, u32[]{:S(2)}) collective-permute-start(bf16[200,768]{1,0:T(8,128)(2,1)S(1)} %fusion.3.refs_0_), channel_id=1, source_target_pairs={{0,52},{4,16},{16,4},{20,32},{32,20},{36,48},{48,36},{52,0},{1,53}... | collective-permute-start | bytes 921608 | tf_op jit(solution)/shard_map/ppermute | solution.py:43
  13.2 10.4 %collective-permute-start.10 = (bf16[192,768]{1,0:T(8,128)(2,1)S(1)}, bf16[192,768]{1,0:T(8,128)(2,1)S(1)}, u32[]{:S(2)}, u32[]{:S(2)}) collective-permute-start(bf16[192,768]{1,0:T(8,128)(2,1)S(1)} %bitcast.18), channel_id=1, source_target_pairs={{0,4},{4,0},{1,5},{5,1},{2,6},{6,2},{3,7},{7,3},{8,12},{12,8},{9,1... | collective-permute-start | bytes 884744 | tf_op jit(solution)/shard_map/ppermute | solution.py:27
  13.2 8.8 %collective-permute-start.8 = (bf16[192,768]{1,0:T(8,128)(2,1)S(1)}, bf16[192,768]{1,0:T(8,128)(2,1)S(1)}, u32[]{:S(2)}, u32[]{:S(2)}) collective-permute-start(bf16[192,768]{1,0:T(8,128)(2,1)S(1)} %bitcast.19), channel_id=1, source_target_pairs={{0,1},{1,2},{2,3},{3,0},{4,5},{5,6},{6,7},{7,4},{8,9},{9,10},{10,1... | collective-permute-start | bytes 884744 | tf_op jit(solution)/shard_map/ppermute | solution.py:23
  14.5 17.1 %collective-permute-start.7 = (bf16[192,768]{1,0:T(8,128)(2,1)S(1)}, bf16[192,768]{1,0:T(8,128)(2,1)}, u32[]{:S(2)}, u32[]{:S(2)}) collective-permute-start(bf16[192,768]{1,0:T(8,128)(2,1)S(1)} %bitcast.20), channel_id=1, source_target_pairs={{0,3},{1,0},{2,1},{3,2},{4,7},{5,4},{6,5},{7,6},{8,11},{9,8},{10,9... | collective-permute-start | bytes 884744 | tf_op jit(solution)/shard_map/ppermute | solution.py:23
  20.2 7.5 %collective-permute-start.3 = (bf16[200,768]{1,0:T(8,128)(2,1)S(1)}, bf16[200,768]{1,0:T(8,128)(2,1)S(1)}, u32[]{:S(2)}, u32[]{:S(2)}) collective-permute-start(bf16[200,768]{1,0:T(8,128)(2,1)S(1)} %collective-permute-done.1.refs_2_), channel_id=1, source_target_pairs={{0,4},{4,0},{1,5},{5,1},{2,6},{6,2},{3,7},{7,3},{8,12},{12,8},{9,1... | collective-permute-start | bytes 921608 | tf_op jit(solution)/shard_map/ppermute | solution.py:27
  22.1 17.6 %copy-start.7 = (bf16[192,768]{1,0:T(8,128)(2,1)}, bf16[192,768]{1,0:T(8,128)(2,1)S(1)}, u32[]{:S(2)}) copy-start(bf16[192,768]{1,0:T(8,128)(2,1)S(1)} %collective-permute-done.8.refs_3_) | copy-start | bytes 884740
  22.1 14.4 %collective-permute-start.13 = (bf16[192,768]{1,0:T(8,128)(2,1)S(1)}, bf16[192,768]{1,0:T(8,128)(2,1)S(1)}, u32[]{:S(2)}, u32[]{:S(2)}) collective-permute-start(bf16[192,768]{1,0:T(8,128)(2,1)S(1)} %collective-permute-done.8.refs_3_), channel_id=1, source_target_pairs={{0,4},{4,0},{1,5},{5,1},{2,6},{6,2},{3,7},{7,3},{8,12},{12,8},{9,1... | collective-permute-start | bytes 884744 | tf_op jit(solution)/shard_map/ppermute | solution.py:27
  23.2 16.5 %collective-permute-start.9 = (bf16[192,768]{1,0:T(8,128)(2,1)S(1)}, bf16[192,768]{1,0:T(8,128)(2,1)S(1)}, u32[]{:S(2)}, u32[]{:S(2)}) collective-permute-start(bf16[192,768]{1,0:T(8,128)(2,1)S(1)} %collective-permute-done.8.refs_3_), channel_id=1, source_target_pairs={{0,1},{1,2},{2,3},{3,0},{4,5},{5,6},{6,7},{7,4},{8,9},{9,10},{10,1... | collective-permute-start | bytes 884744 | tf_op jit(solution)/shard_map/ppermute | solution.py:23
  23.6 12.8 %copy-start.5 = (bf16[192,768]{1,0:T(8,128)(2,1)}, bf16[192,768]{1,0:T(8,128)(2,1)S(1)}, u32[]{:S(2)}) copy-start(bf16[192,768]{1,0:T(8,128)(2,1)S(1)} %collective-permute-done.10.refs_4_) | copy-start | bytes 884740
  23.6 12.8 %collective-permute-start.11 = (bf16[192,768]{1,0:T(8,128)(2,1)S(1)}, bf16[192,768]{1,0:T(8,128)(2,1)}, u32[]{:S(2)}, u32[]{:S(2)}) collective-permute-start(bf16[192,768]{1,0:T(8,128)(2,1)S(1)} %collective-permute-done.10.refs_4_), channel_id=1, source_target_pairs={{0,3},{1,0},{2,1},{3,2},{4,7},{5,4},{6,5},{7,6},{8,11},{9,8},{10,9... | collective-permute-start | bytes 884744 | tf_op jit(solution)/shard_map/ppermute | solution.py:23
  27.8 13.4 %collective-permute-start.5 = (bf16[200,768]{1,0:T(8,128)(2,1)S(1)}, bf16[200,768]{1,0:T(8,128)(2,1)S(1)}, u32[]{:S(2)}, u32[]{:S(2)}) collective-permute-start(bf16[200,768]{1,0:T(8,128)(2,1)S(1)} %collective-permute-done.3.refs_4_), channel_id=1, source_target_pairs={{0,52},{4,16},{16,4},{20,32},{32,20},{36,48},{48,36},{52,0},{1,53}... | collective-permute-start | bytes 921608 | tf_op jit(solution)/shard_map/ppermute | solution.py:43
  31.6 24.1 %collective-permute-start = (bf16[200,768]{1,0:T(8,128)(2,1)S(1)}, bf16[200,768]{1,0:T(8,128)(2,1)S(1)}, u32[]{:S(2)}, u32[]{:S(2)}) collective-permute-start(bf16[200,768]{1,0:T(8,128)(2,1)S(1)} %fusion.3.refs_0_), channel_id=1, source_target_pairs={{0,8},{8,0},{1,9},{9,1},{2,10},{10,2},{3,11},{11,3},{4,12},{12,4},... | collective-permute-start | bytes 921608 | tf_op jit(solution)/shard_map/ppermute | solution.py:31
  36.4 22.8 %collective-permute-start.2 = (bf16[200,768]{1,0:T(8,128)(2,1)S(1)}, bf16[200,768]{1,0:T(8,128)(2,1)S(1)}, u32[]{:S(2)}, u32[]{:S(2)}) collective-permute-start(bf16[200,768]{1,0:T(8,128)(2,1)S(1)} %collective-permute-done.1.refs_2_), channel_id=1, source_target_pairs={{0,8},{8,0},{1,9},{9,1},{2,10},{10,2},{3,11},{11,3},{4,12},{12,4},... | collective-permute-start | bytes 921608 | tf_op jit(solution)/shard_map/ppermute | solution.py:31
  36.5 0.7 copy-start.9
  37.2 8.8 %collective-permute-start.12 = (bf16[192,768]{1,0:T(8,128)(2,1)}, bf16[192,768]{1,0:T(8,128)(2,1)}, u32[]{:S(2)}, u32[]{:S(2)}) collective-permute-start(bf16[192,768]{1,0:T(8,128)(2,1)} %collective-permute-done.11.refs_5_), channel_id=1, source_target_pairs={{0,3},{1,0},{2,1},{3,2},{4,7},{5,4},{6,5},{7,6},{8,11},{9,8},{10,9... | collective-permute-start | bytes 884744 | tf_op jit(solution)/shard_map/ppermute | solution.py:23
  39.7 0.7 copy-start.11
  40.4 18.9 %collective-permute-start.4 = (bf16[200,768]{1,0:T(8,128)(2,1)S(1)}, bf16[200,768]{1,0:T(8,128)(2,1)S(1)}, u32[]{:S(2)}, u32[]{:S(2)}) collective-permute-start(bf16[200,768]{1,0:T(8,128)(2,1)S(1)} %collective-permute-done.3.refs_4_), channel_id=1, source_target_pairs={{0,8},{8,0},{1,9},{9,1},{2,10},{10,2},{3,11},{11,3},{4,12},{12,4},... | collective-permute-start | bytes 921608 | tf_op jit(solution)/shard_map/ppermute | solution.py:31
  41.1 29.1 %collective-permute-start.6 = (bf16[200,768]{1,0:T(8,128)(2,1)S(1)}, bf16[200,768]{1,0:T(8,128)(2,1)}, u32[]{:S(2)}, u32[]{:S(2)}) collective-permute-start(bf16[200,768]{1,0:T(8,128)(2,1)S(1)} %collective-permute-done.5.refs_6_), channel_id=1, source_target_pairs={{0,8},{8,0},{1,9},{9,1},{2,10},{10,2},{3,11},{11,3},{4,12},{12,4},... | collective-permute-start | bytes 921608 | tf_op jit(solution)/shard_map/ppermute | solution.py:31
  46.0 1.0 copy-start.4
  47.0 1.0 copy-start.6
  47.9 1.0 copy-start.8
  48.9 1.0 copy-start.10
  49.9 1.0 copy-start.12
  55.6 7.2 %collective-permute-start.14 = (bf16[2,48,384]{2,1,0:T(8,128)(2,1)}, bf16[2,48,384]{2,1,0:T(8,128)(2,1)S(1)}, u32[]{:S(2)}, u32[]{:S(2)}) collective-permute-start(bf16[2,48,384]{2,1,0:T(8,128)(2,1)} %get-tuple-element.19), channel_id=1, source_target_pairs={{0,16},{4,52},{16,32},{20,4},{32,48},{36,20},{48,0},{52,36},{1,17}... | collective-permute-start | bytes 221192 | tf_op jit(solution)/shard_map/ppermute | solution.py:52
  55.7 9.4 %collective-permute-start.15 = (bf16[2,48,384]{2,1,0:T(8,128)(2,1)S(1)}, bf16[2,48,384]{2,1,0:T(8,128)(2,1)S(1)}, u32[]{:S(2)}, u32[]{:S(2)}) collective-permute-start(bf16[2,48,384]{2,1,0:T(8,128)(2,1)S(1)} %get-tuple-element.20), channel_id=1, source_target_pairs={{0,48},{4,20},{16,0},{20,36},{32,16},{36,52},{48,32},{52,4},{1,49}... | collective-permute-start | bytes 221192 | tf_op jit(solution)/shard_map/ppermute | solution.py:52
  59.2 9.5 %collective-permute-start.16 = (bf16[2,48,384]{2,1,0:T(8,128)(2,1)S(1)}, bf16[2,48,384]{2,1,0:T(8,128)(2,1)S(1)}, u32[]{:S(2)}, u32[]{:S(2)}) collective-permute-start(bf16[2,48,384]{2,1,0:T(8,128)(2,1)S(1)} %get-tuple-element.21), channel_id=1, source_target_pairs={{0,32},{4,36},{16,48},{20,52},{32,0},{36,4},{48,16},{52,20},{1,33}... | collective-permute-start | bytes 221192 | tf_op jit(solution)/shard_map/ppermute | solution.py:52
  59.3 12.3 %collective-permute-start.17 = (bf16[2,48,384]{2,1,0:T(8,128)(2,1)S(1)}, bf16[2,48,384]{2,1,0:T(8,128)(2,1)S(1)}, u32[]{:S(2)}, u32[]{:S(2)}) collective-permute-start(bf16[2,48,384]{2,1,0:T(8,128)(2,1)S(1)} %get-tuple-element.18.refs_8_), channel_id=1, source_target_pairs={{0,8},{8,0},{1,9},{9,1},{2,10},{10,2},{3,11},{11,3},{4,12},{12,4},... | collective-permute-start | bytes 221192 | tf_op jit(solution)/shard_map/ppermute | solution.py:31
  62.8 8.8 %collective-permute-start.18 = (bf16[2,48,384]{2,1,0:T(8,128)(2,1)S(1)}, bf16[2,48,384]{2,1,0:T(8,128)(2,1)S(1)}, u32[]{:S(2)}, u32[]{:S(2)}) collective-permute-start(bf16[2,48,384]{2,1,0:T(8,128)(2,1)S(1)} %collective-permute-done.14.refs_9_), channel_id=1, source_target_pairs={{0,8},{8,0},{1,9},{9,1},{2,10},{10,2},{3,11},{11,3},{4,12},{12,4},... | collective-permute-start | bytes 221192 | tf_op jit(solution)/shard_map/ppermute | solution.py:31
  65.1 6.5 %collective-permute-start.19 = (bf16[2,48,384]{2,1,0:T(8,128)(2,1)S(1)}, bf16[2,48,384]{2,1,0:T(8,128)(2,1)S(1)}, u32[]{:S(2)}, u32[]{:S(2)}) collective-permute-start(bf16[2,48,384]{2,1,0:T(8,128)(2,1)S(1)} %collective-permute-done.15.refs_10_), channel_id=1, source_target_pairs={{0,8},{8,0},{1,9},{9,1},{2,10},{10,2},{3,11},{11,3},{4,12},{12,4},... | collective-permute-start | bytes 221192 | tf_op jit(solution)/shard_map/ppermute | solution.py:31
  68.7 2.9 %collective-permute-start.20 = (bf16[2,48,384]{2,1,0:T(8,128)(2,1)S(1)}, bf16[2,48,384]{2,1,0:T(8,128)(2,1)S(1)}, u32[]{:S(2)}, u32[]{:S(2)}) collective-permute-start(bf16[2,48,384]{2,1,0:T(8,128)(2,1)S(1)} %collective-permute-done.16.refs_11_), channel_id=1, source_target_pairs={{0,8},{8,0},{1,9},{9,1},{2,10},{10,2},{3,11},{11,3},{4,12},{12,4},... | collective-permute-start | bytes 221192 | tf_op jit(solution)/shard_map/ppermute | solution.py:31
  80.9 42.6 %copy-start.13 = (s32[8,128]{1,0:T(8,128)S(1)}, s32[8,128]{1,0:T(8,128)}, u32[]{:S(2)}) copy-start(s32[8,128]{1,0:T(8,128)} %get-tuple-element.36) | copy-start | bytes 12292
  80.9 10.0 %collective-permute-start.21 = (bf16[384,384]{1,0:T(8,128)(2,1)S(1)}, bf16[384,384]{1,0:T(8,128)(2,1)S(1)}, u32[]{:S(2)}, u32[]{:S(2)}) collective-permute-start(bf16[384,384]{1,0:T(8,128)(2,1)S(1)} %get-tuple-element.23), channel_id=1, source_target_pairs={{0,64},{64,128},{128,192},{192,0},{1,65},{65,129},{129,193},{193,1... | collective-permute-start | bytes 884744 | tf_op jit(solution)/shard_map/ppermute | solution.py:35
  82.2 16.1 %collective-permute-start.22 = (bf16[384,384]{1,0:T(8,128)(2,1)S(1)}, bf16[384,384]{1,0:T(8,128)(2,1)S(1)}, u32[]{:S(2)}, u32[]{:S(2)}) collective-permute-start(bf16[384,384]{1,0:T(8,128)(2,1)S(1)} %get-tuple-element.24), channel_id=1, source_target_pairs={{0,128},{64,192},{128,0},{192,64},{1,129},{65,193},{129,1},{193,65... | collective-permute-start | bytes 884744 | tf_op jit(solution)/shard_map/ppermute | solution.py:35
  84.9 13.5 %collective-permute-start.23 = (bf16[384,384]{1,0:T(8,128)(2,1)S(1)}, bf16[384,384]{1,0:T(8,128)(2,1)S(1)}, u32[]{:S(2)}, u32[]{:S(2)}) collective-permute-start(bf16[384,384]{1,0:T(8,128)(2,1)S(1)} %get-tuple-element.25), channel_id=1, source_target_pairs={{0,192},{64,0},{128,64},{192,128},{1,193},{65,1},{129,65},{193,129... | collective-permute-start | bytes 884744 | tf_op jit(solution)/shard_map/ppermute | solution.py:35
  98.3 1.1 copy-start.1
  101.4 23.0 %copy-start.2 = (f32[8,24,768]{2,1,0:T(8,128)S(1)}, f32[8,24,768]{2,1,0:T(8,128)}, u32[]{:S(2)}) copy-start(f32[8,24,768]{2,1,0:T(8,128)} %param.13) | copy-start | bytes 1769476
  101.4 22.9 %all-to-all-start = ((bf16[32,24,192]{2,1,0:T(8,128)(2,1)}), bf16[32,24,192]{2,1,0:T(8,128)(2,1)S(1)}, u32[]{:S(2)}, u32[]{:S(2)}) async-start(bf16[32,24,192]{2,1,0:T(8,128)(2,1)} %get-tuple-element.30), calls=%async_computation | async-start | bytes 786432 | tf_op jit(solution)/shard_map/all_to_all | solution.py:293
  108.7 7.3 %collective-permute-start.24 = (bf16[2,48,384]{2,1,0:T(8,128)(2,1)S(1)}, bf16[2,48,384]{2,1,0:T(8,128)(2,1)S(1)}, u32[]{:S(2)}, u32[]{:S(2)}) collective-permute-start(bf16[2,48,384]{2,1,0:T(8,128)(2,1)S(1)} %get-tuple-element.27), channel_id=1, source_target_pairs={{0,16},{4,52},{16,32},{20,4},{32,48},{36,20},{48,0},{52,36},{1,17}... | collective-permute-start | bytes 221192 | tf_op jit(solution)/shard_map/ppermute | solution.py:52
  110.4 8.7 %collective-permute-start.25 = (bf16[2,48,384]{2,1,0:T(8,128)(2,1)S(1)}, bf16[2,48,384]{2,1,0:T(8,128)(2,1)S(1)}, u32[]{:S(2)}, u32[]{:S(2)}) collective-permute-start(bf16[2,48,384]{2,1,0:T(8,128)(2,1)S(1)} %get-tuple-element.28), channel_id=1, source_target_pairs={{0,48},{4,20},{16,0},{20,36},{32,16},{36,52},{48,32},{52,4},{1,49}... | collective-permute-start | bytes 221192 | tf_op jit(solution)/shard_map/ppermute | solution.py:52
  112.4 7.7 %collective-permute-start.26 = (bf16[2,48,384]{2,1,0:T(8,128)(2,1)S(1)}, bf16[2,48,384]{2,1,0:T(8,128)(2,1)S(1)}, u32[]{:S(2)}, u32[]{:S(2)}) collective-permute-start(bf16[2,48,384]{2,1,0:T(8,128)(2,1)S(1)} %get-tuple-element.29), channel_id=1, source_target_pairs={{0,32},{4,36},{16,48},{20,52},{32,0},{36,4},{48,16},{52,20},{1,33}... | collective-permute-start | bytes 221192 | tf_op jit(solution)/shard_map/ppermute | solution.py:52
  114.0 9.8 %collective-permute-start.27 = (bf16[2,48,384]{2,1,0:T(8,128)(2,1)S(1)}, bf16[2,48,384]{2,1,0:T(8,128)(2,1)S(1)}, u32[]{:S(2)}, u32[]{:S(2)}) collective-permute-start(bf16[2,48,384]{2,1,0:T(8,128)(2,1)S(1)} %get-tuple-element.26.refs_0_), channel_id=1, source_target_pairs={{0,8},{8,0},{1,9},{9,1},{2,10},{10,2},{3,11},{11,3},{4,12},{12,4},... | collective-permute-start | bytes 221192 | tf_op jit(solution)/shard_map/ppermute | solution.py:31
  116.0 7.8 %collective-permute-start.28 = (bf16[2,48,384]{2,1,0:T(8,128)(2,1)S(1)}, bf16[2,48,384]{2,1,0:T(8,128)(2,1)S(1)}, u32[]{:S(2)}, u32[]{:S(2)}) collective-permute-start(bf16[2,48,384]{2,1,0:T(8,128)(2,1)S(1)} %collective-permute-done.24.refs_1_), channel_id=1, source_target_pairs={{0,8},{8,0},{1,9},{9,1},{2,10},{10,2},{3,11},{11,3},{4,12},{12,4},... | collective-permute-start | bytes 221192 | tf_op jit(solution)/shard_map/ppermute | solution.py:31
  119.1 4.6 %collective-permute-start.29 = (bf16[2,48,384]{2,1,0:T(8,128)(2,1)S(1)}, bf16[2,48,384]{2,1,0:T(8,128)(2,1)S(1)}, u32[]{:S(2)}, u32[]{:S(2)}) collective-permute-start(bf16[2,48,384]{2,1,0:T(8,128)(2,1)S(1)} %collective-permute-done.25.refs_2_), channel_id=1, source_target_pairs={{0,8},{8,0},{1,9},{9,1},{2,10},{10,2},{3,11},{11,3},{4,12},{12,4},... | collective-permute-start | bytes 221192 | tf_op jit(solution)/shard_map/ppermute | solution.py:31
  120.0 4.3 %collective-permute-start.30 = (bf16[2,48,384]{2,1,0:T(8,128)(2,1)S(1)}, bf16[2,48,384]{2,1,0:T(8,128)(2,1)S(1)}, u32[]{:S(2)}, u32[]{:S(2)}) collective-permute-start(bf16[2,48,384]{2,1,0:T(8,128)(2,1)S(1)} %collective-permute-done.26.refs_3_), channel_id=1, source_target_pairs={{0,8},{8,0},{1,9},{9,1},{2,10},{10,2},{3,11},{11,3},{4,12},{12,4},... | collective-permute-start | bytes 221192 | tf_op jit(solution)/shard_map/ppermute | solution.py:31

commit v2 on v1

--- a/solution.py
+++ b/solution.py
@@ -1,5 +1,6 @@
 import jax
 import jax.numpy as jnp
+import numpy as np
 from jax import lax
 from jax.experimental import pallas as pl
 from jax.experimental.pallas import tpu as pltpu
@@ -35,11 +36,11 @@
     return lax.ppermute(a, "y", [(i, (i + k) % NY) for i in range(NY)])
 
 
-def cross_z(a):
+def cross_z(a, step):
     moves = []
     for zh in range(NZ):
-        moves.append((zh * 2, (zh - 1) % NZ * 2 + 1))
-        moves.append((zh * 2 + 1, (zh + 1) % NZ * 2))
+        moves.append((zh * 2, (zh - step) % NZ * 2 + 1))
+        moves.append((zh * 2 + 1, (zh + step) % NZ * 2))
     return lax.ppermute(a, ("zh", "zl"), moves)
 
 
@@ -79,13 +80,6 @@
         pltpu.roll(jnp.where(lane < 64, t2, t1), 64, 1),
         pltpu.roll(t2, 96, 1),
     ]
-
-
-def gather_c(own):
-    over, left, right = flip_zl(own), shift_x(own, 1), shift_x(own, -1)
-    over_right, far, over_left = shift_x(over, -1), shift_x(left, 1), flip_zl(left)
-    over_far = shift_x(over_right, -1)
-    return [own, right, far, left, over, over_right, over_far, over_left]
 
 
 def x_kernel(slots, *refs):
@@ -113,18 +107,78 @@
         outs[label // 2][label % 2] = pack([piece[i * 48 : (i + 1) * 48] for i in range(4)]).astype(BF)
 
 
-def a_kernel(lists, *refs):
-    ps, xs, (own_ref, s1, s2, s3) = refs[:8], refs[8:16], refs[16:20]
-    acc, pbuf, xbuf, res, psem, xsem = refs[20:]
+def turn_rows():
+    turn = np.zeros((RT * U, RT * U), np.float32)
+    for z in range(RT):
+        for u in range(U):
+            turn[z * U + u, u * RT + z] = 1.0
+    return jnp.asarray(turn, BF)
+
+
+def tiles_kernel(values, rows, turn, out, wide):
+    for g in range(G):
+        for q in range(U // 4):
+            wide[g * U : (g + 1) * U, q * 128 : (q + 1) * 128] = jnp.concatenate(
+                [values[g, 4 * q + i].astype(F32) for i in range(4)], axis=1
+            )
+    flat = wide[...]
+    blank = jnp.zeros((64, COLS), F32)
+    even = jnp.concatenate([flat, blank], axis=0).astype(BF)
+    odd = jnp.concatenate([blank, flat], axis=0).astype(BF)
+    for q in range(4):
+        turned = lax.dot_general(
+            turn[q * ROWS : (q + 1) * ROWS, :],
+            odd if q % 2 else even,
+            (((1,), (1,)), ((), ())),
+            preferred_element_type=F32,
+        )
+        if q % 2 == 0:
+            kept = turned
+        else:
+            first = (q - 1) * ROWS
+            out[:ROWS, first : first + 128] = kept[:, :128].astype(BF)
+            out[:ROWS, first + 128 : first + 256] = (kept[:, 128:] + turned[:, :128]).astype(BF)
+            out[:ROWS, first + 256 : first + 384] = turned[:, 128:].astype(BF)
+    tile_rows = rows[...].astype(F32)
+    line = [
+        jnp.concatenate([tile_rows[4 * k + i : 4 * k + i + 1] for i in range(4)], axis=1)
+        for k in range(2)
+    ]
+    line = jnp.concatenate(line + [jnp.zeros((1, COLS - G * RT), F32)], axis=1)
+    out[ROWS:, :] = jnp.broadcast_to(line, (8, COLS)).astype(BF)
+
+
+def stack_kernel(after, *refs):
+    parts, out, sems = refs[:NZ], refs[NZ], refs[NZ + 1]
+    copies = [pltpu.make_async_copy(parts[i], out.at[i], sems.at[i]) for i in range(NZ)]
+    for cp in copies:
+        cp.start()
+    for cp in copies:
+        cp.wait()
+
+
+def a_kernel(place, *refs):
+    ps, xs, (own_ref, s1, s2, s3) = refs[:2], refs[2:10], refs[10:14]
+    acc, pbuf, xbuf, res, spots_v, lists, psem, xsem, lsem = refs[14:]
     pc, xc = [], []
     for i in range(NH):
-        pc.append(pltpu.make_async_copy(ps[i].at[pl.ds(0, ROWS)], pbuf.at[i], psem.at[i]))
-        xc.append(pltpu.make_async_copy(xs[i % 2 * NZ + i // 2].at[i % 2], xbuf.at[i], xsem.at[i]))
+        k = i % 2 * NZ + i // 2
+        pc.append(pltpu.make_async_copy(ps[i % 2].at[i // 2], pbuf.at[i], psem.at[i]))
+        xc.append(pltpu.make_async_copy(xs[k].at[i % 2], xbuf.at[i], xsem.at[i]))
     for cp in pc + xc:
         cp.start()
     acc[...] = jnp.zeros_like(acc)
-    for cp in pc + xc:
+    for cp in pc:
         cp.wait()
+    for i in range(NH):
+        tile = pbuf[i, ROWS:, : G * RT].astype(F32)[0:1].astype(jnp.int32)
+        to_y = ((tile >> 3) - place[0]) & (NY - 1)
+        spots_v[i : i + 1] = (to_y * (G * NH) + (tile >> 5) * NH + (tile & 7)) * U
+    to_smem = pltpu.make_async_copy(spots_v, lists, lsem)
+    to_smem.start()
+    for cp in xc:
+        cp.wait()
+    to_smem.wait()
     rows = lax.broadcasted_iota(jnp.int32, (ROWS, 128), 0)
     blank = jnp.zeros((64, 256), F32)
 
@@ -142,7 +196,7 @@
             for q in range(4):
                 first = q * ROWS - q % 2 * 64
                 res[pair % 2, q * ROWS : (q + 1) * ROWS] = jnp.dot(
-                    pbuf[label, :, first : first + 256],
+                    pbuf[label, :ROWS, first : first + 256],
                     odd if q % 2 else even,
                     preferred_element_type=F32,
                 )
@@ -151,8 +205,7 @@
                 for batch in range(4):
                     spots, sums = [], []
                     for z in range(batch * 8, batch * 8 + 8):
-                        t = lists[label * (G * RT) + g * RT + z]
-                        spot = pl.ds(pl.multiple_of(t * U, 8), U)
+                        spot = pl.ds(pl.multiple_of(lists[label, g * RT + z], 8), U)
                         spots.append(spot)
                         sums.append(
                             acc[spot, :]
@@ -209,8 +262,8 @@
     out_ref[...] = total / gaps[...]
 
 
-def params():
-    return pltpu.CompilerParams(vmem_limit_bytes=50 * 1024 * 1024)
+def params(mib):
+    return pltpu.CompilerParams(vmem_limit_bytes=mib * 1024 * 1024)
 
 
 def per_device(c_matrix, beta_values, beta_rows, alpha_values, alpha_rows, gaps):
@@ -222,21 +275,23 @@
     h_to = (zh + sign * steps) % NZ * NC + (core ^ flips)
     h_from = (zh - sign * steps) % NZ * NC + (core ^ flips)
 
-    tiles = alpha_values[0, :, 0].reshape(G, 4, 8, U, U)
-    tiles = jnp.transpose(tiles, (2, 3, 1, 0, 4)).reshape(ROWS, COLS)
-    listed = jnp.pad(alpha_rows[0, :, 0].astype(BF).reshape(1, G * RT), ((0, 7), (0, COLS - G * RT)))
-    tiles = jnp.concatenate([tiles, listed], axis=0)
-    near = cross_z(tiles)
-    next_ = flip_zl(near)
-    far = cross_z(next_)
-    a_parts = []
-    for part in (tiles, near, next_, far):
-        a_parts += [part, flip_core(part)]
-    lists = jnp.stack([a[ROWS, : G * RT] for a in a_parts]).astype(jnp.int32)
-    tile_row = lists % RT
-    lists = ((tile_row // NH - y) % NY) * (G * NH) + lists // RT * NH + tile_row % NH
-
-    blocks = gather_c(c_matrix.reshape(ROWS, COLS))
+    c_own = c_matrix.reshape(ROWS, COLS)
+    over, left, right = flip_zl(c_own), shift_x(c_own, 1), shift_x(c_own, -1)
+    over_right, far, over_left = shift_x(over, -1), shift_x(left, 1), shift_x(over, 1)
+    over_far = shift_x(over_right, -1)
+    blocks = [c_own, right, far, left, over, over_right, over_far, over_left]
+
+    tiles = pl.pallas_call(
+        tiles_kernel,
+        out_shape=jax.ShapeDtypeStruct((ROWS + 8, COLS), BF),
+        in_specs=[VM] * 3,
+        out_specs=VM,
+        scratch_shapes=[pltpu.VMEM((ROWS, COLS), F32)],
+        compiler_params=params(12),
+        name="arrange_tiles",
+    )(jnp.transpose(alpha_values[0, :, 0], (0, 2, 3, 1)), alpha_rows[0, :, 0], turn_rows())
+    a_near = [tiles, cross_z(tiles, 1), send_step(tiles, 2), cross_z(tiles, 2)]
+
     col_block = beta_rows[0] // 6
     slots = (((col_block // NX) ^ zl) * NX + (col_block % NX - x) % NX) * 6 + beta_rows[0] % 6
     lane = jnp.arange(128, dtype=jnp.int32)
@@ -249,37 +304,49 @@
     x_out = pl.pallas_call(
         x_kernel,
         out_shape=[piece] * NZ,
-        in_specs=[SM] + [HBM] * 8 + [VM] * 2,
+        in_specs=[SM, HBM] + [VM] * 9,
         out_specs=[VM] * NZ,
         scratch_shapes=[
             pltpu.VMEM((8, ROWS, COLS), BF),
             pltpu.VMEM((ROWS, COLS), BF),
             pltpu.SemaphoreType.DMA((8,)),
         ],
-        compiler_params=params(),
+        compiler_params=params(12),
         name="beta_product",
-    )(slots.reshape(-1), *blocks, beta_values[0].reshape(6, 768, 128), perm_to)
+    )(slots.reshape(-1), pltpu.with_memory_space_constraint(c_own, pltpu.HBM), *blocks[1:], beta_values[0].reshape(6, 768, 128), perm_to)
     x_parts = exchange(x_out)
+    a_own = pl.pallas_call(
+        stack_kernel,
+        out_shape=jax.ShapeDtypeStruct((NZ, ROWS + 8, COLS), BF),
+        in_specs=[HBM] * 5,
+        out_specs=HBM,
+        scratch_shapes=[pltpu.SemaphoreType.DMA((NZ,))],
+        compiler_params=params(4),
+        name="stack_tiles",
+    )(x_out[0], *a_near)
 
     size = ROWS * NH
     part = jax.ShapeDtypeStruct((size // 4, 384), BF)
     own, s1, s2, s3 = pl.pallas_call(
         a_kernel,
         out_shape=[jax.ShapeDtypeStruct((size, 128), F32), part, part, part],
-        in_specs=[SM] + [HBM] * 16,
+        in_specs=[SM] + [HBM] * 10,
         out_specs=[VM] * 4,
         scratch_shapes=[
             pltpu.VMEM((size * NY, 128), F32),
-            pltpu.VMEM((NH, ROWS, COLS), BF),
+            pltpu.VMEM((NH, ROWS + 8, COLS), BF),
             pltpu.VMEM((NH, ROWS // 4, 384), BF),
             pltpu.VMEM((2, RT * U, 256), F32),
+            pltpu.VMEM((NH, G * RT), jnp.int32),
+            pltpu.SMEM((NH, G * RT), jnp.int32),
             pltpu.SemaphoreType.DMA((NH,)),
             pltpu.SemaphoreType.DMA((NH,)),
+            pltpu.SemaphoreType.DMA,
         ],
-        compiler_params=params(),
+        compiler_params=params(16),
         name="alpha_product",
-    )(lists.reshape(-1), *a_parts, *x_parts)
-    r1, r2, r3 = shift_y(s1, 1), shift_y(s2, 2), shift_y(s3, 3)
+    )(y.reshape(1), a_own, flip_core(a_own), *x_parts)
+    r2, r1, r3 = shift_y(s2, 2), shift_y(s1, 1), shift_y(s3, 3)
 
     y_out = pl.pallas_call(
         y_kernel,
@@ -287,7 +354,7 @@
         in_specs=[SM] + [VM] * 5,
         out_specs=[VM] * (NZ + 1),
         scratch_shapes=[pltpu.VMEM((size, 128), F32)],
-        compiler_params=params(),
+        compiler_params=params(12),
         name="y_sum",
     )(h_to, own, r1, r2, r3, jnp.eye(128, dtype=BF))
     mirrored = lax.all_to_all(y_out[NZ], ("y", "zl", "x"), split_axis=0, concat_axis=0, tiled=True)
@@ -297,7 +364,7 @@
         out_shape=jax.ShapeDtypeStruct((ROWS, COLS), F32),
         in_specs=[VM] * (NH + 3),
         out_specs=VM,
-        compiler_params=params(),
+        compiler_params=params(12),
         name="combine",
     )(*d_parts, mirrored.reshape(NY, ROWS, ROWS), perm_from, gaps.reshape(ROWS, COLS))
     return out.reshape(gaps.shape)

time: 127 us -> 110 us (0.87)
  local copies, waits for them, and re-layouts: 15 us -> 3.49 us
  other arithmetic: 3.63 us -> 1.1 us
  Pallas kernels: 17.8 us -> 16.2 us
    ppermute x12 -> x9, starting transfers between devices: 21.4 us -> 12.2 us  [flip_core(): return lax.ppermute(a, 'core', [(0, 1), (1, 0)])]
    unnamed x38 -> x16, local copies, waits for them, and re-layouts: 9.42 us -> 3.24 us
    ppermute x6 -> x7, starting transfers between devices: 8.85 us -> 14.2 us  [send_step(): return lax.ppermute(a, ('zh', 'zl'), moves)]
    reshape x1 -> x0, local copies, waits for them, and re-layouts: 2.81 us -> none  [per_device(): tiles = jnp.transpose(tiles, (2, 3, 1, 0, 4)).reshape(ROWS, COLS)]
    all_to_all x1, starting transfers between devices: 7.34 us -> 9.43 us  [per_device(): lax.all_to_all(y_out[NZ], ('y', 'zl', 'x'), split_axis=0, concat_axis=0,...]
    ppermute x3 -> x1, waiting for transfers between devices: 1.91 us -> 0.01 us  [flip_zl(): return lax.ppermute(a, 'zl', [(0, 1), (1, 0)])]
    ppermute x2, waiting for transfers between devices: 4.21 us -> 5.76 us  [cross_z(): return lax.ppermute(a, ('zh', 'zl'), moves)]
    ppermute x5 -> x6, starting transfers between devices: 7.91 us -> 8.91 us  [shift_x(): return lax.ppermute(a, 'x', [(i, (i + k) % NX) for i in range(NX)])]
  transfers between devices with their start and end apart: 32 -> 29, of which waited for: 9 -> 10; matrix products, arithmetic and copies ran while one was open for 4% -> 1% of each run, Pallas kernels for 4% -> 3%
where the time goes in v2:
time: 110 us
  starting transfers between devices  59.6 us (54%)
  waiting for transfers between devices  29.5 us (27%)
  Pallas kernels  16.2 us (15%)
  local copies, waits for them, and re-layouts  3.49 us (3%)
  other arithmetic  1.1 us (1%)
    ppermute x7, starting transfers between devices, send_step(): return lax.ppermute(a, ('zh', 'zl'), moves)  14.2 us
    ppermute x9, starting transfers between devices, flip_core(): return lax.ppermute(a, 'core', [(0, 1), (1, 0)])  12.2 us
    ppermute x3, waiting for transfers between devices, shift_y(): return lax.ppermute(a, 'y', [(i, (i + k) % NY) for i in range(NY)])  12 us
    all_to_all x1, starting transfers between devices, per_device(): lax.all_to_all(y_out[NZ], ('y', 'zl', 'x'), split_axis=0, concat_axis=0,...  9.43 us
    ppermute x6, starting transfers between devices, shift_x(): return lax.ppermute(a, 'x', [(i, (i + k) % NX) for i in range(NX)])  8.91 us
    pallas_call x1, Pallas kernels, per_device(): pl.pallas_call(a_kernel, out_shape=[jax.ShapeDtypeStruct((size, 128), F32...  8.24 us
    ppermute x2, starting transfers between devices, cross_z(): return lax.ppermute(a, ('zh', 'zl'), moves)  8.16 us
    ppermute x2, waiting for transfers between devices, cross_z(): return lax.ppermute(a, ('zh', 'zl'), moves)  5.76 us
  transfers between devices with their start and end apart: 29, of which 10 were waited for; matrix products, arithmetic and copies ran while one was open for 1% of the time, Pallas kernels for 3%

profile of v2, /device:TPU:1, one launch (start us, length us, event | category | flops | bytes accessed | tf_op | source)
XLA Modules:
  0.0 110.0 jit_solution(13127515436252965882)
XLA Ops:
  0.0 3.4 %collective-permute-start = (bf16[192,768]{1,0:T(8,128)(2,1)}, bf16[192,768]{1,0:T(8,128)(2,1)S(1)}, u32[]{:S(2)}, u32[]{:S(2)}) collective-permute-start(bf16[192,768]{1,0:T(8,128)(2,1)} %bitcast.17), channel_id=1, source_target_pairs={{0,3},{1,0},{2,1},{3,2},{4,7},{5,4},{6,5},{7,6},{8,11},{9,8},{10,9... | collective-permute-start | bytes 884744 | tf_op jit(solution)/shard_map/ppermute | solution.py:24
  3.4 1.6 %collective-permute-start.3 = (bf16[192,768]{1,0:T(8,128)(2,1)}, bf16[192,768]{1,0:T(8,128)(2,1)S(1)}, u32[]{:S(2)}, u32[]{:S(2)}) collective-permute-start(bf16[192,768]{1,0:T(8,128)(2,1)} %bitcast.19), channel_id=1, source_target_pairs={{0,4},{4,0},{1,5},{5,1},{2,6},{6,2},{3,7},{7,3},{8,12},{12,8},{9,1... | collective-permute-start | bytes 884744 | tf_op jit(solution)/shard_map/ppermute | solution.py:28
  5.0 1.3 %copy-done = bf16[1,8,1,32,24,24]{3,5,4,2,1,0:T(8,128)(2,1)S(1)} copy-done((bf16[1,8,1,32,24,24]{3,5,4,2,1,0:T(8,128)(2,1)S(1)}, bf16[1,8,1,32,24,24]{3,5,4,2,1,0:T(8,128)(2,1)}, u32[]{:S(2)}) %copy-start) | copy-done | bytes 294936
  6.3 1.3 %copy-done.2 = bf16[768,768]{1,0:T(8,128)(2,1)S(1)} copy-done((bf16[768,768]{1,0:T(8,128)(2,1)S(1)}, bf16[768,768]{1,0:T(8,128)(2,1)}, u32[]{:S(2)}) %copy-start.2) | copy-done | bytes 1179672
  7.6 0.7 copy-done.4
  8.3 0.7 arrange_tiles.1.refs_0_
  9.0 4.8 %collective-permute-start.7 = (bf16[200,768]{1,0:T(8,128)(2,1)S(1)}, bf16[200,768]{1,0:T(8,128)(2,1)S(1)}, u32[]{:S(2)}, u32[]{:S(2)}) collective-permute-start(bf16[200,768]{1,0:T(8,128)(2,1)S(1)} %arrange_tiles.1.refs_0_), channel_id=1, source_target_pairs={{0,52},{4,16},{16,4},{20,32},{32,20},{36,48},{48,36},{52,0},{1,53}... | collective-permute-start | bytes 921608 | tf_op jit(solution)/shard_map/ppermute | solution.py:44
  13.8 1.2 %collective-permute-start.8 = (bf16[200,768]{1,0:T(8,128)(2,1)S(1)}, bf16[200,768]{1,0:T(8,128)(2,1)S(1)}, u32[]{:S(2)}, u32[]{:S(2)}) collective-permute-start(bf16[200,768]{1,0:T(8,128)(2,1)S(1)} %arrange_tiles.1.refs_0_), channel_id=1, source_target_pairs={{0,48},{4,20},{16,0},{20,36},{32,16},{36,52},{48,32},{52,4},{1,49}... | collective-permute-start | bytes 921608 | tf_op jit(solution)/shard_map/ppermute | solution.py:53
  15.0 0.1 rem.118
  15.1 0.1 div.33
  15.2 0.1 ne.108
  15.3 0.0 collective-permute-done.1.refs_3_
  15.3 0.3 collective-permute-start.2
  15.6 2.6 %collective-permute-start.4 = (bf16[192,768]{1,0:T(8,128)(2,1)S(1)}, bf16[192,768]{1,0:T(8,128)(2,1)S(1)}, u32[]{:S(2)}, u32[]{:S(2)}) collective-permute-start(bf16[192,768]{1,0:T(8,128)(2,1)S(1)} %collective-permute-done.3.refs_4_), channel_id=1, source_target_pairs={{0,3},{1,0},{2,1},{3,2},{4,7},{5,4},{6,5},{7,6},{8,11},{9,8},{10,9... | collective-permute-start | bytes 884744 | tf_op jit(solution)/shard_map/ppermute | solution.py:24
  18.2 0.1 broadcast_add_fusion
  18.2 0.0 collective-permute-done.refs_1_
  18.2 3.4 %collective-permute-start.9 = (bf16[200,768]{1,0:T(8,128)(2,1)S(1)}, bf16[200,768]{1,0:T(8,128)(2,1)S(1)}, u32[]{:S(2)}, u32[]{:S(2)}) collective-permute-start(bf16[200,768]{1,0:T(8,128)(2,1)S(1)} %arrange_tiles.1.refs_0_), channel_id=1, source_target_pairs={{0,36},{4,32},{16,52},{20,48},{32,4},{36,0},{48,20},{52,16},{1,37}... | collective-permute-start | bytes 921608 | tf_op jit(solution)/shard_map/ppermute | solution.py:44
  21.6 1.6 %collective-permute-done.2.refs_2_ = bf16[192,768]{1,0:T(8,128)(2,1)S(1)} collective-permute-done((bf16[192,768]{1,0:T(8,128)(2,1)S(1)}, bf16[192,768]{1,0:T(8,128)(2,1)S(1)}, u32[]{:S(2)}, u32[]{:S(2)}) %collective-permute-start.2) | collective-permute-done | bytes 294944 | tf_op jit(solution)/shard_map/ppermute | solution.py:24
  23.3 2.7 %collective-permute-start.5 = (bf16[192,768]{1,0:T(8,128)(2,1)S(1)}, bf16[192,768]{1,0:T(8,128)(2,1)S(1)}, u32[]{:S(2)}, u32[]{:S(2)}) collective-permute-start(bf16[192,768]{1,0:T(8,128)(2,1)S(1)} %collective-permute-done.4.refs_5_), channel_id=1, source_target_pairs={{0,3},{1,0},{2,1},{3,2},{4,7},{5,4},{6,5},{7,6},{8,11},{9,8},{10,9... | collective-permute-start | bytes 884744 | tf_op jit(solution)/shard_map/ppermute | solution.py:24
  26.0 0.6 fusion.refs_9_
  26.6 3.5 %collective-permute-done.6.refs_7_ = bf16[192,768]{1,0:T(8,128)(2,1)S(1)} collective-permute-done((bf16[192,768]{1,0:T(8,128)(2,1)S(1)}, bf16[192,768]{1,0:T(8,128)(2,1)S(1)}, u32[]{:S(2)}, u32[]{:S(2)}) %collective-permute-start.6) | collective-permute-done | bytes 294944 | tf_op jit(solution)/shard_map/ppermute | solution.py:24
  30.1 3.0 %beta_product.1 = (bf16[2,48,384]{2,1,0:T(8,128)(2,1)S(1)}, bf16[2,48,384]{2,1,0:T(8,128)(2,1)S(1)}, bf16[2,48,384]{2,1,0:T(8,128)(2,1)S(1)}, bf16[2,48,384]{2,1,0:T(8,128)(2,1)S(1)}) custom-call(s32[36]{0:T(128)S(1)} %fusion.5.slots, bf16[192,768]{1,0:T(8,128)(2,1)} %bitcast.20, bf16[192,768]{1,0:T(8,128)(2,1)S(1)} %collective-permute-done.refs_1_, ...), custom_call_target="tpu_custom_call" | custom-call | tf_op jit(solution)/shard_map/beta_product/pallas_call | solution.py:304
  33.1 0.0 collective-permute-done.7.refs_1_
  33.1 0.0 collective-permute-done.8.refs_2_
  33.1 5.8 %collective-permute-done.9.refs_3_ = bf16[200,768]{1,0:T(8,128)(2,1)S(1)} collective-permute-done((bf16[200,768]{1,0:T(8,128)(2,1)S(1)}, bf16[200,768]{1,0:T(8,128)(2,1)S(1)}, u32[]{:S(2)}, u32[]{:S(2)}) %collective-permute-start.9) | collective-permute-done | bytes 307232 | tf_op jit(solution)/shard_map/ppermute | solution.py:44
  38.9 0.3 stack_tiles.1.refs_0_
  39.2 2.2 %collective-permute-start.10 = (bf16[4,200,768]{2,1,0:T(8,128)(2,1)S(1)}, bf16[4,200,768]{2,1,0:T(8,128)(2,1)S(1)}, u32[]{:S(2)}, u32[]{:S(2)}) collective-permute-start(bf16[4,200,768]{2,1,0:T(8,128)(2,1)S(1)} %stack_tiles.1.refs_0_), channel_id=1, source_target_pairs={{0,8},{8,0},{1,9},{9,1},{2,10},{10,2},{3,11},{11,3},{4,12},{12,4},... | collective-permute-start | bytes 3686408 | tf_op jit(solution)/shard_map/ppermute | solution.py:32
  41.4 2.8 %collective-permute-start.11 = (bf16[2,48,384]{2,1,0:T(8,128)(2,1)S(1)}, bf16[2,48,384]{2,1,0:T(8,128)(2,1)S(1)}, u32[]{:S(2)}, u32[]{:S(2)}) collective-permute-start(bf16[2,48,384]{2,1,0:T(8,128)(2,1)S(1)} %get-tuple-element.19), channel_id=1, source_target_pairs={{0,16},{4,52},{16,32},{20,4},{32,48},{36,20},{48,0},{52,36},{1,17}... | collective-permute-start | bytes 221192 | tf_op jit(solution)/shard_map/ppermute | solution.py:53
  44.3 1.9 %collective-permute-start.12 = (bf16[2,48,384]{2,1,0:T(8,128)(2,1)S(1)}, bf16[2,48,384]{2,1,0:T(8,128)(2,1)S(1)}, u32[]{:S(2)}, u32[]{:S(2)}) collective-permute-start(bf16[2,48,384]{2,1,0:T(8,128)(2,1)S(1)} %get-tuple-element.20), channel_id=1, source_target_pairs={{0,48},{4,20},{16,0},{20,36},{32,16},{36,52},{48,32},{52,4},{1,49}... | collective-permute-start | bytes 221192 | tf_op jit(solution)/shard_map/ppermute | solution.py:53
  46.2 2.1 %collective-permute-start.13 = (bf16[2,48,384]{2,1,0:T(8,128)(2,1)S(1)}, bf16[2,48,384]{2,1,0:T(8,128)(2,1)S(1)}, u32[]{:S(2)}, u32[]{:S(2)}) collective-permute-start(bf16[2,48,384]{2,1,0:T(8,128)(2,1)S(1)} %get-tuple-element.21), channel_id=1, source_target_pairs={{0,32},{4,36},{16,48},{20,52},{32,0},{36,4},{48,16},{52,20},{1,33}... | collective-permute-start | bytes 221192 | tf_op jit(solution)/shard_map/ppermute | solution.py:53
  48.3 0.6 collective-permute-start.14
  48.9 0.6 collective-permute-start.15
  49.5 0.7 collective-permute-done.12.refs_4_
  50.2 0.5 collective-permute-start.16
  50.7 2.6 %collective-permute-done.13.refs_5_ = bf16[2,48,384]{2,1,0:T(8,128)(2,1)S(1)} collective-permute-done((bf16[2,48,384]{2,1,0:T(8,128)(2,1)S(1)}, bf16[2,48,384]{2,1,0:T(8,128)(2,1)S(1)}, u32[]{:S(2)}, u32[]{:S(2)}) %collective-permute-start.13) | collective-permute-done | bytes 73760 | tf_op jit(solution)/shard_map/ppermute | solution.py:53
  53.3 1.6 %collective-permute-start.17 = (bf16[2,48,384]{2,1,0:T(8,128)(2,1)S(1)}, bf16[2,48,384]{2,1,0:T(8,128)(2,1)S(1)}, u32[]{:S(2)}, u32[]{:S(2)}) collective-permute-start(bf16[2,48,384]{2,1,0:T(8,128)(2,1)S(1)} %collective-permute-done.13.refs_5_), channel_id=1, source_target_pairs={{0,8},{8,0},{1,9},{9,1},{2,10},{10,2},{3,11},{11,3},{4,12},{12,4},... | collective-permute-start | bytes 221192 | tf_op jit(solution)/shard_map/ppermute | solution.py:32
  54.9 0.0 collective-permute-done.14.refs_6_
  54.9 0.0 collective-permute-done.15.refs_7_
  54.9 0.0 collective-permute-done.16.refs_8_
  54.9 0.9 collective-permute-done.17.refs_9_
  55.8 0.0 collective-permute-done.10.refs_1_
  55.8 8.2 %alpha_product.1 = (f32[1536,128]{1,0:T(8,128)S(1)}, bf16[384,384]{1,0:T(8,128)(2,1)S(1)}, bf16[384,384]{1,0:T(8,128)(2,1)S(1)}, bf16[384,384]{1,0:T(8,128)(2,1)S(1)}) custom-call(s32[1]{0:T(128)} %bitcast.place, bf16[4,200,768]{2,1,0:T(8,128)(2,1)S(1)} %stack_tiles.1.refs_0_, bf16[4,200,768]{2,1,0:T(8,128)(2,1)S(1)} %collective-permute-done.10.refs_1_, ...), custom_call_target="tpu_custom_call" | custom-call | tf_op jit(solution)/shard_map/alpha_product/pallas_call | solution.py:330
  64.1 1.4 %collective-permute-start.18 = (bf16[384,384]{1,0:T(8,128)(2,1)S(1)}, bf16[384,384]{1,0:T(8,128)(2,1)S(1)}, u32[]{:S(2)}, u32[]{:S(2)}) collective-permute-start(bf16[384,384]{1,0:T(8,128)(2,1)S(1)} %get-tuple-element.23), channel_id=1, source_target_pairs={{0,64},{64,128},{128,192},{192,0},{1,65},{65,129},{129,193},{193,1... | collective-permute-start | bytes 884744 | tf_op jit(solution)/shard_map/ppermute | solution.py:36
  65.5 2.6 %collective-permute-start.19 = (bf16[384,384]{1,0:T(8,128)(2,1)S(1)}, bf16[384,384]{1,0:T(8,128)(2,1)S(1)}, u32[]{:S(2)}, u32[]{:S(2)}) collective-permute-start(bf16[384,384]{1,0:T(8,128)(2,1)S(1)} %get-tuple-element.24), channel_id=1, source_target_pairs={{0,128},{64,192},{128,0},{192,64},{1,129},{65,193},{129,1},{193,65... | collective-permute-start | bytes 884744 | tf_op jit(solution)/shard_map/ppermute | solution.py:36
  68.1 1.1 collective-permute-start.20
  69.2 4.6 %collective-permute-done.18.r1 = bf16[384,384]{1,0:T(8,128)(2,1)S(1)} collective-permute-done((bf16[384,384]{1,0:T(8,128)(2,1)S(1)}, bf16[384,384]{1,0:T(8,128)(2,1)S(1)}, u32[]{:S(2)}, u32[]{:S(2)}) %collective-permute-start.18) | collective-permute-done | bytes 294944 | tf_op jit(solution)/shard_map/ppermute | solution.py:36
  73.7 7.4 %collective-permute-done.19.r2 = bf16[384,384]{1,0:T(8,128)(2,1)S(1)} collective-permute-done((bf16[384,384]{1,0:T(8,128)(2,1)S(1)}, bf16[384,384]{1,0:T(8,128)(2,1)S(1)}, u32[]{:S(2)}, u32[]{:S(2)}) %collective-permute-start.19) | collective-permute-done | bytes 294944 | tf_op jit(solution)/shard_map/ppermute | solution.py:36
  81.2 0.0 collective-permute-done.20.r3
  81.2 1.9 %y_sum.1 = (bf16[2,48,384]{2,1,0:T(8,128)(2,1)S(1)}, bf16[2,48,384]{2,1,0:T(8,128)(2,1)S(1)}, bf16[2,48,384]{2,1,0:T(8,128)(2,1)S(1)}, bf16[2,48,384]{2,1,0:T(8,128)(2,1)S(1)}, bf16[32,24,192]{2,1,0:T(8,128)(2,1)}) custom-call(s32[8]{0:T(128)S(1)} %get-tuple-element.34.dests, f32[1536,128]{1,0:T(8,128)S(1)} %get-tuple-element.22.own, ...), custom_call_target="tpu_custom_call" | custom-call | tf_op jit(solution)/shard_map/y_sum/pallas_call | solution.py:351
  83.1 9.4 %all-to-all-start = ((bf16[32,24,192]{2,1,0:T(8,128)(2,1)}), bf16[32,24,192]{2,1,0:T(8,128)(2,1)S(1)}, u32[]{:S(2)}, u32[]{:S(2)}) async-start(bf16[32,24,192]{2,1,0:T(8,128)(2,1)} %get-tuple-element.30), calls=%async_computation | async-start | bytes 786432 | tf_op jit(solution)/shard_map/all_to_all | solution.py:360
  92.5 0.8 collective-permute-start.21
  93.3 2.9 %collective-permute-start.22 = (bf16[2,48,384]{2,1,0:T(8,128)(2,1)S(1)}, bf16[2,48,384]{2,1,0:T(8,128)(2,1)S(1)}, u32[]{:S(2)}, u32[]{:S(2)}) collective-permute-start(bf16[2,48,384]{2,1,0:T(8,128)(2,1)S(1)} %get-tuple-element.28), channel_id=1, source_target_pairs={{0,48},{4,20},{16,0},{20,36},{32,16},{36,52},{48,32},{52,4},{1,49}... | collective-permute-start | bytes 221192 | tf_op jit(solution)/shard_map/ppermute | solution.py:53
  96.2 2.5 %collective-permute-start.23 = (bf16[2,48,384]{2,1,0:T(8,128)(2,1)S(1)}, bf16[2,48,384]{2,1,0:T(8,128)(2,1)S(1)}, u32[]{:S(2)}, u32[]{:S(2)}) collective-permute-start(bf16[2,48,384]{2,1,0:T(8,128)(2,1)S(1)} %get-tuple-element.29), channel_id=1, source_target_pairs={{0,32},{4,36},{16,48},{20,52},{32,0},{36,4},{48,16},{52,20},{1,33}... | collective-permute-start | bytes 221192 | tf_op jit(solution)/shard_map/ppermute | solution.py:53
  98.7 2.0 %collective-permute-start.24 = (bf16[2,48,384]{2,1,0:T(8,128)(2,1)S(1)}, bf16[2,48,384]{2,1,0:T(8,128)(2,1)S(1)}, u32[]{:S(2)}, u32[]{:S(2)}) collective-permute-start(bf16[2,48,384]{2,1,0:T(8,128)(2,1)S(1)} %get-tuple-element.26.refs_0_), channel_id=1, source_target_pairs={{0,8},{8,0},{1,9},{9,1},{2,10},{10,2},{3,11},{11,3},{4,12},{12,4},... | collective-permute-start | bytes 221192 | tf_op jit(solution)/shard_map/ppermute | solution.py:32
  100.7 2.8 %collective-permute-start.25 = (bf16[2,48,384]{2,1,0:T(8,128)(2,1)S(1)}, bf16[2,48,384]{2,1,0:T(8,128)(2,1)S(1)}, u32[]{:S(2)}, u32[]{:S(2)}) collective-permute-start(bf16[2,48,384]{2,1,0:T(8,128)(2,1)S(1)} %collective-permute-done.21.refs_1_), channel_id=1, source_target_pairs={{0,8},{8,0},{1,9},{9,1},{2,10},{10,2},{3,11},{11,3},{4,12},{12,4},... | collective-permute-start | bytes 221192 | tf_op jit(solution)/shard_map/ppermute | solution.py:32
  103.5 0.0 collective-permute-done.22.refs_2_
  103.5 0.0 collective-permute-start.26
  103.5 1.8 %collective-permute-done.23.refs_3_ = bf16[2,48,384]{2,1,0:T(8,128)(2,1)S(1)} collective-permute-done((bf16[2,48,384]{2,1,0:T(8,128)(2,1)S(1)}, bf16[2,48,384]{2,1,0:T(8,128)(2,1)S(1)}, u32[]{:S(2)}, u32[]{:S(2)}) %collective-permute-start.23) | collective-permute-done | bytes 73760 | tf_op jit(solution)/shard_map/ppermute | solution.py:53
  105.3 1.9 %collective-permute-start.27 = (bf16[2,48,384]{2,1,0:T(8,128)(2,1)S(1)}, bf16[2,48,384]{2,1,0:T(8,128)(2,1)S(1)}, u32[]{:S(2)}, u32[]{:S(2)}) collective-permute-start(bf16[2,48,384]{2,1,0:T(8,128)(2,1)S(1)} %collective-permute-done.23.refs_3_), channel_id=1, source_target_pairs={{0,8},{8,0},{1,9},{9,1},{2,10},{10,2},{3,11},{11,3},{4,12},{12,4},... | collective-permute-start | bytes 221192 | tf_op jit(solution)/shard_map/ppermute | solution.py:32
  107.1 0.3 fusion.1.refs_9_
  107.5 0.0 collective-permute-done.24.refs_4_
  107.5 0.0 collective-permute-done.26.refs_6_
  107.5 0.6 collective-permute-done.27.refs_7_
  108.1 1.9 %combine.1 = f32[192,768]{1,0:T(8,128)} custom-call(bf16[2,48,384]{2,1,0:T(8,128)(2,1)S(1)} %get-tuple-element.26.refs_0_, bf16[2,48,384]{2,1,0:T(8,128)(2,1)S(1)} %collective-permute-done.21.refs_1_, bf16[2,48,384]{2,1,0:T(8,128)(2,1)S(1)} %collective-permute-done.22.refs_2_, bf16[2,48,384]{2,1,0:T(8,128)(2,1)S(1)} %collective-permute-done.23.refs_3_, ...), custom_call_target="tpu_custom_call" | custom-call | tf_op jit(solution)/shard_map/combine/pallas_call | solution.py:362
  (28 shorter events, 0.2 us)
Async XLA Ops:
  0.0 15.3 %copy-start.6 = (s32[8]{0:T(128)S(1)}, s32[8]{0:T(128)}, u32[]{:S(2)}) copy-start(s32[8]{0:T(128)} %constant.114.clone) | copy-start | bytes 100
  0.0 15.3 %copy-start.7 = (s32[8]{0:T(128)S(1)}, s32[8]{0:T(128)}, u32[]{:S(2)}) copy-start(s32[8]{0:T(128)} %constant.113.clone) | copy-start | bytes 100
  0.0 14.9 %copy-start.5 = (s32[1,6,6]{2,0,1:T(1,128)S(1)}, s32[1,6,6]{2,0,1:T(1,128)}, u32[]{:S(2)}) copy-start(s32[1,6,6]{2,0,1:T(1,128)} %param.11) | copy-start | bytes 436
  0.0 18.2 %collective-permute-start = (bf16[192,768]{1,0:T(8,128)(2,1)}, bf16[192,768]{1,0:T(8,128)(2,1)S(1)}, u32[]{:S(2)}, u32[]{:S(2)}) collective-permute-start(bf16[192,768]{1,0:T(8,128)(2,1)} %bitcast.17), channel_id=1, source_target_pairs={{0,3},{1,0},{2,1},{3,2},{4,7},{5,4},{6,5},{7,6},{8,11},{9,8},{10,9... | collective-permute-start | bytes 884744 | tf_op jit(solution)/shard_map/ppermute | solution.py:24
  3.4 11.9 %collective-permute-start.1 = (bf16[192,768]{1,0:T(8,128)(2,1)}, bf16[192,768]{1,0:T(8,128)(2,1)S(1)}, u32[]{:S(2)}, u32[]{:S(2)}) collective-permute-start(bf16[192,768]{1,0:T(8,128)(2,1)} %bitcast.18), channel_id=1, source_target_pairs={{0,1},{1,2},{2,3},{3,0},{4,5},{5,6},{6,7},{7,4},{8,9},{9,10},{10,1... | collective-permute-start | bytes 884744 | tf_op jit(solution)/shard_map/ppermute | solution.py:24
  3.4 12.2 %collective-permute-start.3 = (bf16[192,768]{1,0:T(8,128)(2,1)}, bf16[192,768]{1,0:T(8,128)(2,1)S(1)}, u32[]{:S(2)}, u32[]{:S(2)}) collective-permute-start(bf16[192,768]{1,0:T(8,128)(2,1)} %bitcast.19), channel_id=1, source_target_pairs={{0,4},{4,0},{1,5},{5,1},{2,6},{6,2},{3,7},{7,3},{8,12},{12,8},{9,1... | collective-permute-start | bytes 884744 | tf_op jit(solution)/shard_map/ppermute | solution.py:28
  5.0 1.3 %copy-start = (bf16[1,8,1,32,24,24]{3,5,4,2,1,0:T(8,128)(2,1)S(1)}, bf16[1,8,1,32,24,24]{3,5,4,2,1,0:T(8,128)(2,1)}, u32[]{:S(2)}) copy-start(bf16[1,8,1,32,24,24]{3,5,4,2,1,0:T(8,128)(2,1)} %param.12) | copy-start | bytes 884740
  6.3 1.3 %copy-start.2 = (bf16[768,768]{1,0:T(8,128)(2,1)S(1)}, bf16[768,768]{1,0:T(8,128)(2,1)}, u32[]{:S(2)}) copy-start(bf16[768,768]{1,0:T(8,128)(2,1)} %constant.115.clone.turn) | copy-start | bytes 3538948
  7.6 0.7 copy-start.4
  8.3 21.8 %copy-start.1 = (bf16[1,6,6,128,128]{4,3,2,1,0:T(8,128)(2,1)S(1)}, bf16[1,6,6,128,128]{4,3,2,1,0:T(8,128)(2,1)}, u32[]{:S(2)}) copy-start(bf16[1,6,6,128,128]{4,3,2,1,0:T(8,128)(2,1)} %param.10) | copy-start | bytes 3538948
  9.0 24.1 %collective-permute-start.7 = (bf16[200,768]{1,0:T(8,128)(2,1)S(1)}, bf16[200,768]{1,0:T(8,128)(2,1)S(1)}, u32[]{:S(2)}, u32[]{:S(2)}) collective-permute-start(bf16[200,768]{1,0:T(8,128)(2,1)S(1)} %arrange_tiles.1.refs_0_), channel_id=1, source_target_pairs={{0,52},{4,16},{16,4},{20,32},{32,20},{36,48},{48,36},{52,0},{1,53}... | collective-permute-start | bytes 921608 | tf_op jit(solution)/shard_map/ppermute | solution.py:44
  13.8 19.3 %collective-permute-start.8 = (bf16[200,768]{1,0:T(8,128)(2,1)S(1)}, bf16[200,768]{1,0:T(8,128)(2,1)S(1)}, u32[]{:S(2)}, u32[]{:S(2)}) collective-permute-start(bf16[200,768]{1,0:T(8,128)(2,1)S(1)} %arrange_tiles.1.refs_0_), channel_id=1, source_target_pairs={{0,48},{4,20},{16,0},{20,36},{32,16},{36,52},{48,32},{52,4},{1,49}... | collective-permute-start | bytes 921608 | tf_op jit(solution)/shard_map/ppermute | solution.py:53
  15.3 8.0 %collective-permute-start.2 = (bf16[192,768]{1,0:T(8,128)(2,1)S(1)}, bf16[192,768]{1,0:T(8,128)(2,1)S(1)}, u32[]{:S(2)}, u32[]{:S(2)}) collective-permute-start(bf16[192,768]{1,0:T(8,128)(2,1)S(1)} %collective-permute-done.1.refs_3_), channel_id=1, source_target_pairs={{0,1},{1,2},{2,3},{3,0},{4,5},{5,6},{6,7},{7,4},{8,9},{9,10},{10,1... | collective-permute-start | bytes 884744 | tf_op jit(solution)/shard_map/ppermute | solution.py:24
  15.6 7.7 %collective-permute-start.4 = (bf16[192,768]{1,0:T(8,128)(2,1)S(1)}, bf16[192,768]{1,0:T(8,128)(2,1)S(1)}, u32[]{:S(2)}, u32[]{:S(2)}) collective-permute-start(bf16[192,768]{1,0:T(8,128)(2,1)S(1)} %collective-permute-done.3.refs_4_), channel_id=1, source_target_pairs={{0,3},{1,0},{2,1},{3,2},{4,7},{5,4},{6,5},{7,6},{8,11},{9,8},{10,9... | collective-permute-start | bytes 884744 | tf_op jit(solution)/shard_map/ppermute | solution.py:24
  18.2 20.6 %collective-permute-start.9 = (bf16[200,768]{1,0:T(8,128)(2,1)S(1)}, bf16[200,768]{1,0:T(8,128)(2,1)S(1)}, u32[]{:S(2)}, u32[]{:S(2)}) collective-permute-start(bf16[200,768]{1,0:T(8,128)(2,1)S(1)} %arrange_tiles.1.refs_0_), channel_id=1, source_target_pairs={{0,36},{4,32},{16,52},{20,48},{32,4},{36,0},{48,20},{52,16},{1,37}... | collective-permute-start | bytes 921608 | tf_op jit(solution)/shard_map/ppermute | solution.py:44
  23.3 6.8 %collective-permute-start.6 = (bf16[192,768]{1,0:T(8,128)(2,1)S(1)}, bf16[192,768]{1,0:T(8,128)(2,1)S(1)}, u32[]{:S(2)}, u32[]{:S(2)}) collective-permute-start(bf16[192,768]{1,0:T(8,128)(2,1)S(1)} %collective-permute-done.3.refs_4_), channel_id=1, source_target_pairs={{0,1},{1,2},{2,3},{3,0},{4,5},{5,6},{6,7},{7,4},{8,9},{9,10},{10,1... | collective-permute-start | bytes 884744 | tf_op jit(solution)/shard_map/ppermute | solution.py:24
  23.3 6.8 %collective-permute-start.5 = (bf16[192,768]{1,0:T(8,128)(2,1)S(1)}, bf16[192,768]{1,0:T(8,128)(2,1)S(1)}, u32[]{:S(2)}, u32[]{:S(2)}) collective-permute-start(bf16[192,768]{1,0:T(8,128)(2,1)S(1)} %collective-permute-done.4.refs_5_), channel_id=1, source_target_pairs={{0,3},{1,0},{2,1},{3,2},{4,7},{5,4},{6,5},{7,6},{8,11},{9,8},{10,9... | collective-permute-start | bytes 884744 | tf_op jit(solution)/shard_map/ppermute | solution.py:24
  39.2 16.6 %collective-permute-start.10 = (bf16[4,200,768]{2,1,0:T(8,128)(2,1)S(1)}, bf16[4,200,768]{2,1,0:T(8,128)(2,1)S(1)}, u32[]{:S(2)}, u32[]{:S(2)}) collective-permute-start(bf16[4,200,768]{2,1,0:T(8,128)(2,1)S(1)} %stack_tiles.1.refs_0_), channel_id=1, source_target_pairs={{0,8},{8,0},{1,9},{9,1},{2,10},{10,2},{3,11},{11,3},{4,12},{12,4},... | collective-permute-start | bytes 3686408 | tf_op jit(solution)/shard_map/ppermute | solution.py:32
  41.4 7.5 %collective-permute-start.11 = (bf16[2,48,384]{2,1,0:T(8,128)(2,1)S(1)}, bf16[2,48,384]{2,1,0:T(8,128)(2,1)S(1)}, u32[]{:S(2)}, u32[]{:S(2)}) collective-permute-start(bf16[2,48,384]{2,1,0:T(8,128)(2,1)S(1)} %get-tuple-element.19), channel_id=1, source_target_pairs={{0,16},{4,52},{16,32},{20,4},{32,48},{36,20},{48,0},{52,36},{1,17}... | collective-permute-start | bytes 221192 | tf_op jit(solution)/shard_map/ppermute | solution.py:53
  44.3 6.0 %collective-permute-start.12 = (bf16[2,48,384]{2,1,0:T(8,128)(2,1)S(1)}, bf16[2,48,384]{2,1,0:T(8,128)(2,1)S(1)}, u32[]{:S(2)}, u32[]{:S(2)}) collective-permute-start(bf16[2,48,384]{2,1,0:T(8,128)(2,1)S(1)} %get-tuple-element.20), channel_id=1, source_target_pairs={{0,48},{4,20},{16,0},{20,36},{32,16},{36,52},{48,32},{52,4},{1,49}... | collective-permute-start | bytes 221192 | tf_op jit(solution)/shard_map/ppermute | solution.py:53
  46.2 7.1 %collective-permute-start.13 = (bf16[2,48,384]{2,1,0:T(8,128)(2,1)S(1)}, bf16[2,48,384]{2,1,0:T(8,128)(2,1)S(1)}, u32[]{:S(2)}, u32[]{:S(2)}) collective-permute-start(bf16[2,48,384]{2,1,0:T(8,128)(2,1)S(1)} %get-tuple-element.21), channel_id=1, source_target_pairs={{0,32},{4,36},{16,48},{20,52},{32,0},{36,4},{48,16},{52,20},{1,33}... | collective-permute-start | bytes 221192 | tf_op jit(solution)/shard_map/ppermute | solution.py:53
  48.3 6.6 %collective-permute-start.14 = (bf16[2,48,384]{2,1,0:T(8,128)(2,1)S(1)}, bf16[2,48,384]{2,1,0:T(8,128)(2,1)S(1)}, u32[]{:S(2)}, u32[]{:S(2)}) collective-permute-start(bf16[2,48,384]{2,1,0:T(8,128)(2,1)S(1)} %get-tuple-element.18.after.refs_2_), channel_id=1, source_target_pairs={{0,8},{8,0},{1,9},{9,1},{2,10},{10,2},{3,11},{11,3},{4,12},{12,4},... | collective-permute-start | bytes 221192 | tf_op jit(solution)/shard_map/ppermute | solution.py:32
  48.9 6.0 %collective-permute-start.15 = (bf16[2,48,384]{2,1,0:T(8,128)(2,1)S(1)}, bf16[2,48,384]{2,1,0:T(8,128)(2,1)S(1)}, u32[]{:S(2)}, u32[]{:S(2)}) collective-permute-start(bf16[2,48,384]{2,1,0:T(8,128)(2,1)S(1)} %collective-permute-done.11.refs_3_), channel_id=1, source_target_pairs={{0,8},{8,0},{1,9},{9,1},{2,10},{10,2},{3,11},{11,3},{4,12},{12,4},... | collective-permute-start | bytes 221192 | tf_op jit(solution)/shard_map/ppermute | solution.py:32
  50.2 4.7 %collective-permute-start.16 = (bf16[2,48,384]{2,1,0:T(8,128)(2,1)S(1)}, bf16[2,48,384]{2,1,0:T(8,128)(2,1)S(1)}, u32[]{:S(2)}, u32[]{:S(2)}) collective-permute-start(bf16[2,48,384]{2,1,0:T(8,128)(2,1)S(1)} %collective-permute-done.12.refs_4_), channel_id=1, source_target_pairs={{0,8},{8,0},{1,9},{9,1},{2,10},{10,2},{3,11},{11,3},{4,12},{12,4},... | collective-permute-start | bytes 221192 | tf_op jit(solution)/shard_map/ppermute | solution.py:32
  53.3 2.5 %collective-permute-start.17 = (bf16[2,48,384]{2,1,0:T(8,128)(2,1)S(1)}, bf16[2,48,384]{2,1,0:T(8,128)(2,1)S(1)}, u32[]{:S(2)}, u32[]{:S(2)}) collective-permute-start(bf16[2,48,384]{2,1,0:T(8,128)(2,1)S(1)} %collective-permute-done.13.refs_5_), channel_id=1, source_target_pairs={{0,8},{8,0},{1,9},{9,1},{2,10},{10,2},{3,11},{11,3},{4,12},{12,4},... | collective-permute-start | bytes 221192 | tf_op jit(solution)/shard_map/ppermute | solution.py:32
  64.1 9.6 %collective-permute-start.18 = (bf16[384,384]{1,0:T(8,128)(2,1)S(1)}, bf16[384,384]{1,0:T(8,128)(2,1)S(1)}, u32[]{:S(2)}, u32[]{:S(2)}) collective-permute-start(bf16[384,384]{1,0:T(8,128)(2,1)S(1)} %get-tuple-element.23), channel_id=1, source_target_pairs={{0,64},{64,128},{128,192},{192,0},{1,65},{65,129},{129,193},{193,1... | collective-permute-start | bytes 884744 | tf_op jit(solution)/shard_map/ppermute | solution.py:36
  65.5 15.7 %collective-permute-start.19 = (bf16[384,384]{1,0:T(8,128)(2,1)S(1)}, bf16[384,384]{1,0:T(8,128)(2,1)S(1)}, u32[]{:S(2)}, u32[]{:S(2)}) collective-permute-start(bf16[384,384]{1,0:T(8,128)(2,1)S(1)} %get-tuple-element.24), channel_id=1, source_target_pairs={{0,128},{64,192},{128,0},{192,64},{1,129},{65,193},{129,1},{193,65... | collective-permute-start | bytes 884744 | tf_op jit(solution)/shard_map/ppermute | solution.py:36
  68.1 13.1 %collective-permute-start.20 = (bf16[384,384]{1,0:T(8,128)(2,1)S(1)}, bf16[384,384]{1,0:T(8,128)(2,1)S(1)}, u32[]{:S(2)}, u32[]{:S(2)}) collective-permute-start(bf16[384,384]{1,0:T(8,128)(2,1)S(1)} %get-tuple-element.25), channel_id=1, source_target_pairs={{0,192},{64,0},{128,64},{192,128},{1,193},{65,1},{129,65},{193,129... | collective-permute-start | bytes 884744 | tf_op jit(solution)/shard_map/ppermute | solution.py:36
  83.1 25.0 %copy-start.3 = (f32[8,24,768]{2,1,0:T(8,128)S(1)}, f32[8,24,768]{2,1,0:T(8,128)}, u32[]{:S(2)}) copy-start(f32[8,24,768]{2,1,0:T(8,128)} %param.14) | copy-start | bytes 1769476
  83.1 25.0 %all-to-all-start = ((bf16[32,24,192]{2,1,0:T(8,128)(2,1)}), bf16[32,24,192]{2,1,0:T(8,128)(2,1)S(1)}, u32[]{:S(2)}, u32[]{:S(2)}) async-start(bf16[32,24,192]{2,1,0:T(8,128)(2,1)} %get-tuple-element.30), calls=%async_computation | async-start | bytes 786432 | tf_op jit(solution)/shard_map/all_to_all | solution.py:360
  92.5 8.2 %collective-permute-start.21 = (bf16[2,48,384]{2,1,0:T(8,128)(2,1)S(1)}, bf16[2,48,384]{2,1,0:T(8,128)(2,1)S(1)}, u32[]{:S(2)}, u32[]{:S(2)}) collective-permute-start(bf16[2,48,384]{2,1,0:T(8,128)(2,1)S(1)} %get-tuple-element.27), channel_id=1, source_target_pairs={{0,16},{4,52},{16,32},{20,4},{32,48},{36,20},{48,0},{52,36},{1,17}... | collective-permute-start | bytes 221192 | tf_op jit(solution)/shard_map/ppermute | solution.py:53
  93.3 10.2 %collective-permute-start.22 = (bf16[2,48,384]{2,1,0:T(8,128)(2,1)S(1)}, bf16[2,48,384]{2,1,0:T(8,128)(2,1)S(1)}, u32[]{:S(2)}, u32[]{:S(2)}) collective-permute-start(bf16[2,48,384]{2,1,0:T(8,128)(2,1)S(1)} %get-tuple-element.28), channel_id=1, source_target_pairs={{0,48},{4,20},{16,0},{20,36},{32,16},{36,52},{48,32},{52,4},{1,49}... | collective-permute-start | bytes 221192 | tf_op jit(solution)/shard_map/ppermute | solution.py:53
  96.2 9.1 %collective-permute-start.23 = (bf16[2,48,384]{2,1,0:T(8,128)(2,1)S(1)}, bf16[2,48,384]{2,1,0:T(8,128)(2,1)S(1)}, u32[]{:S(2)}, u32[]{:S(2)}) collective-permute-start(bf16[2,48,384]{2,1,0:T(8,128)(2,1)S(1)} %get-tuple-element.29), channel_id=1, source_target_pairs={{0,32},{4,36},{16,48},{20,52},{32,0},{36,4},{48,16},{52,20},{1,33}... | collective-permute-start | bytes 221192 | tf_op jit(solution)/shard_map/ppermute | solution.py:53
  98.7 8.8 %collective-permute-start.24 = (bf16[2,48,384]{2,1,0:T(8,128)(2,1)S(1)}, bf16[2,48,384]{2,1,0:T(8,128)(2,1)S(1)}, u32[]{:S(2)}, u32[]{:S(2)}) collective-permute-start(bf16[2,48,384]{2,1,0:T(8,128)(2,1)S(1)} %get-tuple-element.26.refs_0_), channel_id=1, source_target_pairs={{0,8},{8,0},{1,9},{9,1},{2,10},{10,2},{3,11},{11,3},{4,12},{12,4},... | collective-permute-start | bytes 221192 | tf_op jit(solution)/shard_map/ppermute | solution.py:32
  100.7 6.8 %collective-permute-start.25 = (bf16[2,48,384]{2,1,0:T(8,128)(2,1)S(1)}, bf16[2,48,384]{2,1,0:T(8,128)(2,1)S(1)}, u32[]{:S(2)}, u32[]{:S(2)}) collective-permute-start(bf16[2,48,384]{2,1,0:T(8,128)(2,1)S(1)} %collective-permute-done.21.refs_1_), channel_id=1, source_target_pairs={{0,8},{8,0},{1,9},{9,1},{2,10},{10,2},{3,11},{11,3},{4,12},{12,4},... | collective-permute-start | bytes 221192 | tf_op jit(solution)/shard_map/ppermute | solution.py:32
  103.5 4.0 %collective-permute-start.26 = (bf16[2,48,384]{2,1,0:T(8,128)(2,1)S(1)}, bf16[2,48,384]{2,1,0:T(8,128)(2,1)S(1)}, u32[]{:S(2)}, u32[]{:S(2)}) collective-permute-start(bf16[2,48,384]{2,1,0:T(8,128)(2,1)S(1)} %collective-permute-done.22.refs_2_), channel_id=1, source_target_pairs={{0,8},{8,0},{1,9},{9,1},{2,10},{10,2},{3,11},{11,3},{4,12},{12,4},... | collective-permute-start | bytes 221192 | tf_op jit(solution)/shard_map/ppermute | solution.py:32
  105.3 2.8 %collective-permute-start.27 = (bf16[2,48,384]{2,1,0:T(8,128)(2,1)S(1)}, bf16[2,48,384]{2,1,0:T(8,128)(2,1)S(1)}, u32[]{:S(2)}, u32[]{:S(2)}) collective-permute-start(bf16[2,48,384]{2,1,0:T(8,128)(2,1)S(1)} %collective-permute-done.23.refs_3_), channel_id=1, source_target_pairs={{0,8},{8,0},{1,9},{9,1},{2,10},{10,2},{3,11},{11,3},{4,12},{12,4},... | collective-permute-start | bytes 221192 | tf_op jit(solution)/shard_map/ppermute | solution.py:32

commit v3 on v2

--- a/solution.py
+++ b/solution.py
@@ -14,6 +14,8 @@
 ROWS = G * U
 COLS = 768
 PART = COLS // NH
+FIRST = 6
+ARRIVAL = (4, 6, 5, 7, 3, 2, 1, 0)
 STEPS = (0, 1, -1, 2)
 HBM = pl.BlockSpec(memory_space=pltpu.HBM)
 VM = pl.BlockSpec(memory_space=pltpu.VMEM)
@@ -51,11 +53,6 @@
             to = (zh + (1 - 2 * zl) * STEPS[label]) % NZ
             moves.append((zh * 2 + zl, to * 2 + zl))
     return lax.ppermute(a, ("zh", "zl"), moves)
-
-
-def exchange(payloads):
-    direct = [payloads[0]] + [send_step(payloads[k], k) for k in range(1, NZ)]
-    return direct + [flip_core(a) for a in direct]
 
 
 def pack(pieces):
@@ -85,7 +82,7 @@
 def x_kernel(slots, *refs):
     blocks, (b_ref, perm_ref), outs = refs[:8], refs[8:10], refs[10 : 10 + NZ]
     cbuf, xs, sems = refs[10 + NZ :]
-    copies = [pltpu.make_async_copy(blocks[k], cbuf.at[k], sems.at[k]) for k in range(8)]
+    copies = [pltpu.make_async_copy(blocks[i], cbuf.at[k], sems.at[i]) for i, k in enumerate(ARRIVAL)]
     for cp in copies:
         cp.start()
     for cp in copies:
@@ -157,20 +154,21 @@
         cp.wait()
 
 
-def a_kernel(place, *refs):
-    ps, xs, (own_ref, s1, s2, s3) = refs[:2], refs[2:10], refs[10:14]
-    acc, pbuf, xbuf, res, spots_v, lists, psem, xsem, lsem = refs[14:]
+def add_products(labels, place, ps, xs, acc, pbuf, xbuf, spots_v, lists, psem, xsem, lsem, fresh):
+    first_label, last_label = labels
+    count = last_label - first_label
     pc, xc = [], []
-    for i in range(NH):
-        k = i % 2 * NZ + i // 2
-        pc.append(pltpu.make_async_copy(ps[i % 2].at[i // 2], pbuf.at[i], psem.at[i]))
-        xc.append(pltpu.make_async_copy(xs[k].at[i % 2], xbuf.at[i], xsem.at[i]))
+    for i in range(count):
+        k, side = (first_label + i) // 2, (first_label + i) % 2
+        pc.append(pltpu.make_async_copy(ps[side].at[k], pbuf.at[i], psem.at[i]))
+        xc.append(pltpu.make_async_copy(xs[i].at[side], xbuf.at[i], xsem.at[i]))
     for cp in pc + xc:
         cp.start()
-    acc[...] = jnp.zeros_like(acc)
+    if fresh:
+        acc[...] = jnp.zeros_like(acc)
     for cp in pc:
         cp.wait()
-    for i in range(NH):
+    for i in range(count):
         tile = pbuf[i, ROWS:, : G * RT].astype(F32)[0:1].astype(jnp.int32)
         to_y = ((tile >> 3) - place[0]) & (NY - 1)
         spots_v[i : i + 1] = (to_y * (G * NH) + (tile >> 5) * NH + (tile & 7)) * U
@@ -182,7 +180,7 @@
     rows = lax.broadcasted_iota(jnp.int32, (ROWS, 128), 0)
     blank = jnp.zeros((64, 256), F32)
 
-    @pl.loop(0, NH)
+    @pl.loop(0, count)
     def _(label):
         x = jnp.concatenate(unpack(xbuf[label].astype(F32)), axis=0)
         for pair in range(4):
@@ -191,41 +189,90 @@
                 keep = (rows >= g * U) & (rows < (g + 1) * U)
                 sides.append(jnp.where(keep, x, 0.0))
             diag = jnp.concatenate(sides, axis=1)
-            even = jnp.concatenate([diag, blank], axis=0).astype(BF)
-            odd = jnp.concatenate([blank, diag], axis=0).astype(BF)
-            for q in range(4):
-                first = q * ROWS - q % 2 * 64
-                res[pair % 2, q * ROWS : (q + 1) * ROWS] = jnp.dot(
-                    pbuf[label, :ROWS, first : first + 256],
-                    odd if q % 2 else even,
+            for odd in range(2):
+                order = [blank, diag] if odd else [diag, blank]
+                windows = []
+                for q in (odd, odd + 2):
+                    first = q * ROWS - odd * 64
+                    windows.append(pbuf[label, :ROWS, first : first + 256])
+                terms = jnp.dot(
+                    jnp.concatenate(windows, axis=0),
+                    jnp.concatenate(order, axis=0).astype(BF),
                     preferred_element_type=F32,
                 )
-            for side in range(2):
-                g = 2 * pair + side
-                for batch in range(4):
-                    spots, sums = [], []
-                    for z in range(batch * 8, batch * 8 + 8):
-                        spot = pl.ds(pl.multiple_of(lists[label, g * RT + z], 8), U)
-                        spots.append(spot)
-                        sums.append(
-                            acc[spot, :]
-                            + res[pair % 2, z * U : (z + 1) * U, side * 128 : (side + 1) * 128]
-                        )
-                    for spot, total in zip(spots, sums):
-                        acc[spot, :] = total
-
+                for side in range(2):
+                    g = 2 * pair + side
+                    for half in range(2):
+                        spots, sums = [], []
+                        for z in range(8):
+                            row = lists[label, g * RT + (odd + 2 * half) * 8 + z]
+                            spot = pl.ds(pl.multiple_of(row, 8), U)
+                            spots.append(spot)
+                            at = (half * 8 + z) * U
+                            sums.append(
+                                acc[spot, :] + terms[at : at + U, side * 128 : (side + 1) * 128]
+                            )
+                        for spot, total in zip(spots, sums):
+                            acc[spot, :] = total
+
+
+def finish_products(acc, own_ref, sends):
     size = ROWS * NH
     own_ref[...] = acc[0:size]
     quarter = size // 4
-    for k, ref in enumerate((s1, s2, s3)):
+    for k, ref in enumerate(sends):
         first = (k + 1) * size
         ref[...] = pack(
             [acc[first + i * quarter : first + (i + 1) * quarter] for i in range(4)]
         ).astype(BF)
 
 
-def y_kernel(dests, own, r1, r2, r3, ident, *refs):
-    ds, m_ref, y = refs[:NZ], refs[NZ], refs[NZ + 1]
+def first_kernel(place, *refs):
+    ps, xs, acc, done = refs[:2], refs[2 : 2 + FIRST], refs[2 + FIRST], refs[3 + FIRST]
+    add_products((0, FIRST), place, ps, xs, acc, *refs[4 + FIRST :], fresh=True)
+    done[...] = jnp.zeros_like(done)
+
+
+def last_kernel(place, *refs):
+    more = NH - FIRST
+    ps, xs = refs[:2], refs[2 : 2 + more]
+    acc, own_ref, *sends = refs[4 + more : 9 + more]
+    add_products((FIRST, NH), place, ps, xs, acc, *refs[9 + more :], fresh=False)
+    finish_products(acc, own_ref, sends)
+
+
+def a_kernel(place, *refs):
+    ps, xs, (own_ref, *sends) = refs[:2], refs[2:10], refs[10:14]
+    add_products((0, NH), place, ps, xs, *refs[14:], fresh=True)
+    finish_products(refs[14], own_ref, sends)
+
+
+def product_scratch(count):
+    return [
+        pltpu.VMEM((count, ROWS + 8, COLS), BF),
+        pltpu.VMEM((count, ROWS // 4, 384), BF),
+        pltpu.VMEM((count, G * RT), jnp.int32),
+        pltpu.SMEM((count, G * RT), jnp.int32),
+        pltpu.SemaphoreType.DMA((count,)),
+        pltpu.SemaphoreType.DMA((count,)),
+        pltpu.SemaphoreType.DMA,
+    ]
+
+
+def pair_kernel(stay, came, *refs):
+    outs, sems = refs[:NZ], refs[NZ]
+    copies = []
+    for k in range(NZ):
+        copies.append(pltpu.make_async_copy(stay.at[k], outs[k].at[0], sems.at[2 * k]))
+        copies.append(pltpu.make_async_copy(came.at[k], outs[k].at[1], sems.at[2 * k + 1]))
+    for cp in copies:
+        cp.start()
+    for cp in copies:
+        cp.wait()
+
+
+def y_kernel(dests, r2, own, r1, r3, ident, *refs):
+    ds, m_ref, y = refs[:NC], refs[NC], refs[NC + 1]
     quarter = ROWS * NH // 4
     parts = [unpack(r[...].astype(F32)) for r in (r1, r2, r3)]
     for i in range(4):
@@ -237,7 +284,7 @@
         for g in range(G):
             pieces.append(y[pl.ds(pl.multiple_of((g * NH + h) * U, 8), U), :])
         pairs = [jnp.concatenate(pieces[2 * i : 2 * i + 2], axis=0) for i in range(4)]
-        ds[label // 2][label % 2] = pack(pairs).astype(BF)
+        ds[label % 2][label // 2] = pack(pairs).astype(BF)
     for g in range(G):
         block = y[g * ROWS : (g + 1) * ROWS, :].astype(BF)
         turned = lax.dot_general(
@@ -248,10 +295,10 @@
 
 
 def out_kernel(*refs):
-    ds, (m_ref, perm_ref, gaps, out_ref) = refs[:NH], refs[NH:]
+    ds, (m_ref, perm_ref, gaps, out_ref) = refs[1:NZ] + refs[:1], refs[NZ:]
     total = jnp.zeros((ROWS, COLS), F32)
     for label in range(NH):
-        packed = ds[label % 2 * NZ + label // 2][label % 2].astype(F32)
+        packed = ds[label // 2][label % 2].astype(F32)
         piece = jnp.concatenate(unpack(packed), axis=0).astype(BF)
         total = total + jnp.dot(piece, perm_ref[label], preferred_element_type=F32)
     row = lax.broadcasted_iota(jnp.int32, (ROWS, COLS), 0)
@@ -262,6 +309,10 @@
     out_ref[...] = total / gaps[...]
 
 
+def cost(us):
+    return pl.CostEstimate(flops=int(us * 1.15e9), bytes_accessed=1 << 20, transcendentals=0)
+
+
 def params(mib):
     return pltpu.CompilerParams(vmem_limit_bytes=mib * 1024 * 1024)
 
@@ -279,7 +330,7 @@
     over, left, right = flip_zl(c_own), shift_x(c_own, 1), shift_x(c_own, -1)
     over_right, far, over_left = shift_x(over, -1), shift_x(left, 1), shift_x(over, 1)
     over_far = shift_x(over_right, -1)
-    blocks = [c_own, right, far, left, over, over_right, over_far, over_left]
+    blocks = [pltpu.with_memory_space_constraint(c_own, pltpu.HBM), right, far, left, over, over_right, over_far, over_left]
 
     tiles = pl.pallas_call(
         tiles_kernel,
@@ -290,7 +341,8 @@
         compiler_params=params(12),
         name="arrange_tiles",
     )(jnp.transpose(alpha_values[0, :, 0], (0, 2, 3, 1)), alpha_rows[0, :, 0], turn_rows())
-    a_near = [tiles, cross_z(tiles, 1), send_step(tiles, 2), cross_z(tiles, 2)]
+    a_next = send_step(tiles, 2)
+    a_near = [tiles, cross_z(tiles, 1), a_next, cross_z(a_next, 1)]
 
     col_block = beta_rows[0] // 6
     slots = (((col_block // NX) ^ zl) * NX + (col_block % NX - x) % NX) * 6 + beta_rows[0] % 6
@@ -304,7 +356,7 @@
     x_out = pl.pallas_call(
         x_kernel,
         out_shape=[piece] * NZ,
-        in_specs=[SM, HBM] + [VM] * 9,
+        in_specs=[SM] + [VM] * 7 + [HBM] + [VM] * 2,
         out_specs=[VM] * NZ,
         scratch_shapes=[
             pltpu.VMEM((8, ROWS, COLS), BF),
@@ -313,8 +365,9 @@
         ],
         compiler_params=params(12),
         name="beta_product",
-    )(slots.reshape(-1), pltpu.with_memory_space_constraint(c_own, pltpu.HBM), *blocks[1:], beta_values[0].reshape(6, 768, 128), perm_to)
-    x_parts = exchange(x_out)
+    )(slots.reshape(-1), *[blocks[k] for k in ARRIVAL], beta_values[0].reshape(6, 768, 128), perm_to)
+    direct = [x_out[0]] + [send_step(x_out[k], k) for k in range(1, NZ)]
+    x_parts = direct + [flip_core(a) for a in direct[:3]]
     a_own = pl.pallas_call(
         stack_kernel,
         out_shape=jax.ShapeDtypeStruct((NZ, ROWS + 8, COLS), BF),
@@ -327,46 +380,62 @@
 
     size = ROWS * NH
     part = jax.ShapeDtypeStruct((size // 4, 384), BF)
-    own, s1, s2, s3 = pl.pallas_call(
-        a_kernel,
-        out_shape=[jax.ShapeDtypeStruct((size, 128), F32), part, part, part],
-        in_specs=[SM] + [HBM] * 10,
-        out_specs=[VM] * 4,
-        scratch_shapes=[
-            pltpu.VMEM((size * NY, 128), F32),
-            pltpu.VMEM((NH, ROWS + 8, COLS), BF),
-            pltpu.VMEM((NH, ROWS // 4, 384), BF),
-            pltpu.VMEM((2, RT * U, 256), F32),
-            pltpu.VMEM((NH, G * RT), jnp.int32),
-            pltpu.SMEM((NH, G * RT), jnp.int32),
-            pltpu.SemaphoreType.DMA((NH,)),
-            pltpu.SemaphoreType.DMA((NH,)),
-            pltpu.SemaphoreType.DMA,
-        ],
+    by_label = [x_parts[i % 2 * NZ + i // 2] for i in range(FIRST)]
+    a_pair = (a_own, flip_core(a_own))
+    total = jax.ShapeDtypeStruct((size * NY, 128), F32)
+    acc, done = pl.pallas_call(
+        first_kernel,
+        out_shape=[total, jax.ShapeDtypeStruct((8, 128), F32)],
+        in_specs=[SM] + [HBM] * (2 + FIRST),
+        out_specs=[VM] * 2,
+        scratch_shapes=product_scratch(FIRST),
         compiler_params=params(16),
-        name="alpha_product",
-    )(y.reshape(1), a_own, flip_core(a_own), *x_parts)
+        cost_estimate=cost(6),
+        name="alpha_product_first",
+    )(y.reshape(1), *a_pair, *by_label)
+    farthest, done = lax.optimization_barrier((direct[3], done))
+    _, own, s1, s2, s3 = pl.pallas_call(
+        last_kernel,
+        out_shape=[total, jax.ShapeDtypeStruct((size, 128), F32), part, part, part],
+        in_specs=[SM] + [HBM] * (2 + NH - FIRST) + [VM] * 2,
+        out_specs=[VM] * 5,
+        input_output_aliases={3 + NH - FIRST: 0},
+        scratch_shapes=product_scratch(NH - FIRST),
+        compiler_params=params(16),
+        name="alpha_product_last",
+    )(y.reshape(1), *a_pair, farthest, flip_core(farthest), acc, done)
     r2, r1, r3 = shift_y(s2, 2), shift_y(s1, 1), shift_y(s3, 3)
 
     y_out = pl.pallas_call(
         y_kernel,
-        out_shape=[piece] * NZ + [jax.ShapeDtypeStruct((NY * G, U, ROWS), BF)],
+        out_shape=[jax.ShapeDtypeStruct((NZ, ROWS // 4, 384), BF)] * NC
+        + [jax.ShapeDtypeStruct((NY * G, U, ROWS), BF)],
         in_specs=[SM] + [VM] * 5,
-        out_specs=[VM] * (NZ + 1),
+        out_specs=[VM] * (NC + 1),
         scratch_shapes=[pltpu.VMEM((size, 128), F32)],
         compiler_params=params(12),
         name="y_sum",
-    )(h_to, own, r1, r2, r3, jnp.eye(128, dtype=BF))
-    mirrored = lax.all_to_all(y_out[NZ], ("y", "zl", "x"), split_axis=0, concat_axis=0, tiled=True)
-    d_parts = exchange(y_out[:NZ])
+    )(h_to, r2, own, r1, r3, jnp.eye(128, dtype=BF))
+    came = flip_core(y_out[1])
+    mirrored = lax.all_to_all(y_out[NC], ("y", "zl", "x"), split_axis=0, concat_axis=0, tiled=True)
+    pairs = pl.pallas_call(
+        pair_kernel,
+        out_shape=[piece] * NZ,
+        in_specs=[HBM] * 2,
+        out_specs=[HBM] * NZ,
+        scratch_shapes=[pltpu.SemaphoreType.DMA((2 * NZ,))],
+        compiler_params=params(4),
+        name="pair_pieces",
+    )(y_out[0], came)
+    d_parts = [pairs[0]] + [send_step(pairs[k], k) for k in range(1, NZ)]
     out = pl.pallas_call(
         out_kernel,
         out_shape=jax.ShapeDtypeStruct((ROWS, COLS), F32),
-        in_specs=[VM] * (NH + 3),
+        in_specs=[VM] * (NZ + 3),
         out_specs=VM,
         compiler_params=params(12),
         name="combine",
-    )(*d_parts, mirrored.reshape(NY, ROWS, ROWS), perm_from, gaps.reshape(ROWS, COLS))
+    )(d_parts[3], *d_parts[:3], mirrored.reshape(NY, ROWS, ROWS), perm_from, gaps.reshape(ROWS, COLS))
     return out.reshape(gaps.shape)
 
 

time: 110 us -> 107 us (0.973)
  starting transfers between devices: 59.6 us -> 51.2 us
  waiting for transfers between devices: 29.5 us -> 32.7 us
  Pallas kernels: 16.2 us -> 17.7 us
    ppermute x7, waiting for transfers between devices: 5.12 us -> 15.6 us  [send_step(): return lax.ppermute(a, ('zh', 'zl'), moves)]
    ppermute x2, waiting for transfers between devices: 5.76 us -> 0.01 us  [cross_z(): return lax.ppermute(a, ('zh', 'zl'), moves)]
    ppermute x9 -> x6, starting transfers between devices: 12.2 us -> 6.78 us  [flip_core(): return lax.ppermute(a, 'core', [(0, 1), (1, 0)])]
    ppermute x6, starting transfers between devices: 8.91 us -> 5.62 us  [shift_x(): return lax.ppermute(a, 'x', [(i, (i + k) % NX) for i in range(NX)])]
    all_to_all x1, starting transfers between devices: 9.43 us -> 7.76 us  [per_device(): lax.all_to_all(y_out[NC], ('y', 'zl', 'x'), split_axis=0, concat_axis=0,...]
    pallas_call x3 -> x5, Pallas kernels: 13.2 us -> 14.7 us  [the longest x1 6.24 us: per_device(): pl.pallas_call(first_kernel, out_shape=[total, jax.ShapeDtypeStruct((8, 1...]
    ppermute x7, starting transfers between devices: 14.2 us -> 15.4 us  [send_step(): return lax.ppermute(a, ('zh', 'zl'), moves)]
    ppermute x6, waiting for transfers between devices: 5.14 us -> 3.98 us  [shift_x(): return lax.ppermute(a, 'x', [(i, (i + k) % NX) for i in range(NX)])]
  transfers between devices with their start and end apart: 29 -> 26, of which waited for: 10 -> 11; matrix products, arithmetic and copies ran while one was open for 1% -> 1% of each run, Pallas kernels for 3% -> 10%
where the time goes in v3:
time: 107 us; the launch traced here: 106 us
  starting transfers between devices  51.2 us (48%)
  waiting for transfers between devices  32.7 us (31%)
  Pallas kernels  17.7 us (17%)
  local copies, waits for them, and re-layouts  3.49 us (3%)
  other arithmetic  1.1 us (1%)
    ppermute x7, waiting for transfers between devices, send_step(): return lax.ppermute(a, ('zh', 'zl'), moves)  15.6 us
    ppermute x7, starting transfers between devices, send_step(): return lax.ppermute(a, ('zh', 'zl'), moves)  15.4 us
    ppermute x3, waiting for transfers between devices, shift_y(): return lax.ppermute(a, 'y', [(i, (i + k) % NY) for i in range(NY)])  11.1 us
    all_to_all x1, starting transfers between devices, per_device(): lax.all_to_all(y_out[NC], ('y', 'zl', 'x'), split_axis=0, concat_axis=0,...  7.76 us
    ppermute x2, starting transfers between devices, cross_z(): return lax.ppermute(a, ('zh', 'zl'), moves)  7.41 us
    ppermute x6, starting transfers between devices, flip_core(): return lax.ppermute(a, 'core', [(0, 1), (1, 0)])  6.78 us
    pallas_call x1, Pallas kernels, per_device(): pl.pallas_call(first_kernel, out_shape=[total, jax.ShapeDtypeStruct((8, 1...  6.24 us
    ppermute x3, starting transfers between devices, shift_y(): return lax.ppermute(a, 'y', [(i, (i + k) % NY) for i in range(NY)])  5.69 us
  transfers between devices with their start and end apart: 26, of which 11 were waited for; matrix products, arithmetic and copies ran while one was open for 1% of the time, Pallas kernels for 10%

profile of v3, /device:TPU:1, one launch (start us, length us, event | category | flops | bytes accessed | tf_op | source)
XLA Modules:
  0.0 106.5 jit_solution(3971673034801298383)
XLA Ops:
  0.0 2.6 %collective-permute-start = (bf16[192,768]{1,0:T(8,128)(2,1)}, bf16[192,768]{1,0:T(8,128)(2,1)S(1)}, u32[]{:S(2)}, u32[]{:S(2)}) collective-permute-start(bf16[192,768]{1,0:T(8,128)(2,1)} %bitcast.17), channel_id=1, source_target_pairs={{0,4},{4,0},{1,5},{5,1},{2,6},{6,2},{3,7},{7,3},{8,12},{12,8},{9,1... | collective-permute-start | bytes 884744 | tf_op jit(solution)/shard_map/ppermute | solution.py:30
  2.6 1.2 %collective-permute-start.4 = (bf16[192,768]{1,0:T(8,128)(2,1)}, bf16[192,768]{1,0:T(8,128)(2,1)S(1)}, u32[]{:S(2)}, u32[]{:S(2)}) collective-permute-start(bf16[192,768]{1,0:T(8,128)(2,1)} %bitcast.18), channel_id=1, source_target_pairs={{0,1},{1,2},{2,3},{3,0},{4,5},{5,6},{6,7},{7,4},{8,9},{9,10},{10,1... | collective-permute-start | bytes 884744 | tf_op jit(solution)/shard_map/ppermute | solution.py:26
  3.8 1.5 %collective-permute-start.6 = (bf16[192,768]{1,0:T(8,128)(2,1)}, bf16[192,768]{1,0:T(8,128)(2,1)S(1)}, u32[]{:S(2)}, u32[]{:S(2)}) collective-permute-start(bf16[192,768]{1,0:T(8,128)(2,1)} %bitcast.19), channel_id=1, source_target_pairs={{0,3},{1,0},{2,1},{3,2},{4,7},{5,4},{6,5},{7,6},{8,11},{9,8},{10,9... | collective-permute-start | bytes 884744 | tf_op jit(solution)/shard_map/ppermute | solution.py:26
  5.2 1.3 %copy-done = bf16[1,8,1,32,24,24]{3,5,4,2,1,0:T(8,128)(2,1)S(1)} copy-done((bf16[1,8,1,32,24,24]{3,5,4,2,1,0:T(8,128)(2,1)S(1)}, bf16[1,8,1,32,24,24]{3,5,4,2,1,0:T(8,128)(2,1)}, u32[]{:S(2)}) %copy-start) | copy-done | bytes 294936
  6.5 1.3 %copy-done.2 = bf16[768,768]{1,0:T(8,128)(2,1)S(1)} copy-done((bf16[768,768]{1,0:T(8,128)(2,1)S(1)}, bf16[768,768]{1,0:T(8,128)(2,1)}, u32[]{:S(2)}) %copy-start.2) | copy-done | bytes 1179672
  7.8 0.7 copy-done.4
  8.5 0.7 arrange_tiles.1.refs_0_
  9.2 4.7 %collective-permute-start.7 = (bf16[200,768]{1,0:T(8,128)(2,1)S(1)}, bf16[200,768]{1,0:T(8,128)(2,1)S(1)}, u32[]{:S(2)}, u32[]{:S(2)}) collective-permute-start(bf16[200,768]{1,0:T(8,128)(2,1)S(1)} %arrange_tiles.1.refs_0_), channel_id=1, source_target_pairs={{0,52},{4,16},{16,4},{20,32},{32,20},{36,48},{48,36},{52,0},{1,53}... | collective-permute-start | bytes 921608 | tf_op jit(solution)/shard_map/ppermute | solution.py:46
  14.0 1.2 %collective-permute-start.8 = (bf16[200,768]{1,0:T(8,128)(2,1)S(1)}, bf16[200,768]{1,0:T(8,128)(2,1)S(1)}, u32[]{:S(2)}, u32[]{:S(2)}) collective-permute-start(bf16[200,768]{1,0:T(8,128)(2,1)S(1)} %arrange_tiles.1.refs_0_), channel_id=1, source_target_pairs={{0,48},{4,20},{16,0},{20,36},{32,16},{36,52},{48,32},{52,4},{1,49}... | collective-permute-start | bytes 921608 | tf_op jit(solution)/shard_map/ppermute | solution.py:55
  15.2 0.1 rem.118
  15.3 0.1 div.33
  15.4 0.1 ne.108
  15.5 0.0 collective-permute-done.refs_0_
  15.5 1.3 %collective-permute-start.1 = (bf16[192,768]{1,0:T(8,128)(2,1)S(1)}, bf16[192,768]{1,0:T(8,128)(2,1)S(1)}, u32[]{:S(2)}, u32[]{:S(2)}) collective-permute-start(bf16[192,768]{1,0:T(8,128)(2,1)S(1)} %collective-permute-done.refs_0_), channel_id=1, source_target_pairs={{0,3},{1,0},{2,1},{3,2},{4,7},{5,4},{6,5},{7,6},{8,11},{9,8},{10,9... | collective-permute-start | bytes 884744 | tf_op jit(solution)/shard_map/ppermute | solution.py:26
  16.9 0.1 broadcast_add_fusion
  16.9 0.0 collective-permute-done.4.refs_4_
  16.9 0.2 collective-permute-start.3
  17.2 0.0 collective-permute-done.6.refs_6_
  17.2 0.1 collective-permute-start.5
  17.3 8.3 %collective-permute-done.8.refs_2_ = bf16[200,768]{1,0:T(8,128)(2,1)S(1)} collective-permute-done((bf16[200,768]{1,0:T(8,128)(2,1)S(1)}, bf16[200,768]{1,0:T(8,128)(2,1)S(1)}, u32[]{:S(2)}, u32[]{:S(2)}) %collective-permute-start.8) | collective-permute-done | bytes 307232 | tf_op jit(solution)/shard_map/ppermute | solution.py:55
  25.6 2.7 %collective-permute-start.9 = (bf16[200,768]{1,0:T(8,128)(2,1)S(1)}, bf16[200,768]{1,0:T(8,128)(2,1)S(1)}, u32[]{:S(2)}, u32[]{:S(2)}) collective-permute-start(bf16[200,768]{1,0:T(8,128)(2,1)S(1)} %collective-permute-done.8.refs_2_), channel_id=1, source_target_pairs={{0,52},{4,16},{16,4},{20,32},{32,20},{36,48},{48,36},{52,0},{1,53}... | collective-permute-start | bytes 921608 | tf_op jit(solution)/shard_map/ppermute | solution.py:46
  28.3 0.0 collective-permute-done.1.refs_2_
  28.3 1.3 %collective-permute-start.2 = (bf16[192,768]{1,0:T(8,128)(2,1)S(1)}, bf16[192,768]{1,0:T(8,128)(2,1)S(1)}, u32[]{:S(2)}, u32[]{:S(2)}) collective-permute-start(bf16[192,768]{1,0:T(8,128)(2,1)S(1)} %collective-permute-done.1.refs_2_), channel_id=1, source_target_pairs={{0,3},{1,0},{2,1},{3,2},{4,7},{5,4},{6,5},{7,6},{8,11},{9,8},{10,9... | collective-permute-start | bytes 884744 | tf_op jit(solution)/shard_map/ppermute | solution.py:26
  29.6 0.6 fusion.refs_9_
  30.2 0.0 collective-permute-done.3.refs_3_
  30.2 0.5 collective-permute-done.5.refs_5_
  30.6 3.5 %collective-permute-done.2.refs_1_ = bf16[192,768]{1,0:T(8,128)(2,1)S(1)} collective-permute-done((bf16[192,768]{1,0:T(8,128)(2,1)S(1)}, bf16[192,768]{1,0:T(8,128)(2,1)S(1)}, u32[]{:S(2)}, u32[]{:S(2)}) %collective-permute-start.2) | collective-permute-done | bytes 294944 | tf_op jit(solution)/shard_map/ppermute | solution.py:26
  34.1 3.4 %beta_product.1 = (bf16[2,48,384]{2,1,0:T(8,128)(2,1)S(1)}, bf16[2,48,384]{2,1,0:T(8,128)(2,1)S(1)}, bf16[2,48,384]{2,1,0:T(8,128)(2,1)S(1)}, bf16[2,48,384]{2,1,0:T(8,128)(2,1)S(1)}) custom-call(s32[36]{0:T(128)S(1)} %fusion.5.slots, bf16[192,768]{1,0:T(8,128)(2,1)S(1)} %collective-permute-done.refs_0_, ...), custom_call_target="tpu_custom_call" | custom-call | tf_op jit(solution)/shard_map/beta_product/pallas_call | solution.py:356
  37.5 0.0 collective-permute-done.7.refs_1_
  37.5 0.0 collective-permute-done.9.refs_3_
  37.6 0.3 stack_tiles.1.refs_0_
  37.9 3.7 %collective-permute-start.10 = (bf16[4,200,768]{2,1,0:T(8,128)(2,1)S(1)}, bf16[4,200,768]{2,1,0:T(8,128)(2,1)S(1)}, u32[]{:S(2)}, u32[]{:S(2)}) collective-permute-start(bf16[4,200,768]{2,1,0:T(8,128)(2,1)S(1)} %stack_tiles.1.refs_0_), channel_id=1, source_target_pairs={{0,8},{8,0},{1,9},{9,1},{2,10},{10,2},{3,11},{11,3},{4,12},{12,4},... | collective-permute-start | bytes 3686408 | tf_op jit(solution)/shard_map/ppermute | solution.py:34
  41.6 0.7 collective-permute-start.13
  42.3 2.9 %collective-permute-start.15 = (bf16[2,48,384]{2,1,0:T(8,128)(2,1)S(1)}, bf16[2,48,384]{2,1,0:T(8,128)(2,1)S(1)}, u32[]{:S(2)}, u32[]{:S(2)}) collective-permute-start(bf16[2,48,384]{2,1,0:T(8,128)(2,1)S(1)} %get-tuple-element.27), channel_id=1, source_target_pairs={{0,48},{4,20},{16,0},{20,36},{32,16},{36,52},{48,32},{52,4},{1,49}... | collective-permute-start | bytes 221192 | tf_op jit(solution)/shard_map/ppermute | solution.py:55
  45.2 0.6 collective-permute-start.12
  45.8 1.7 %collective-permute-done.13.refs_4_ = bf16[2,48,384]{2,1,0:T(8,128)(2,1)S(1)} collective-permute-done((bf16[2,48,384]{2,1,0:T(8,128)(2,1)S(1)}, bf16[2,48,384]{2,1,0:T(8,128)(2,1)S(1)}, u32[]{:S(2)}, u32[]{:S(2)}) %collective-permute-start.13) | collective-permute-done | bytes 73760 | tf_op jit(solution)/shard_map/ppermute | solution.py:55
  47.5 1.0 collective-permute-start.14
  48.5 0.2 collective-permute-start.16
  48.7 3.8 %collective-permute-start.11 = (bf16[2,48,384]{2,1,0:T(8,128)(2,1)S(1)}, bf16[2,48,384]{2,1,0:T(8,128)(2,1)S(1)}, u32[]{:S(2)}, u32[]{:S(2)}) collective-permute-start(bf16[2,48,384]{2,1,0:T(8,128)(2,1)S(1)} %get-tuple-element.25), channel_id=1, source_target_pairs={{0,32},{4,36},{16,48},{20,52},{32,0},{36,4},{48,16},{52,20},{1,33}... | collective-permute-start | bytes 221192 | tf_op jit(solution)/shard_map/ppermute | solution.py:55
  52.5 0.0 collective-permute-done.16.refs_7_
  52.5 0.0 collective-permute-done.10.refs_1_
  52.5 6.2 %alpha_product_first.1 = (f32[6144,128]{1,0:T(8,128)S(1)}, f32[8,128]{1,0:T(8,128)S(1)}) custom-call(s32[1]{0:T(128)} %bitcast.place, bf16[4,200,768]{2,1,0:T(8,128)(2,1)S(1)} %stack_tiles.1.refs_0_, bf16[4,200,768]{2,1,0:T(8,128)(2,1)S(1)} %collective-permute-done.10.refs_1_, bf16[2,48,384]{2,1,0:T(8,128)(2,1)S(1)} %get-tuple-element.24.after.refs_2_, ...), custom_call_target="tpu_custom_call" | custom-call | flops 6899999744 | bytes 1048576 | tf_op jit(solution)/shard_map/alpha_product_first/pallas_call | solution.py:386
  58.8 0.4 collective-permute-start.17
  59.2 0.9 collective-permute-done.17.refs_3_
  60.1 2.7 %alpha_product_last.1 = (f32[6144,128]{1,0:T(8,128)S(1)}, f32[1536,128]{1,0:T(8,128)S(1)}, bf16[384,384]{1,0:T(8,128)(2,1)S(1)}, bf16[384,384]{1,0:T(8,128)(2,1)S(1)}, bf16[384,384]{1,0:T(8,128)(2,1)S(1)}) custom-call(s32[1]{0:T(128)} %bitcast.place, bf16[4,200,768]{2,1,0:T(8,128)(2,1)S(1)} %stack_tiles.1.refs_0_, ...), custom_call_target="tpu_custom_call", output_to_operand_aliasing={{0}: (5, {})} | custom-call | tf_op jit(solution)/shard_map/alpha_product_last/pallas_call | solution.py:397
  62.9 3.0 %collective-permute-start.18 = (bf16[384,384]{1,0:T(8,128)(2,1)S(1)}, bf16[384,384]{1,0:T(8,128)(2,1)S(1)}, u32[]{:S(2)}, u32[]{:S(2)}) collective-permute-start(bf16[384,384]{1,0:T(8,128)(2,1)S(1)} %get-tuple-element.32), channel_id=1, source_target_pairs={{0,128},{64,192},{128,0},{192,64},{1,129},{65,193},{129,1},{193,65... | collective-permute-start | bytes 884744 | tf_op jit(solution)/shard_map/ppermute | solution.py:38
  65.9 0.4 collective-permute-start.19
  66.3 2.3 %collective-permute-start.20 = (bf16[384,384]{1,0:T(8,128)(2,1)S(1)}, bf16[384,384]{1,0:T(8,128)(2,1)S(1)}, u32[]{:S(2)}, u32[]{:S(2)}) collective-permute-start(bf16[384,384]{1,0:T(8,128)(2,1)S(1)} %get-tuple-element.35), channel_id=1, source_target_pairs={{0,192},{64,0},{128,64},{192,128},{1,193},{65,1},{129,65},{193,129... | collective-permute-start | bytes 884744 | tf_op jit(solution)/shard_map/ppermute | solution.py:38
  68.6 4.2 %collective-permute-done.18.r2 = bf16[384,384]{1,0:T(8,128)(2,1)S(1)} collective-permute-done((bf16[384,384]{1,0:T(8,128)(2,1)S(1)}, bf16[384,384]{1,0:T(8,128)(2,1)S(1)}, u32[]{:S(2)}, u32[]{:S(2)}) %collective-permute-start.18) | collective-permute-done | bytes 294944 | tf_op jit(solution)/shard_map/ppermute | solution.py:38
  72.8 6.9 %collective-permute-done.19.r1 = bf16[384,384]{1,0:T(8,128)(2,1)S(1)} collective-permute-done((bf16[384,384]{1,0:T(8,128)(2,1)S(1)}, bf16[384,384]{1,0:T(8,128)(2,1)S(1)}, u32[]{:S(2)}, u32[]{:S(2)}) %collective-permute-start.19) | collective-permute-done | bytes 294944 | tf_op jit(solution)/shard_map/ppermute | solution.py:38
  79.7 1.9 %y_sum.1 = (bf16[4,48,384]{2,1,0:T(8,128)(2,1)S(1)}, bf16[4,48,384]{2,1,0:T(8,128)(2,1)S(1)}, bf16[32,24,192]{2,1,0:T(8,128)(2,1)}) custom-call(s32[8]{0:T(128)S(1)} %get-tuple-element.46.dests, bf16[384,384]{1,0:T(8,128)(2,1)S(1)} %collective-permute-done.18.r2, f32[1536,128]{1,0:T(8,128)S(1)} %get-tuple-element.33.own, ...), custom_call_target="tpu_custom_call" | custom-call | tf_op jit(solution)/shard_map/y_sum/pallas_call | solution.py:409
  81.6 7.8 %all-to-all-start = ((bf16[32,24,192]{2,1,0:T(8,128)(2,1)}), bf16[32,24,192]{2,1,0:T(8,128)(2,1)S(1)}, u32[]{:S(2)}, u32[]{:S(2)}) async-start(bf16[32,24,192]{2,1,0:T(8,128)(2,1)} %get-tuple-element.42), calls=%async_computation | async-start | bytes 786432 | tf_op jit(solution)/shard_map/all_to_all | solution.py:420
  89.4 0.9 collective-permute-start.21
  90.3 1.0 collective-permute-done.21.came
  91.3 0.4 pair_pieces.1
  91.7 3.3 %collective-permute-start.22 = (bf16[2,48,384]{2,1,0:T(8,128)(2,1)S(1)}, bf16[2,48,384]{2,1,0:T(8,128)(2,1)S(1)}, u32[]{:S(2)}, u32[]{:S(2)}) collective-permute-start(bf16[2,48,384]{2,1,0:T(8,128)(2,1)S(1)} %get-tuple-element.38), channel_id=1, source_target_pairs={{0,32},{4,36},{16,48},{20,52},{32,0},{36,4},{48,16},{52,20},{1,33}... | collective-permute-start | bytes 221192 | tf_op jit(solution)/shard_map/ppermute | solution.py:55
  95.0 0.7 collective-permute-start.23
  95.8 2.8 %collective-permute-start.24 = (bf16[2,48,384]{2,1,0:T(8,128)(2,1)S(1)}, bf16[2,48,384]{2,1,0:T(8,128)(2,1)S(1)}, u32[]{:S(2)}, u32[]{:S(2)}) collective-permute-start(bf16[2,48,384]{2,1,0:T(8,128)(2,1)S(1)} %get-tuple-element.41), channel_id=1, source_target_pairs={{0,48},{4,20},{16,0},{20,36},{32,16},{36,52},{48,32},{52,4},{1,49}... | collective-permute-start | bytes 221192 | tf_op jit(solution)/shard_map/ppermute | solution.py:55
  98.6 0.3 fusion.1.refs_5_
  98.9 0.3 collective-permute-done.22.refs_0_
  99.2 1.6 %collective-permute-done.23.refs_2_ = bf16[2,48,384]{2,1,0:T(8,128)(2,1)S(1)} collective-permute-done((bf16[2,48,384]{2,1,0:T(8,128)(2,1)S(1)}, bf16[2,48,384]{2,1,0:T(8,128)(2,1)S(1)}, u32[]{:S(2)}, u32[]{:S(2)}) %collective-permute-start.23) | collective-permute-done | bytes 73760 | tf_op jit(solution)/shard_map/ppermute | solution.py:55
  100.8 3.7 %collective-permute-done.24.refs_3_ = bf16[2,48,384]{2,1,0:T(8,128)(2,1)S(1)} collective-permute-done((bf16[2,48,384]{2,1,0:T(8,128)(2,1)S(1)}, bf16[2,48,384]{2,1,0:T(8,128)(2,1)S(1)}, u32[]{:S(2)}, u32[]{:S(2)}) %collective-permute-start.24) | collective-permute-done | bytes 73760 | tf_op jit(solution)/shard_map/ppermute | solution.py:55
  104.5 0.0 all-to-all-done
  104.5 1.9 %combine.1 = f32[192,768]{1,0:T(8,128)} custom-call(bf16[2,48,384]{2,1,0:T(8,128)(2,1)S(1)} %collective-permute-done.22.refs_0_, bf16[2,48,384]{2,1,0:T(8,128)(2,1)S(1)} %get-tuple-element.39.refs_1_, bf16[2,48,384]{2,1,0:T(8,128)(2,1)S(1)} %collective-permute-done.23.refs_2_, bf16[2,48,384]{2,1,0:T(8,128)(2,1)S(1)} %collective-permute-done.24.refs_3_, ...), custom_call_target="tpu_custom_call" | custom-call | tf_op jit(solution)/shard_map/combine/pallas_call | solution.py:431
  (24 shorter events, 0.2 us)
Async XLA Ops:
  0.0 15.5 %copy-start.6 = (s32[8]{0:T(128)S(1)}, s32[8]{0:T(128)}, u32[]{:S(2)}) copy-start(s32[8]{0:T(128)} %constant.114.clone) | copy-start | bytes 100
  0.0 15.5 %copy-start.7 = (s32[8]{0:T(128)S(1)}, s32[8]{0:T(128)}, u32[]{:S(2)}) copy-start(s32[8]{0:T(128)} %constant.113.clone) | copy-start | bytes 100
  0.0 15.2 %copy-start.5 = (s32[1,6,6]{2,0,1:T(1,128)S(1)}, s32[1,6,6]{2,0,1:T(1,128)}, u32[]{:S(2)}) copy-start(s32[1,6,6]{2,0,1:T(1,128)} %param.11) | copy-start | bytes 436
  0.0 15.5 %collective-permute-start = (bf16[192,768]{1,0:T(8,128)(2,1)}, bf16[192,768]{1,0:T(8,128)(2,1)S(1)}, u32[]{:S(2)}, u32[]{:S(2)}) collective-permute-start(bf16[192,768]{1,0:T(8,128)(2,1)} %bitcast.17), channel_id=1, source_target_pairs={{0,4},{4,0},{1,5},{5,1},{2,6},{6,2},{3,7},{7,3},{8,12},{12,8},{9,1... | collective-permute-start | bytes 884744 | tf_op jit(solution)/shard_map/ppermute | solution.py:30
  2.6 14.4 %collective-permute-start.4 = (bf16[192,768]{1,0:T(8,128)(2,1)}, bf16[192,768]{1,0:T(8,128)(2,1)S(1)}, u32[]{:S(2)}, u32[]{:S(2)}) collective-permute-start(bf16[192,768]{1,0:T(8,128)(2,1)} %bitcast.18), channel_id=1, source_target_pairs={{0,1},{1,2},{2,3},{3,0},{4,5},{5,6},{6,7},{7,4},{8,9},{9,10},{10,1... | collective-permute-start | bytes 884744 | tf_op jit(solution)/shard_map/ppermute | solution.py:26
  3.8 13.4 %collective-permute-start.6 = (bf16[192,768]{1,0:T(8,128)(2,1)}, bf16[192,768]{1,0:T(8,128)(2,1)S(1)}, u32[]{:S(2)}, u32[]{:S(2)}) collective-permute-start(bf16[192,768]{1,0:T(8,128)(2,1)} %bitcast.19), channel_id=1, source_target_pairs={{0,3},{1,0},{2,1},{3,2},{4,7},{5,4},{6,5},{7,6},{8,11},{9,8},{10,9... | collective-permute-start | bytes 884744 | tf_op jit(solution)/shard_map/ppermute | solution.py:26
  5.2 1.3 %copy-start = (bf16[1,8,1,32,24,24]{3,5,4,2,1,0:T(8,128)(2,1)S(1)}, bf16[1,8,1,32,24,24]{3,5,4,2,1,0:T(8,128)(2,1)}, u32[]{:S(2)}) copy-start(bf16[1,8,1,32,24,24]{3,5,4,2,1,0:T(8,128)(2,1)} %param.12) | copy-start | bytes 884740
  6.5 1.3 %copy-start.2 = (bf16[768,768]{1,0:T(8,128)(2,1)S(1)}, bf16[768,768]{1,0:T(8,128)(2,1)}, u32[]{:S(2)}) copy-start(bf16[768,768]{1,0:T(8,128)(2,1)} %constant.115.clone.turn) | copy-start | bytes 3538948
  7.8 0.7 copy-start.4
  8.5 25.7 %copy-start.1 = (bf16[1,6,6,128,128]{4,3,2,1,0:T(8,128)(2,1)S(1)}, bf16[1,6,6,128,128]{4,3,2,1,0:T(8,128)(2,1)}, u32[]{:S(2)}) copy-start(bf16[1,6,6,128,128]{4,3,2,1,0:T(8,128)(2,1)} %param.10) | copy-start | bytes 3538948
  9.2 28.3 %collective-permute-start.7 = (bf16[200,768]{1,0:T(8,128)(2,1)S(1)}, bf16[200,768]{1,0:T(8,128)(2,1)S(1)}, u32[]{:S(2)}, u32[]{:S(2)}) collective-permute-start(bf16[200,768]{1,0:T(8,128)(2,1)S(1)} %arrange_tiles.1.refs_0_), channel_id=1, source_target_pairs={{0,52},{4,16},{16,4},{20,32},{32,20},{36,48},{48,36},{52,0},{1,53}... | collective-permute-start | bytes 921608 | tf_op jit(solution)/shard_map/ppermute | solution.py:46
  14.0 11.6 %collective-permute-start.8 = (bf16[200,768]{1,0:T(8,128)(2,1)S(1)}, bf16[200,768]{1,0:T(8,128)(2,1)S(1)}, u32[]{:S(2)}, u32[]{:S(2)}) collective-permute-start(bf16[200,768]{1,0:T(8,128)(2,1)S(1)} %arrange_tiles.1.refs_0_), channel_id=1, source_target_pairs={{0,48},{4,20},{16,0},{20,36},{32,16},{36,52},{48,32},{52,4},{1,49}... | collective-permute-start | bytes 921608 | tf_op jit(solution)/shard_map/ppermute | solution.py:55
  15.5 12.8 %collective-permute-start.1 = (bf16[192,768]{1,0:T(8,128)(2,1)S(1)}, bf16[192,768]{1,0:T(8,128)(2,1)S(1)}, u32[]{:S(2)}, u32[]{:S(2)}) collective-permute-start(bf16[192,768]{1,0:T(8,128)(2,1)S(1)} %collective-permute-done.refs_0_), channel_id=1, source_target_pairs={{0,3},{1,0},{2,1},{3,2},{4,7},{5,4},{6,5},{7,6},{8,11},{9,8},{10,9... | collective-permute-start | bytes 884744 | tf_op jit(solution)/shard_map/ppermute | solution.py:26
  16.9 13.2 %collective-permute-start.3 = (bf16[192,768]{1,0:T(8,128)(2,1)S(1)}, bf16[192,768]{1,0:T(8,128)(2,1)S(1)}, u32[]{:S(2)}, u32[]{:S(2)}) collective-permute-start(bf16[192,768]{1,0:T(8,128)(2,1)S(1)} %collective-permute-done.refs_0_), channel_id=1, source_target_pairs={{0,1},{1,2},{2,3},{3,0},{4,5},{5,6},{6,7},{7,4},{8,9},{9,10},{10,1... | collective-permute-start | bytes 884744 | tf_op jit(solution)/shard_map/ppermute | solution.py:26
  17.2 13.5 %collective-permute-start.5 = (bf16[192,768]{1,0:T(8,128)(2,1)S(1)}, bf16[192,768]{1,0:T(8,128)(2,1)S(1)}, u32[]{:S(2)}, u32[]{:S(2)}) collective-permute-start(bf16[192,768]{1,0:T(8,128)(2,1)S(1)} %collective-permute-done.4.refs_4_), channel_id=1, source_target_pairs={{0,1},{1,2},{2,3},{3,0},{4,5},{5,6},{6,7},{7,4},{8,9},{9,10},{10,1... | collective-permute-start | bytes 884744 | tf_op jit(solution)/shard_map/ppermute | solution.py:26
  25.6 11.9 %collective-permute-start.9 = (bf16[200,768]{1,0:T(8,128)(2,1)S(1)}, bf16[200,768]{1,0:T(8,128)(2,1)S(1)}, u32[]{:S(2)}, u32[]{:S(2)}) collective-permute-start(bf16[200,768]{1,0:T(8,128)(2,1)S(1)} %collective-permute-done.8.refs_2_), channel_id=1, source_target_pairs={{0,52},{4,16},{16,4},{20,32},{32,20},{36,48},{48,36},{52,0},{1,53}... | collective-permute-start | bytes 921608 | tf_op jit(solution)/shard_map/ppermute | solution.py:46
  28.3 5.9 %collective-permute-start.2 = (bf16[192,768]{1,0:T(8,128)(2,1)S(1)}, bf16[192,768]{1,0:T(8,128)(2,1)S(1)}, u32[]{:S(2)}, u32[]{:S(2)}) collective-permute-start(bf16[192,768]{1,0:T(8,128)(2,1)S(1)} %collective-permute-done.1.refs_2_), channel_id=1, source_target_pairs={{0,3},{1,0},{2,1},{3,2},{4,7},{5,4},{6,5},{7,6},{8,11},{9,8},{10,9... | collective-permute-start | bytes 884744 | tf_op jit(solution)/shard_map/ppermute | solution.py:26
  37.9 14.6 %collective-permute-start.10 = (bf16[4,200,768]{2,1,0:T(8,128)(2,1)S(1)}, bf16[4,200,768]{2,1,0:T(8,128)(2,1)S(1)}, u32[]{:S(2)}, u32[]{:S(2)}) collective-permute-start(bf16[4,200,768]{2,1,0:T(8,128)(2,1)S(1)} %stack_tiles.1.refs_0_), channel_id=1, source_target_pairs={{0,8},{8,0},{1,9},{9,1},{2,10},{10,2},{3,11},{11,3},{4,12},{12,4},... | collective-permute-start | bytes 3686408 | tf_op jit(solution)/shard_map/ppermute | solution.py:34
  41.6 5.9 %collective-permute-start.13 = (bf16[2,48,384]{2,1,0:T(8,128)(2,1)S(1)}, bf16[2,48,384]{2,1,0:T(8,128)(2,1)S(1)}, u32[]{:S(2)}, u32[]{:S(2)}) collective-permute-start(bf16[2,48,384]{2,1,0:T(8,128)(2,1)S(1)} %get-tuple-element.26), channel_id=1, source_target_pairs={{0,16},{4,52},{16,32},{20,4},{32,48},{36,20},{48,0},{52,36},{1,17}... | collective-permute-start | bytes 221192 | tf_op jit(solution)/shard_map/ppermute | solution.py:55
  42.3 6.2 %collective-permute-start.15 = (bf16[2,48,384]{2,1,0:T(8,128)(2,1)S(1)}, bf16[2,48,384]{2,1,0:T(8,128)(2,1)S(1)}, u32[]{:S(2)}, u32[]{:S(2)}) collective-permute-start(bf16[2,48,384]{2,1,0:T(8,128)(2,1)S(1)} %get-tuple-element.27), channel_id=1, source_target_pairs={{0,48},{4,20},{16,0},{20,36},{32,16},{36,52},{48,32},{52,4},{1,49}... | collective-permute-start | bytes 221192 | tf_op jit(solution)/shard_map/ppermute | solution.py:55
  45.2 7.3 %collective-permute-start.12 = (bf16[2,48,384]{2,1,0:T(8,128)(2,1)S(1)}, bf16[2,48,384]{2,1,0:T(8,128)(2,1)S(1)}, u32[]{:S(2)}, u32[]{:S(2)}) collective-permute-start(bf16[2,48,384]{2,1,0:T(8,128)(2,1)S(1)} %get-tuple-element.24.after.refs_2_), channel_id=1, source_target_pairs={{0,8},{8,0},{1,9},{9,1},{2,10},{10,2},{3,11},{11,3},{4,12},{12,4},... | collective-permute-start | bytes 221192 | tf_op jit(solution)/shard_map/ppermute | solution.py:34
  47.5 5.0 %collective-permute-start.14 = (bf16[2,48,384]{2,1,0:T(8,128)(2,1)S(1)}, bf16[2,48,384]{2,1,0:T(8,128)(2,1)S(1)}, u32[]{:S(2)}, u32[]{:S(2)}) collective-permute-start(bf16[2,48,384]{2,1,0:T(8,128)(2,1)S(1)} %collective-permute-done.13.refs_4_), channel_id=1, source_target_pairs={{0,8},{8,0},{1,9},{9,1},{2,10},{10,2},{3,11},{11,3},{4,12},{12,4},... | collective-permute-start | bytes 221192 | tf_op jit(solution)/shard_map/ppermute | solution.py:34
  48.5 4.0 %collective-permute-start.16 = (bf16[2,48,384]{2,1,0:T(8,128)(2,1)S(1)}, bf16[2,48,384]{2,1,0:T(8,128)(2,1)S(1)}, u32[]{:S(2)}, u32[]{:S(2)}) collective-permute-start(bf16[2,48,384]{2,1,0:T(8,128)(2,1)S(1)} %collective-permute-done.15.refs_6_), channel_id=1, source_target_pairs={{0,8},{8,0},{1,9},{9,1},{2,10},{10,2},{3,11},{11,3},{4,12},{12,4},... | collective-permute-start | bytes 221192 | tf_op jit(solution)/shard_map/ppermute | solution.py:34
  48.7 10.0 %collective-permute-start.11 = (bf16[2,48,384]{2,1,0:T(8,128)(2,1)S(1)}, bf16[2,48,384]{2,1,0:T(8,128)(2,1)S(1)}, u32[]{:S(2)}, u32[]{:S(2)}) collective-permute-start(bf16[2,48,384]{2,1,0:T(8,128)(2,1)S(1)} %get-tuple-element.25), channel_id=1, source_target_pairs={{0,32},{4,36},{16,48},{20,52},{32,0},{36,4},{48,16},{52,20},{1,33}... | collective-permute-start | bytes 221192 | tf_op jit(solution)/shard_map/ppermute | solution.py:55
  58.8 1.4 %collective-permute-start.17 = (bf16[2,48,384]{2,1,0:T(8,128)(2,1)S(1)}, bf16[2,48,384]{2,1,0:T(8,128)(2,1)S(1)}, u32[]{:S(2)}, u32[]{:S(2)}) collective-permute-start(bf16[2,48,384]{2,1,0:T(8,128)(2,1)S(1)} %collective-permute-done.11.refs_2_), channel_id=1, source_target_pairs={{0,8},{8,0},{1,9},{9,1},{2,10},{10,2},{3,11},{11,3},{4,12},{12,4},... | collective-permute-start | bytes 221192 | tf_op jit(solution)/shard_map/ppermute | solution.py:34
  62.9 9.9 %collective-permute-start.18 = (bf16[384,384]{1,0:T(8,128)(2,1)S(1)}, bf16[384,384]{1,0:T(8,128)(2,1)S(1)}, u32[]{:S(2)}, u32[]{:S(2)}) collective-permute-start(bf16[384,384]{1,0:T(8,128)(2,1)S(1)} %get-tuple-element.32), channel_id=1, source_target_pairs={{0,128},{64,192},{128,0},{192,64},{1,129},{65,193},{129,1},{193,65... | collective-permute-start | bytes 884744 | tf_op jit(solution)/shard_map/ppermute | solution.py:38
  65.9 13.8 %collective-permute-start.19 = (bf16[384,384]{1,0:T(8,128)(2,1)S(1)}, bf16[384,384]{1,0:T(8,128)(2,1)S(1)}, u32[]{:S(2)}, u32[]{:S(2)}) collective-permute-start(bf16[384,384]{1,0:T(8,128)(2,1)S(1)} %get-tuple-element.34), channel_id=1, source_target_pairs={{0,64},{64,128},{128,192},{192,0},{1,65},{65,129},{129,193},{193,1... | collective-permute-start | bytes 884744 | tf_op jit(solution)/shard_map/ppermute | solution.py:38
  66.3 13.4 %collective-permute-start.20 = (bf16[384,384]{1,0:T(8,128)(2,1)S(1)}, bf16[384,384]{1,0:T(8,128)(2,1)S(1)}, u32[]{:S(2)}, u32[]{:S(2)}) collective-permute-start(bf16[384,384]{1,0:T(8,128)(2,1)S(1)} %get-tuple-element.35), channel_id=1, source_target_pairs={{0,192},{64,0},{128,64},{192,128},{1,193},{65,1},{129,65},{193,129... | collective-permute-start | bytes 884744 | tf_op jit(solution)/shard_map/ppermute | solution.py:38
  81.6 22.9 %copy-start.3 = (f32[8,24,768]{2,1,0:T(8,128)S(1)}, f32[8,24,768]{2,1,0:T(8,128)}, u32[]{:S(2)}) copy-start(f32[8,24,768]{2,1,0:T(8,128)} %param.14) | copy-start | bytes 1769476
  81.6 22.9 %all-to-all-start = ((bf16[32,24,192]{2,1,0:T(8,128)(2,1)}), bf16[32,24,192]{2,1,0:T(8,128)(2,1)S(1)}, u32[]{:S(2)}, u32[]{:S(2)}) async-start(bf16[32,24,192]{2,1,0:T(8,128)(2,1)} %get-tuple-element.42), calls=%async_computation | async-start | bytes 786432 | tf_op jit(solution)/shard_map/all_to_all | solution.py:420
  89.4 1.9 %collective-permute-start.21 = (bf16[4,48,384]{2,1,0:T(8,128)(2,1)S(1)}, bf16[4,48,384]{2,1,0:T(8,128)(2,1)S(1)}, u32[]{:S(2)}, u32[]{:S(2)}) collective-permute-start(bf16[4,48,384]{2,1,0:T(8,128)(2,1)S(1)} %get-tuple-element.37), channel_id=1, source_target_pairs={{0,8},{8,0},{1,9},{9,1},{2,10},{10,2},{3,11},{11,3},{4,12},{12,4},... | collective-permute-start | bytes 442376 | tf_op jit(solution)/shard_map/ppermute | solution.py:34
  91.7 7.5 %collective-permute-start.22 = (bf16[2,48,384]{2,1,0:T(8,128)(2,1)S(1)}, bf16[2,48,384]{2,1,0:T(8,128)(2,1)S(1)}, u32[]{:S(2)}, u32[]{:S(2)}) collective-permute-start(bf16[2,48,384]{2,1,0:T(8,128)(2,1)S(1)} %get-tuple-element.38), channel_id=1, source_target_pairs={{0,32},{4,36},{16,48},{20,52},{32,0},{36,4},{48,16},{52,20},{1,33}... | collective-permute-start | bytes 221192 | tf_op jit(solution)/shard_map/ppermute | solution.py:55
  95.0 5.7 %collective-permute-start.23 = (bf16[2,48,384]{2,1,0:T(8,128)(2,1)S(1)}, bf16[2,48,384]{2,1,0:T(8,128)(2,1)S(1)}, u32[]{:S(2)}, u32[]{:S(2)}) collective-permute-start(bf16[2,48,384]{2,1,0:T(8,128)(2,1)S(1)} %get-tuple-element.40), channel_id=1, source_target_pairs={{0,16},{4,52},{16,32},{20,4},{32,48},{36,20},{48,0},{52,36},{1,17}... | collective-permute-start | bytes 221192 | tf_op jit(solution)/shard_map/ppermute | solution.py:55
  95.8 8.7 %collective-permute-start.24 = (bf16[2,48,384]{2,1,0:T(8,128)(2,1)S(1)}, bf16[2,48,384]{2,1,0:T(8,128)(2,1)S(1)}, u32[]{:S(2)}, u32[]{:S(2)}) collective-permute-start(bf16[2,48,384]{2,1,0:T(8,128)(2,1)S(1)} %get-tuple-element.41), channel_id=1, source_target_pairs={{0,48},{4,20},{16,0},{20,36},{32,16},{36,52},{48,32},{52,4},{1,49}... | collective-permute-start | bytes 221192 | tf_op jit(solution)/shard_map/ppermute | solution.py:55

commit v4 on v3

--- a/solution.py
+++ b/solution.py
@@ -146,8 +146,9 @@
 
 
 def stack_kernel(after, *refs):
-    parts, out, sems = refs[:NZ], refs[NZ], refs[NZ + 1]
-    copies = [pltpu.make_async_copy(parts[i], out.at[i], sems.at[i]) for i in range(NZ)]
+    count = NZ - 1
+    parts, out, sems = refs[:count], refs[count], refs[count + 1]
+    copies = [pltpu.make_async_copy(parts[i], out.at[i], sems.at[i]) for i in range(count)]
     for cp in copies:
         cp.start()
     for cp in copies:
@@ -160,7 +161,8 @@
     pc, xc = [], []
     for i in range(count):
         k, side = (first_label + i) // 2, (first_label + i) % 2
-        pc.append(pltpu.make_async_copy(ps[side].at[k], pbuf.at[i], psem.at[i]))
+        tiles = ps[side].at[k] if fresh else ps[side]
+        pc.append(pltpu.make_async_copy(tiles, pbuf.at[i], psem.at[i]))
         xc.append(pltpu.make_async_copy(xs[i].at[side], xbuf.at[i], xsem.at[i]))
     for cp in pc + xc:
         cp.start()
@@ -241,12 +243,6 @@
     finish_products(acc, own_ref, sends)
 
 
-def a_kernel(place, *refs):
-    ps, xs, (own_ref, *sends) = refs[:2], refs[2:10], refs[10:14]
-    add_products((0, NH), place, ps, xs, *refs[14:], fresh=True)
-    finish_products(refs[14], own_ref, sends)
-
-
 def product_scratch(count):
     return [
         pltpu.VMEM((count, ROWS + 8, COLS), BF),
@@ -341,8 +337,8 @@
         compiler_params=params(12),
         name="arrange_tiles",
     )(jnp.transpose(alpha_values[0, :, 0], (0, 2, 3, 1)), alpha_rows[0, :, 0], turn_rows())
-    a_next = send_step(tiles, 2)
-    a_near = [tiles, cross_z(tiles, 1), a_next, cross_z(a_next, 1)]
+    a_near = [tiles, cross_z(tiles, 1), send_step(tiles, 2)]
+    a_far = cross_z(tiles, 2)
 
     col_block = beta_rows[0] // 6
     slots = (((col_block // NX) ^ zl) * NX + (col_block % NX - x) % NX) * 6 + beta_rows[0] % 6
@@ -370,10 +366,10 @@
     x_parts = direct + [flip_core(a) for a in direct[:3]]
     a_own = pl.pallas_call(
         stack_kernel,
-        out_shape=jax.ShapeDtypeStruct((NZ, ROWS + 8, COLS), BF),
-        in_specs=[HBM] * 5,
+        out_shape=jax.ShapeDtypeStruct((NZ - 1, ROWS + 8, COLS), BF),
+        in_specs=[HBM] * NZ,
         out_specs=HBM,
-        scratch_shapes=[pltpu.SemaphoreType.DMA((NZ,))],
+        scratch_shapes=[pltpu.SemaphoreType.DMA((NZ - 1,))],
         compiler_params=params(4),
         name="stack_tiles",
     )(x_out[0], *a_near)
@@ -393,7 +389,7 @@
         cost_estimate=cost(6),
         name="alpha_product_first",
     )(y.reshape(1), *a_pair, *by_label)
-    farthest, done = lax.optimization_barrier((direct[3], done))
+    farthest, a_far, done = lax.optimization_barrier((direct[3], a_far, done))
     _, own, s1, s2, s3 = pl.pallas_call(
         last_kernel,
         out_shape=[total, jax.ShapeDtypeStruct((size, 128), F32), part, part, part],
@@ -403,7 +399,7 @@
         scratch_shapes=product_scratch(NH - FIRST),
         compiler_params=params(16),
         name="alpha_product_last",
-    )(y.reshape(1), *a_pair, farthest, flip_core(farthest), acc, done)
+    )(y.reshape(1), a_far, flip_core(a_far), farthest, flip_core(farthest), acc, done)
     r2, r1, r3 = shift_y(s2, 2), shift_y(s1, 1), shift_y(s3, 3)
 
     y_out = pl.pallas_call(

time: 107 us -> 113 us (1.056)
  waiting for transfers between devices: 32.7 us -> 39.6 us
    ppermute x2, waiting for transfers between devices: 0.01 us -> 7.24 us  [cross_z(): return lax.ppermute(a, ('zh', 'zl'), moves)]
    ppermute x7, waiting for transfers between devices: 15.6 us -> 8.64 us  [send_step(): return lax.ppermute(a, ('zh', 'zl'), moves)]
    ppermute x6, waiting for transfers between devices: 3.98 us -> 10.3 us  [shift_x(): return lax.ppermute(a, 'x', [(i, (i + k) % NX) for i in range(NX)])]
    ppermute x7, starting transfers between devices: 15.4 us -> 12.7 us  [send_step(): return lax.ppermute(a, ('zh', 'zl'), moves)]
    all_to_all x1, starting transfers between devices: 7.76 us -> 9.85 us  [per_device(): lax.all_to_all(y_out[NC], ('y', 'zl', 'x'), split_axis=0, concat_axis=0,...]
    ppermute x6, starting transfers between devices: 5.62 us -> 6.82 us  [shift_x(): return lax.ppermute(a, 'x', [(i, (i + k) % NX) for i in range(NX)])]
    ppermute x6 -> x7, starting transfers between devices: 6.78 us -> 6.24 us  [flip_core(): return lax.ppermute(a, 'core', [(0, 1), (1, 0)])]
    ppermute x6 -> x7, waiting for transfers between devices: 1.96 us -> 2.3 us  [flip_core(): return lax.ppermute(a, 'core', [(0, 1), (1, 0)])]
  transfers between devices with their start and end apart: 26 -> 27, of which waited for: 11 -> 10; matrix products, arithmetic and copies ran while one was open for 1% -> 1% of each run, Pallas kernels for 10% -> 10%
where the time goes in v4:
time: 113 us
  starting transfers between devices  51 us (45%)
  waiting for transfers between devices  39.6 us (35%)
  Pallas kernels  17.6 us (16%)
  local copies, waits for them, and re-layouts  3.49 us (3%)
    ppermute x7, starting transfers between devices, send_step(): return lax.ppermute(a, ('zh', 'zl'), moves)  12.7 us
    ppermute x3, waiting for transfers between devices, shift_y(): return lax.ppermute(a, 'y', [(i, (i + k) % NY) for i in range(NY)])  11.1 us
    ppermute x6, waiting for transfers between devices, shift_x(): return lax.ppermute(a, 'x', [(i, (i + k) % NX) for i in range(NX)])  10.3 us
    all_to_all x1, starting transfers between devices, per_device(): lax.all_to_all(y_out[NC], ('y', 'zl', 'x'), split_axis=0, concat_axis=0,...  9.85 us
    ppermute x7, waiting for transfers between devices, send_step(): return lax.ppermute(a, ('zh', 'zl'), moves)  8.64 us
    ppermute x2, waiting for transfers between devices, cross_z(): return lax.ppermute(a, ('zh', 'zl'), moves)  7.24 us
    ppermute x2, starting transfers between devices, cross_z(): return lax.ppermute(a, ('zh', 'zl'), moves)  7.22 us
    ppermute x6, starting transfers between devices, shift_x(): return lax.ppermute(a, 'x', [(i, (i + k) % NX) for i in range(NX)])  6.82 us
  transfers between devices with their start and end apart: 27, of which 10 were waited for; matrix products, arithmetic and copies ran while one was open for 1% of the time, Pallas kernels for 10%

profile of v4, /device:TPU:1, one launch (start us, length us, event | category | flops | bytes accessed | tf_op | source)
XLA Modules:
  0.0 113.0 jit_solution(12880394148619308625)
XLA Ops:
  0.0 2.6 %collective-permute-start = (bf16[192,768]{1,0:T(8,128)(2,1)}, bf16[192,768]{1,0:T(8,128)(2,1)S(1)}, u32[]{:S(2)}, u32[]{:S(2)}) collective-permute-start(bf16[192,768]{1,0:T(8,128)(2,1)} %bitcast.17), channel_id=1, source_target_pairs={{0,4},{4,0},{1,5},{5,1},{2,6},{6,2},{3,7},{7,3},{8,12},{12,8},{9,1... | collective-permute-start | bytes 884744 | tf_op jit(solution)/shard_map/ppermute | solution.py:30
  2.6 1.2 %collective-permute-start.4 = (bf16[192,768]{1,0:T(8,128)(2,1)}, bf16[192,768]{1,0:T(8,128)(2,1)S(1)}, u32[]{:S(2)}, u32[]{:S(2)}) collective-permute-start(bf16[192,768]{1,0:T(8,128)(2,1)} %bitcast.18), channel_id=1, source_target_pairs={{0,1},{1,2},{2,3},{3,0},{4,5},{5,6},{6,7},{7,4},{8,9},{9,10},{10,1... | collective-permute-start | bytes 884744 | tf_op jit(solution)/shard_map/ppermute | solution.py:26
  3.8 1.5 %collective-permute-start.6 = (bf16[192,768]{1,0:T(8,128)(2,1)}, bf16[192,768]{1,0:T(8,128)(2,1)S(1)}, u32[]{:S(2)}, u32[]{:S(2)}) collective-permute-start(bf16[192,768]{1,0:T(8,128)(2,1)} %bitcast.19), channel_id=1, source_target_pairs={{0,3},{1,0},{2,1},{3,2},{4,7},{5,4},{6,5},{7,6},{8,11},{9,8},{10,9... | collective-permute-start | bytes 884744 | tf_op jit(solution)/shard_map/ppermute | solution.py:26
  5.2 1.3 %copy-done = bf16[1,8,1,32,24,24]{3,5,4,2,1,0:T(8,128)(2,1)S(1)} copy-done((bf16[1,8,1,32,24,24]{3,5,4,2,1,0:T(8,128)(2,1)S(1)}, bf16[1,8,1,32,24,24]{3,5,4,2,1,0:T(8,128)(2,1)}, u32[]{:S(2)}) %copy-start) | copy-done | bytes 294936
  6.5 1.3 %copy-done.2 = bf16[768,768]{1,0:T(8,128)(2,1)S(1)} copy-done((bf16[768,768]{1,0:T(8,128)(2,1)S(1)}, bf16[768,768]{1,0:T(8,128)(2,1)}, u32[]{:S(2)}) %copy-start.2) | copy-done | bytes 1179672
  7.8 0.7 copy-done.4
  8.5 0.7 arrange_tiles.1.refs_0_
  9.2 4.7 %collective-permute-start.9 = (bf16[200,768]{1,0:T(8,128)(2,1)S(1)}, bf16[200,768]{1,0:T(8,128)(2,1)S(1)}, u32[]{:S(2)}, u32[]{:S(2)}) collective-permute-start(bf16[200,768]{1,0:T(8,128)(2,1)S(1)} %arrange_tiles.1.refs_0_), channel_id=1, source_target_pairs={{0,52},{4,16},{16,4},{20,32},{32,20},{36,48},{48,36},{52,0},{1,53}... | collective-permute-start | bytes 921608 | tf_op jit(solution)/shard_map/ppermute | solution.py:46
  14.0 1.2 %collective-permute-start.10 = (bf16[200,768]{1,0:T(8,128)(2,1)S(1)}, bf16[200,768]{1,0:T(8,128)(2,1)S(1)}, u32[]{:S(2)}, u32[]{:S(2)}) collective-permute-start(bf16[200,768]{1,0:T(8,128)(2,1)S(1)} %arrange_tiles.1.refs_0_), channel_id=1, source_target_pairs={{0,48},{4,20},{16,0},{20,36},{32,16},{36,52},{48,32},{52,4},{1,49}... | collective-permute-start | bytes 921608 | tf_op jit(solution)/shard_map/ppermute | solution.py:55
  15.2 0.1 rem.118
  15.3 0.1 div.33
  15.4 0.1 ne.108
  15.5 0.0 collective-permute-done.refs_0_
  15.5 1.3 %collective-permute-start.1 = (bf16[192,768]{1,0:T(8,128)(2,1)S(1)}, bf16[192,768]{1,0:T(8,128)(2,1)S(1)}, u32[]{:S(2)}, u32[]{:S(2)}) collective-permute-start(bf16[192,768]{1,0:T(8,128)(2,1)S(1)} %collective-permute-done.refs_0_), channel_id=1, source_target_pairs={{0,3},{1,0},{2,1},{3,2},{4,7},{5,4},{6,5},{7,6},{8,11},{9,8},{10,9... | collective-permute-start | bytes 884744 | tf_op jit(solution)/shard_map/ppermute | solution.py:26
  16.9 0.1 broadcast_add_fusion
  16.9 0.0 collective-permute-done.4.refs_4_
  16.9 0.2 collective-permute-start.3
  17.2 0.0 collective-permute-done.6.refs_6_
  17.2 0.1 collective-permute-start.5
  17.3 4.7 %collective-permute-done.1.refs_2_ = bf16[192,768]{1,0:T(8,128)(2,1)S(1)} collective-permute-done((bf16[192,768]{1,0:T(8,128)(2,1)S(1)}, bf16[192,768]{1,0:T(8,128)(2,1)S(1)}, u32[]{:S(2)}, u32[]{:S(2)}) %collective-permute-start.1) | collective-permute-done | bytes 294944 | tf_op jit(solution)/shard_map/ppermute | solution.py:26
  22.0 2.5 %collective-permute-start.2 = (bf16[192,768]{1,0:T(8,128)(2,1)S(1)}, bf16[192,768]{1,0:T(8,128)(2,1)S(1)}, u32[]{:S(2)}, u32[]{:S(2)}) collective-permute-start(bf16[192,768]{1,0:T(8,128)(2,1)S(1)} %collective-permute-done.1.refs_2_), channel_id=1, source_target_pairs={{0,3},{1,0},{2,1},{3,2},{4,7},{5,4},{6,5},{7,6},{8,11},{9,8},{10,9... | collective-permute-start | bytes 884744 | tf_op jit(solution)/shard_map/ppermute | solution.py:26
  24.5 0.6 fusion.refs_9_
  25.1 5.5 %collective-permute-done.5.refs_5_ = bf16[192,768]{1,0:T(8,128)(2,1)S(1)} collective-permute-done((bf16[192,768]{1,0:T(8,128)(2,1)S(1)}, bf16[192,768]{1,0:T(8,128)(2,1)S(1)}, u32[]{:S(2)}, u32[]{:S(2)}) %collective-permute-start.5) | collective-permute-done | bytes 294944 | tf_op jit(solution)/shard_map/ppermute | solution.py:26
  30.6 0.0 collective-permute-done.2.refs_1_
  30.6 3.4 %beta_product.1 = (bf16[2,48,384]{2,1,0:T(8,128)(2,1)S(1)}, bf16[2,48,384]{2,1,0:T(8,128)(2,1)S(1)}, bf16[2,48,384]{2,1,0:T(8,128)(2,1)S(1)}, bf16[2,48,384]{2,1,0:T(8,128)(2,1)S(1)}) custom-call(s32[36]{0:T(128)S(1)} %fusion.5.slots, bf16[192,768]{1,0:T(8,128)(2,1)S(1)} %collective-permute-done.refs_0_, ...), custom_call_target="tpu_custom_call" | custom-call | tf_op jit(solution)/shard_map/beta_product/pallas_call | solution.py:352
  34.0 0.0 collective-permute-done.9.refs_1_
  34.1 0.0 collective-permute-done.10.refs_2_
  34.1 0.3 stack_tiles.1.refs_0_
  34.3 3.4 %collective-permute-start.11 = (bf16[3,200,768]{2,1,0:T(8,128)(2,1)S(1)}, bf16[3,200,768]{2,1,0:T(8,128)(2,1)S(1)}, u32[]{:S(2)}, u32[]{:S(2)}) collective-permute-start(bf16[3,200,768]{2,1,0:T(8,128)(2,1)S(1)} %stack_tiles.1.refs_0_), channel_id=1, source_target_pairs={{0,8},{8,0},{1,9},{9,1},{2,10},{10,2},{3,11},{11,3},{4,12},{12,4},... | collective-permute-start | bytes 2764808 | tf_op jit(solution)/shard_map/ppermute | solution.py:34
  37.7 1.2 %collective-permute-start.13 = (bf16[2,48,384]{2,1,0:T(8,128)(2,1)S(1)}, bf16[2,48,384]{2,1,0:T(8,128)(2,1)S(1)}, u32[]{:S(2)}, u32[]{:S(2)}) collective-permute-start(bf16[2,48,384]{2,1,0:T(8,128)(2,1)S(1)} %get-tuple-element.27), channel_id=1, source_target_pairs={{0,16},{4,52},{16,32},{20,4},{32,48},{36,20},{48,0},{52,36},{1,17}... | collective-permute-start | bytes 221192 | tf_op jit(solution)/shard_map/ppermute | solution.py:55
  38.9 2.4 %collective-permute-start.15 = (bf16[2,48,384]{2,1,0:T(8,128)(2,1)S(1)}, bf16[2,48,384]{2,1,0:T(8,128)(2,1)S(1)}, u32[]{:S(2)}, u32[]{:S(2)}) collective-permute-start(bf16[2,48,384]{2,1,0:T(8,128)(2,1)S(1)} %get-tuple-element.28), channel_id=1, source_target_pairs={{0,48},{4,20},{16,0},{20,36},{32,16},{36,52},{48,32},{52,4},{1,49}... | collective-permute-start | bytes 221192 | tf_op jit(solution)/shard_map/ppermute | solution.py:55
  41.3 0.6 collective-permute-start.12
  41.9 3.3 %collective-permute-done.13.refs_4_ = bf16[2,48,384]{2,1,0:T(8,128)(2,1)S(1)} collective-permute-done((bf16[2,48,384]{2,1,0:T(8,128)(2,1)S(1)}, bf16[2,48,384]{2,1,0:T(8,128)(2,1)S(1)}, u32[]{:S(2)}, u32[]{:S(2)}) %collective-permute-start.13) | collective-permute-done | bytes 73760 | tf_op jit(solution)/shard_map/ppermute | solution.py:55
  45.2 0.9 collective-permute-start.14
  46.1 0.0 collective-permute-done.15.refs_6_
  46.1 0.0 collective-permute-start.16
  46.1 2.5 %collective-permute-start.8 = (bf16[200,768]{1,0:T(8,128)(2,1)S(1)}, bf16[200,768]{1,0:T(8,128)(2,1)S(1)}, u32[]{:S(2)}, u32[]{:S(2)}) collective-permute-start(bf16[200,768]{1,0:T(8,128)(2,1)S(1)} %arrange_tiles.1.refs_0_), channel_id=1, source_target_pairs={{0,36},{4,32},{16,52},{20,48},{32,4},{36,0},{48,20},{52,16},{1,37}... | collective-permute-start | bytes 921608 | tf_op jit(solution)/shard_map/ppermute | solution.py:46
  48.6 2.2 %collective-permute-start.7 = (bf16[2,48,384]{2,1,0:T(8,128)(2,1)S(1)}, bf16[2,48,384]{2,1,0:T(8,128)(2,1)S(1)}, u32[]{:S(2)}, u32[]{:S(2)}) collective-permute-start(bf16[2,48,384]{2,1,0:T(8,128)(2,1)S(1)} %get-tuple-element.25), channel_id=1, source_target_pairs={{0,32},{4,36},{16,48},{20,52},{32,0},{36,4},{48,16},{52,20},{1,33}... | collective-permute-start | bytes 221192 | tf_op jit(solution)/shard_map/ppermute | solution.py:55
  50.7 0.0 collective-permute-done.11.refs_1_
  50.8 6.2 %alpha_product_first.1 = (f32[6144,128]{1,0:T(8,128)S(1)}, f32[8,128]{1,0:T(8,128)S(1)}) custom-call(s32[1]{0:T(128)} %bitcast.place, bf16[3,200,768]{2,1,0:T(8,128)(2,1)S(1)} %stack_tiles.1.refs_0_, bf16[3,200,768]{2,1,0:T(8,128)(2,1)S(1)} %collective-permute-done.11.refs_1_, bf16[2,48,384]{2,1,0:T(8,128)(2,1)S(1)} %get-tuple-element.26.after.refs_2_, ...), custom_call_target="tpu_custom_call" | custom-call | flops 6899999744 | bytes 1048576 | tf_op jit(solution)/shard_map/alpha_product_first/pallas_call | solution.py:382
  57.0 7.2 %collective-permute-done.8.refs_0_ = bf16[200,768]{1,0:T(8,128)(2,1)S(1)} collective-permute-done((bf16[200,768]{1,0:T(8,128)(2,1)S(1)}, bf16[200,768]{1,0:T(8,128)(2,1)S(1)}, u32[]{:S(2)}, u32[]{:S(2)}) %collective-permute-start.8) | collective-permute-done | bytes 307232 | tf_op jit(solution)/shard_map/ppermute | solution.py:46
  64.2 0.5 collective-permute-start.17
  64.7 0.0 collective-permute-start.18
  64.8 1.3 %collective-permute-done.18.refs_3_ = bf16[2,48,384]{2,1,0:T(8,128)(2,1)S(1)} collective-permute-done((bf16[2,48,384]{2,1,0:T(8,128)(2,1)S(1)}, bf16[2,48,384]{2,1,0:T(8,128)(2,1)S(1)}, u32[]{:S(2)}, u32[]{:S(2)}) %collective-permute-start.18) | collective-permute-done | bytes 73760 | tf_op jit(solution)/shard_map/ppermute | solution.py:34
  66.0 0.0 collective-permute-done.17.refs_1_
  66.0 2.7 %alpha_product_last.1 = (f32[6144,128]{1,0:T(8,128)S(1)}, f32[1536,128]{1,0:T(8,128)S(1)}, bf16[384,384]{1,0:T(8,128)(2,1)S(1)}, bf16[384,384]{1,0:T(8,128)(2,1)S(1)}, bf16[384,384]{1,0:T(8,128)(2,1)S(1)}) custom-call(s32[1]{0:T(128)} %bitcast.place, bf16[200,768]{1,0:T(8,128)(2,1)S(1)} %collective-permute-done.8.refs_0_, ...), custom_call_target="tpu_custom_call", output_to_operand_aliasing={{0}: (5, {})} | custom-call | tf_op jit(solution)/shard_map/alpha_product_last/pallas_call | solution.py:393
  68.8 3.0 %collective-permute-start.19 = (bf16[384,384]{1,0:T(8,128)(2,1)S(1)}, bf16[384,384]{1,0:T(8,128)(2,1)S(1)}, u32[]{:S(2)}, u32[]{:S(2)}) collective-permute-start(bf16[384,384]{1,0:T(8,128)(2,1)S(1)} %get-tuple-element.34), channel_id=1, source_target_pairs={{0,128},{64,192},{128,0},{192,64},{1,129},{65,193},{129,1},{193,65... | collective-permute-start | bytes 884744 | tf_op jit(solution)/shard_map/ppermute | solution.py:38
  71.8 0.4 collective-permute-start.20
  72.2 2.3 %collective-permute-start.21 = (bf16[384,384]{1,0:T(8,128)(2,1)S(1)}, bf16[384,384]{1,0:T(8,128)(2,1)S(1)}, u32[]{:S(2)}, u32[]{:S(2)}) collective-permute-start(bf16[384,384]{1,0:T(8,128)(2,1)S(1)} %get-tuple-element.37), channel_id=1, source_target_pairs={{0,192},{64,0},{128,64},{192,128},{1,193},{65,1},{129,65},{193,129... | collective-permute-start | bytes 884744 | tf_op jit(solution)/shard_map/ppermute | solution.py:38
  74.5 4.2 %collective-permute-done.19.r2 = bf16[384,384]{1,0:T(8,128)(2,1)S(1)} collective-permute-done((bf16[384,384]{1,0:T(8,128)(2,1)S(1)}, bf16[384,384]{1,0:T(8,128)(2,1)S(1)}, u32[]{:S(2)}, u32[]{:S(2)}) %collective-permute-start.19) | collective-permute-done | bytes 294944 | tf_op jit(solution)/shard_map/ppermute | solution.py:38
  78.6 7.0 %collective-permute-done.20.r1 = bf16[384,384]{1,0:T(8,128)(2,1)S(1)} collective-permute-done((bf16[384,384]{1,0:T(8,128)(2,1)S(1)}, bf16[384,384]{1,0:T(8,128)(2,1)S(1)}, u32[]{:S(2)}, u32[]{:S(2)}) %collective-permute-start.20) | collective-permute-done | bytes 294944 | tf_op jit(solution)/shard_map/ppermute | solution.py:38
  85.6 1.9 %y_sum.1 = (bf16[4,48,384]{2,1,0:T(8,128)(2,1)S(1)}, bf16[4,48,384]{2,1,0:T(8,128)(2,1)S(1)}, bf16[32,24,192]{2,1,0:T(8,128)(2,1)}) custom-call(s32[8]{0:T(128)S(1)} %get-tuple-element.48.dests, bf16[384,384]{1,0:T(8,128)(2,1)S(1)} %collective-permute-done.19.r2, f32[1536,128]{1,0:T(8,128)S(1)} %get-tuple-element.35.own, ...), custom_call_target="tpu_custom_call" | custom-call | tf_op jit(solution)/shard_map/y_sum/pallas_call | solution.py:405
  87.5 9.9 %all-to-all-start = ((bf16[32,24,192]{2,1,0:T(8,128)(2,1)}), bf16[32,24,192]{2,1,0:T(8,128)(2,1)S(1)}, u32[]{:S(2)}, u32[]{:S(2)}) async-start(bf16[32,24,192]{2,1,0:T(8,128)(2,1)} %get-tuple-element.44), calls=%async_computation | async-start | bytes 786432 | tf_op jit(solution)/shard_map/all_to_all | solution.py:416
  97.4 0.9 collective-permute-start.22
  98.2 1.0 collective-permute-done.22.came
  99.3 0.4 pair_pieces.1
  99.7 2.2 %collective-permute-start.23 = (bf16[2,48,384]{2,1,0:T(8,128)(2,1)S(1)}, bf16[2,48,384]{2,1,0:T(8,128)(2,1)S(1)}, u32[]{:S(2)}, u32[]{:S(2)}) collective-permute-start(bf16[2,48,384]{2,1,0:T(8,128)(2,1)S(1)} %get-tuple-element.40), channel_id=1, source_target_pairs={{0,32},{4,36},{16,48},{20,52},{32,0},{36,4},{48,16},{52,20},{1,33}... | collective-permute-start | bytes 221192 | tf_op jit(solution)/shard_map/ppermute | solution.py:55
  101.8 0.7 collective-permute-start.24
  102.6 2.9 %collective-permute-start.25 = (bf16[2,48,384]{2,1,0:T(8,128)(2,1)S(1)}, bf16[2,48,384]{2,1,0:T(8,128)(2,1)S(1)}, u32[]{:S(2)}, u32[]{:S(2)}) collective-permute-start(bf16[2,48,384]{2,1,0:T(8,128)(2,1)S(1)} %get-tuple-element.43), channel_id=1, source_target_pairs={{0,48},{4,20},{16,0},{20,36},{32,16},{36,52},{48,32},{52,4},{1,49}... | collective-permute-start | bytes 221192 | tf_op jit(solution)/shard_map/ppermute | solution.py:55
  105.4 0.3 fusion.1.refs_5_
  105.8 3.2 %collective-permute-done.23.refs_0_ = bf16[2,48,384]{2,1,0:T(8,128)(2,1)S(1)} collective-permute-done((bf16[2,48,384]{2,1,0:T(8,128)(2,1)S(1)}, bf16[2,48,384]{2,1,0:T(8,128)(2,1)S(1)}, u32[]{:S(2)}, u32[]{:S(2)}) %collective-permute-start.23) | collective-permute-done | bytes 73760 | tf_op jit(solution)/shard_map/ppermute | solution.py:55
  108.9 0.0 collective-permute-done.24.refs_2_
  108.9 2.2 %collective-permute-done.25.refs_3_ = bf16[2,48,384]{2,1,0:T(8,128)(2,1)S(1)} collective-permute-done((bf16[2,48,384]{2,1,0:T(8,128)(2,1)S(1)}, bf16[2,48,384]{2,1,0:T(8,128)(2,1)S(1)}, u32[]{:S(2)}, u32[]{:S(2)}) %collective-permute-start.25) | collective-permute-done | bytes 73760 | tf_op jit(solution)/shard_map/ppermute | solution.py:55
  111.1 1.9 %combine.1 = f32[192,768]{1,0:T(8,128)} custom-call(bf16[2,48,384]{2,1,0:T(8,128)(2,1)S(1)} %collective-permute-done.23.refs_0_, bf16[2,48,384]{2,1,0:T(8,128)(2,1)S(1)} %get-tuple-element.41.refs_1_, bf16[2,48,384]{2,1,0:T(8,128)(2,1)S(1)} %collective-permute-done.24.refs_2_, bf16[2,48,384]{2,1,0:T(8,128)(2,1)S(1)} %collective-permute-done.25.refs_3_, ...), custom_call_target="tpu_custom_call" | custom-call | tf_op jit(solution)/shard_map/combine/pallas_call | solution.py:427
  (26 shorter events, 0.2 us)
Async XLA Ops:
  0.0 15.5 %copy-start.6 = (s32[8]{0:T(128)S(1)}, s32[8]{0:T(128)}, u32[]{:S(2)}) copy-start(s32[8]{0:T(128)} %constant.114.clone) | copy-start | bytes 100
  0.0 15.5 %copy-start.7 = (s32[8]{0:T(128)S(1)}, s32[8]{0:T(128)}, u32[]{:S(2)}) copy-start(s32[8]{0:T(128)} %constant.113.clone) | copy-start | bytes 100
  0.0 15.2 %copy-start.5 = (s32[1,6,6]{2,0,1:T(1,128)S(1)}, s32[1,6,6]{2,0,1:T(1,128)}, u32[]{:S(2)}) copy-start(s32[1,6,6]{2,0,1:T(1,128)} %param.11) | copy-start | bytes 436
  0.0 15.5 %collective-permute-start = (bf16[192,768]{1,0:T(8,128)(2,1)}, bf16[192,768]{1,0:T(8,128)(2,1)S(1)}, u32[]{:S(2)}, u32[]{:S(2)}) collective-permute-start(bf16[192,768]{1,0:T(8,128)(2,1)} %bitcast.17), channel_id=1, source_target_pairs={{0,4},{4,0},{1,5},{5,1},{2,6},{6,2},{3,7},{7,3},{8,12},{12,8},{9,1... | collective-permute-start | bytes 884744 | tf_op jit(solution)/shard_map/ppermute | solution.py:30
  2.6 14.4 %collective-permute-start.4 = (bf16[192,768]{1,0:T(8,128)(2,1)}, bf16[192,768]{1,0:T(8,128)(2,1)S(1)}, u32[]{:S(2)}, u32[]{:S(2)}) collective-permute-start(bf16[192,768]{1,0:T(8,128)(2,1)} %bitcast.18), channel_id=1, source_target_pairs={{0,1},{1,2},{2,3},{3,0},{4,5},{5,6},{6,7},{7,4},{8,9},{9,10},{10,1... | collective-permute-start | bytes 884744 | tf_op jit(solution)/shard_map/ppermute | solution.py:26
  3.8 13.4 %collective-permute-start.6 = (bf16[192,768]{1,0:T(8,128)(2,1)}, bf16[192,768]{1,0:T(8,128)(2,1)S(1)}, u32[]{:S(2)}, u32[]{:S(2)}) collective-permute-start(bf16[192,768]{1,0:T(8,128)(2,1)} %bitcast.19), channel_id=1, source_target_pairs={{0,3},{1,0},{2,1},{3,2},{4,7},{5,4},{6,5},{7,6},{8,11},{9,8},{10,9... | collective-permute-start | bytes 884744 | tf_op jit(solution)/shard_map/ppermute | solution.py:26
  5.2 1.3 %copy-start = (bf16[1,8,1,32,24,24]{3,5,4,2,1,0:T(8,128)(2,1)S(1)}, bf16[1,8,1,32,24,24]{3,5,4,2,1,0:T(8,128)(2,1)}, u32[]{:S(2)}) copy-start(bf16[1,8,1,32,24,24]{3,5,4,2,1,0:T(8,128)(2,1)} %param.12) | copy-start | bytes 884740
  6.5 1.3 %copy-start.2 = (bf16[768,768]{1,0:T(8,128)(2,1)S(1)}, bf16[768,768]{1,0:T(8,128)(2,1)}, u32[]{:S(2)}) copy-start(bf16[768,768]{1,0:T(8,128)(2,1)} %constant.115.clone.turn) | copy-start | bytes 3538948
  7.8 0.7 copy-start.4
  8.5 22.2 %copy-start.1 = (bf16[1,6,6,128,128]{4,3,2,1,0:T(8,128)(2,1)S(1)}, bf16[1,6,6,128,128]{4,3,2,1,0:T(8,128)(2,1)}, u32[]{:S(2)}) copy-start(bf16[1,6,6,128,128]{4,3,2,1,0:T(8,128)(2,1)} %param.10) | copy-start | bytes 3538948
  9.2 24.8 %collective-permute-start.9 = (bf16[200,768]{1,0:T(8,128)(2,1)S(1)}, bf16[200,768]{1,0:T(8,128)(2,1)S(1)}, u32[]{:S(2)}, u32[]{:S(2)}) collective-permute-start(bf16[200,768]{1,0:T(8,128)(2,1)S(1)} %arrange_tiles.1.refs_0_), channel_id=1, source_target_pairs={{0,52},{4,16},{16,4},{20,32},{32,20},{36,48},{48,36},{52,0},{1,53}... | collective-permute-start | bytes 921608 | tf_op jit(solution)/shard_map/ppermute | solution.py:46
  14.0 20.1 %collective-permute-start.10 = (bf16[200,768]{1,0:T(8,128)(2,1)S(1)}, bf16[200,768]{1,0:T(8,128)(2,1)S(1)}, u32[]{:S(2)}, u32[]{:S(2)}) collective-permute-start(bf16[200,768]{1,0:T(8,128)(2,1)S(1)} %arrange_tiles.1.refs_0_), channel_id=1, source_target_pairs={{0,48},{4,20},{16,0},{20,36},{32,16},{36,52},{48,32},{52,4},{1,49}... | collective-permute-start | bytes 921608 | tf_op jit(solution)/shard_map/ppermute | solution.py:55
  15.5 6.5 %collective-permute-start.1 = (bf16[192,768]{1,0:T(8,128)(2,1)S(1)}, bf16[192,768]{1,0:T(8,128)(2,1)S(1)}, u32[]{:S(2)}, u32[]{:S(2)}) collective-permute-start(bf16[192,768]{1,0:T(8,128)(2,1)S(1)} %collective-permute-done.refs_0_), channel_id=1, source_target_pairs={{0,3},{1,0},{2,1},{3,2},{4,7},{5,4},{6,5},{7,6},{8,11},{9,8},{10,9... | collective-permute-start | bytes 884744 | tf_op jit(solution)/shard_map/ppermute | solution.py:26
  16.9 8.2 %collective-permute-start.3 = (bf16[192,768]{1,0:T(8,128)(2,1)S(1)}, bf16[192,768]{1,0:T(8,128)(2,1)S(1)}, u32[]{:S(2)}, u32[]{:S(2)}) collective-permute-start(bf16[192,768]{1,0:T(8,128)(2,1)S(1)} %collective-permute-done.refs_0_), channel_id=1, source_target_pairs={{0,1},{1,2},{2,3},{3,0},{4,5},{5,6},{6,7},{7,4},{8,9},{9,10},{10,1... | collective-permute-start | bytes 884744 | tf_op jit(solution)/shard_map/ppermute | solution.py:26
  17.2 13.5 %collective-permute-start.5 = (bf16[192,768]{1,0:T(8,128)(2,1)S(1)}, bf16[192,768]{1,0:T(8,128)(2,1)S(1)}, u32[]{:S(2)}, u32[]{:S(2)}) collective-permute-start(bf16[192,768]{1,0:T(8,128)(2,1)S(1)} %collective-permute-done.4.refs_4_), channel_id=1, source_target_pairs={{0,1},{1,2},{2,3},{3,0},{4,5},{5,6},{6,7},{7,4},{8,9},{9,10},{10,1... | collective-permute-start | bytes 884744 | tf_op jit(solution)/shard_map/ppermute | solution.py:26
  22.0 8.6 %collective-permute-start.2 = (bf16[192,768]{1,0:T(8,128)(2,1)S(1)}, bf16[192,768]{1,0:T(8,128)(2,1)S(1)}, u32[]{:S(2)}, u32[]{:S(2)}) collective-permute-start(bf16[192,768]{1,0:T(8,128)(2,1)S(1)} %collective-permute-done.1.refs_2_), channel_id=1, source_target_pairs={{0,3},{1,0},{2,1},{3,2},{4,7},{5,4},{6,5},{7,6},{8,11},{9,8},{10,9... | collective-permute-start | bytes 884744 | tf_op jit(solution)/shard_map/ppermute | solution.py:26
  34.3 16.4 %collective-permute-start.11 = (bf16[3,200,768]{2,1,0:T(8,128)(2,1)S(1)}, bf16[3,200,768]{2,1,0:T(8,128)(2,1)S(1)}, u32[]{:S(2)}, u32[]{:S(2)}) collective-permute-start(bf16[3,200,768]{2,1,0:T(8,128)(2,1)S(1)} %stack_tiles.1.refs_0_), channel_id=1, source_target_pairs={{0,8},{8,0},{1,9},{9,1},{2,10},{10,2},{3,11},{11,3},{4,12},{12,4},... | collective-permute-start | bytes 2764808 | tf_op jit(solution)/shard_map/ppermute | solution.py:34
  37.7 7.5 %collective-permute-start.13 = (bf16[2,48,384]{2,1,0:T(8,128)(2,1)S(1)}, bf16[2,48,384]{2,1,0:T(8,128)(2,1)S(1)}, u32[]{:S(2)}, u32[]{:S(2)}) collective-permute-start(bf16[2,48,384]{2,1,0:T(8,128)(2,1)S(1)} %get-tuple-element.27), channel_id=1, source_target_pairs={{0,16},{4,52},{16,32},{20,4},{32,48},{36,20},{48,0},{52,36},{1,17}... | collective-permute-start | bytes 221192 | tf_op jit(solution)/shard_map/ppermute | solution.py:55
  38.9 7.2 %collective-permute-start.15 = (bf16[2,48,384]{2,1,0:T(8,128)(2,1)S(1)}, bf16[2,48,384]{2,1,0:T(8,128)(2,1)S(1)}, u32[]{:S(2)}, u32[]{:S(2)}) collective-permute-start(bf16[2,48,384]{2,1,0:T(8,128)(2,1)S(1)} %get-tuple-element.28), channel_id=1, source_target_pairs={{0,48},{4,20},{16,0},{20,36},{32,16},{36,52},{48,32},{52,4},{1,49}... | collective-permute-start | bytes 221192 | tf_op jit(solution)/shard_map/ppermute | solution.py:55
  41.3 7.3 %collective-permute-start.12 = (bf16[2,48,384]{2,1,0:T(8,128)(2,1)S(1)}, bf16[2,48,384]{2,1,0:T(8,128)(2,1)S(1)}, u32[]{:S(2)}, u32[]{:S(2)}) collective-permute-start(bf16[2,48,384]{2,1,0:T(8,128)(2,1)S(1)} %get-tuple-element.26.after.refs_2_), channel_id=1, source_target_pairs={{0,8},{8,0},{1,9},{9,1},{2,10},{10,2},{3,11},{11,3},{4,12},{12,4},... | collective-permute-start | bytes 221192 | tf_op jit(solution)/shard_map/ppermute | solution.py:34
  45.2 5.5 %collective-permute-start.14 = (bf16[2,48,384]{2,1,0:T(8,128)(2,1)S(1)}, bf16[2,48,384]{2,1,0:T(8,128)(2,1)S(1)}, u32[]{:S(2)}, u32[]{:S(2)}) collective-permute-start(bf16[2,48,384]{2,1,0:T(8,128)(2,1)S(1)} %collective-permute-done.13.refs_4_), channel_id=1, source_target_pairs={{0,8},{8,0},{1,9},{9,1},{2,10},{10,2},{3,11},{11,3},{4,12},{12,4},... | collective-permute-start | bytes 221192 | tf_op jit(solution)/shard_map/ppermute | solution.py:34
  46.1 4.7 %collective-permute-start.16 = (bf16[2,48,384]{2,1,0:T(8,128)(2,1)S(1)}, bf16[2,48,384]{2,1,0:T(8,128)(2,1)S(1)}, u32[]{:S(2)}, u32[]{:S(2)}) collective-permute-start(bf16[2,48,384]{2,1,0:T(8,128)(2,1)S(1)} %collective-permute-done.15.refs_6_), channel_id=1, source_target_pairs={{0,8},{8,0},{1,9},{9,1},{2,10},{10,2},{3,11},{11,3},{4,12},{12,4},... | collective-permute-start | bytes 221192 | tf_op jit(solution)/shard_map/ppermute | solution.py:34
  46.1 18.1 %collective-permute-start.8 = (bf16[200,768]{1,0:T(8,128)(2,1)S(1)}, bf16[200,768]{1,0:T(8,128)(2,1)S(1)}, u32[]{:S(2)}, u32[]{:S(2)}) collective-permute-start(bf16[200,768]{1,0:T(8,128)(2,1)S(1)} %arrange_tiles.1.refs_0_), channel_id=1, source_target_pairs={{0,36},{4,32},{16,52},{20,48},{32,4},{36,0},{48,20},{52,16},{1,37}... | collective-permute-start | bytes 921608 | tf_op jit(solution)/shard_map/ppermute | solution.py:46
  48.6 15.7 %collective-permute-start.7 = (bf16[2,48,384]{2,1,0:T(8,128)(2,1)S(1)}, bf16[2,48,384]{2,1,0:T(8,128)(2,1)S(1)}, u32[]{:S(2)}, u32[]{:S(2)}) collective-permute-start(bf16[2,48,384]{2,1,0:T(8,128)(2,1)S(1)} %get-tuple-element.25), channel_id=1, source_target_pairs={{0,32},{4,36},{16,48},{20,52},{32,0},{36,4},{48,16},{52,20},{1,33}... | collective-permute-start | bytes 221192 | tf_op jit(solution)/shard_map/ppermute | solution.py:55
  64.2 1.8 %collective-permute-start.17 = (bf16[200,768]{1,0:T(8,128)(2,1)S(1)}, bf16[200,768]{1,0:T(8,128)(2,1)S(1)}, u32[]{:S(2)}, u32[]{:S(2)}) collective-permute-start(bf16[200,768]{1,0:T(8,128)(2,1)S(1)} %collective-permute-done.8.refs_0_), channel_id=1, source_target_pairs={{0,8},{8,0},{1,9},{9,1},{2,10},{10,2},{3,11},{11,3},{4,12},{12,4},... | collective-permute-start | bytes 921608 | tf_op jit(solution)/shard_map/ppermute | solution.py:34
  64.7 1.3 %collective-permute-start.18 = (bf16[2,48,384]{2,1,0:T(8,128)(2,1)S(1)}, bf16[2,48,384]{2,1,0:T(8,128)(2,1)S(1)}, u32[]{:S(2)}, u32[]{:S(2)}) collective-permute-start(bf16[2,48,384]{2,1,0:T(8,128)(2,1)S(1)} %collective-permute-done.7.refs_2_), channel_id=1, source_target_pairs={{0,8},{8,0},{1,9},{9,1},{2,10},{10,2},{3,11},{11,3},{4,12},{12,4},... | collective-permute-start | bytes 221192 | tf_op jit(solution)/shard_map/ppermute | solution.py:34
  68.8 9.9 %collective-permute-start.19 = (bf16[384,384]{1,0:T(8,128)(2,1)S(1)}, bf16[384,384]{1,0:T(8,128)(2,1)S(1)}, u32[]{:S(2)}, u32[]{:S(2)}) collective-permute-start(bf16[384,384]{1,0:T(8,128)(2,1)S(1)} %get-tuple-element.34), channel_id=1, source_target_pairs={{0,128},{64,192},{128,0},{192,64},{1,129},{65,193},{129,1},{193,65... | collective-permute-start | bytes 884744 | tf_op jit(solution)/shard_map/ppermute | solution.py:38
  71.8 13.8 %collective-permute-start.20 = (bf16[384,384]{1,0:T(8,128)(2,1)S(1)}, bf16[384,384]{1,0:T(8,128)(2,1)S(1)}, u32[]{:S(2)}, u32[]{:S(2)}) collective-permute-start(bf16[384,384]{1,0:T(8,128)(2,1)S(1)} %get-tuple-element.36), channel_id=1, source_target_pairs={{0,64},{64,128},{128,192},{192,0},{1,65},{65,129},{129,193},{193,1... | collective-permute-start | bytes 884744 | tf_op jit(solution)/shard_map/ppermute | solution.py:38
  72.2 13.4 %collective-permute-start.21 = (bf16[384,384]{1,0:T(8,128)(2,1)S(1)}, bf16[384,384]{1,0:T(8,128)(2,1)S(1)}, u32[]{:S(2)}, u32[]{:S(2)}) collective-permute-start(bf16[384,384]{1,0:T(8,128)(2,1)S(1)} %get-tuple-element.37), channel_id=1, source_target_pairs={{0,192},{64,0},{128,64},{192,128},{1,193},{65,1},{129,65},{193,129... | collective-permute-start | bytes 884744 | tf_op jit(solution)/shard_map/ppermute | solution.py:38
  87.5 23.6 %copy-start.3 = (f32[8,24,768]{2,1,0:T(8,128)S(1)}, f32[8,24,768]{2,1,0:T(8,128)}, u32[]{:S(2)}) copy-start(f32[8,24,768]{2,1,0:T(8,128)} %param.14) | copy-start | bytes 1769476
  87.5 23.6 %all-to-all-start = ((bf16[32,24,192]{2,1,0:T(8,128)(2,1)}), bf16[32,24,192]{2,1,0:T(8,128)(2,1)S(1)}, u32[]{:S(2)}, u32[]{:S(2)}) async-start(bf16[32,24,192]{2,1,0:T(8,128)(2,1)} %get-tuple-element.44), calls=%async_computation | async-start | bytes 786432 | tf_op jit(solution)/shard_map/all_to_all | solution.py:416
  97.4 1.9 %collective-permute-start.22 = (bf16[4,48,384]{2,1,0:T(8,128)(2,1)S(1)}, bf16[4,48,384]{2,1,0:T(8,128)(2,1)S(1)}, u32[]{:S(2)}, u32[]{:S(2)}) collective-permute-start(bf16[4,48,384]{2,1,0:T(8,128)(2,1)S(1)} %get-tuple-element.39), channel_id=1, source_target_pairs={{0,8},{8,0},{1,9},{9,1},{2,10},{10,2},{3,11},{11,3},{4,12},{12,4},... | collective-permute-start | bytes 442376 | tf_op jit(solution)/shard_map/ppermute | solution.py:34
  99.7 9.2 %collective-permute-start.23 = (bf16[2,48,384]{2,1,0:T(8,128)(2,1)S(1)}, bf16[2,48,384]{2,1,0:T(8,128)(2,1)S(1)}, u32[]{:S(2)}, u32[]{:S(2)}) collective-permute-start(bf16[2,48,384]{2,1,0:T(8,128)(2,1)S(1)} %get-tuple-element.40), channel_id=1, source_target_pairs={{0,32},{4,36},{16,48},{20,52},{32,0},{36,4},{48,16},{52,20},{1,33}... | collective-permute-start | bytes 221192 | tf_op jit(solution)/shard_map/ppermute | solution.py:55
  101.8 7.1 %collective-permute-start.24 = (bf16[2,48,384]{2,1,0:T(8,128)(2,1)S(1)}, bf16[2,48,384]{2,1,0:T(8,128)(2,1)S(1)}, u32[]{:S(2)}, u32[]{:S(2)}) collective-permute-start(bf16[2,48,384]{2,1,0:T(8,128)(2,1)S(1)} %get-tuple-element.42), channel_id=1, source_target_pairs={{0,16},{4,52},{16,32},{20,4},{32,48},{36,20},{48,0},{52,36},{1,17}... | collective-permute-start | bytes 221192 | tf_op jit(solution)/shard_map/ppermute | solution.py:55
  102.6 8.5 %collective-permute-start.25 = (bf16[2,48,384]{2,1,0:T(8,128)(2,1)S(1)}, bf16[2,48,384]{2,1,0:T(8,128)(2,1)S(1)}, u32[]{:S(2)}, u32[]{:S(2)}) collective-permute-start(bf16[2,48,384]{2,1,0:T(8,128)(2,1)S(1)} %get-tuple-element.43), channel_id=1, source_target_pairs={{0,48},{4,20},{16,0},{20,36},{32,16},{36,52},{48,32},{52,4},{1,49}... | collective-permute-start | bytes 221192 | tf_op jit(solution)/shard_map/ppermute | solution.py:55

commit v5 on v4

--- a/solution.py
+++ b/solution.py
@@ -230,8 +230,8 @@
 
 
 def first_kernel(place, *refs):
-    ps, xs, acc, done = refs[:2], refs[2 : 2 + FIRST], refs[2 + FIRST], refs[3 + FIRST]
-    add_products((0, FIRST), place, ps, xs, acc, *refs[4 + FIRST :], fresh=True)
+    ps, xs, acc, done = refs[:2], refs[2 : 2 + FIRST], refs[3 + FIRST], refs[4 + FIRST]
+    add_products((0, FIRST), place, ps, xs, acc, *refs[5 + FIRST :], fresh=True)
     done[...] = jnp.zeros_like(done)
 
 
@@ -382,13 +382,13 @@
     acc, done = pl.pallas_call(
         first_kernel,
         out_shape=[total, jax.ShapeDtypeStruct((8, 128), F32)],
-        in_specs=[SM] + [HBM] * (2 + FIRST),
+        in_specs=[SM] + [HBM] * (3 + FIRST),
         out_specs=[VM] * 2,
         scratch_shapes=product_scratch(FIRST),
         compiler_params=params(16),
         cost_estimate=cost(6),
         name="alpha_product_first",
-    )(y.reshape(1), *a_pair, *by_label)
+    )(y.reshape(1), *a_pair, *by_label, a_far)
     farthest, a_far, done = lax.optimization_barrier((direct[3], a_far, done))
     _, own, s1, s2, s3 = pl.pallas_call(
         last_kernel,

time: 113 us -> 115 us (1.018)
    ppermute x7, waiting for transfers between devices: 8.64 us -> 16.5 us  [send_step(): return lax.ppermute(a, ('zh', 'zl'), moves)]
    ppermute x2, waiting for transfers between devices: 7.24 us -> 0.01 us  [cross_z(): return lax.ppermute(a, ('zh', 'zl'), moves)]
    ppermute x7, starting transfers between devices: 12.7 us -> 16.9 us  [send_step(): return lax.ppermute(a, ('zh', 'zl'), moves)]
    all_to_all x1, starting transfers between devices: 9.85 us -> 6.74 us  [per_device(): lax.all_to_all(y_out[NC], ('y', 'zl', 'x'), split_axis=0, concat_axis=0,...]
    ppermute x2, starting transfers between devices: 7.22 us -> 5.88 us  [cross_z(): return lax.ppermute(a, ('zh', 'zl'), moves)]
    ppermute x7, starting transfers between devices: 6.24 us -> 7.54 us  [flip_core(): return lax.ppermute(a, 'core', [(0, 1), (1, 0)])]
  transfers between devices with their start and end apart: 27 -> 27, of which waited for: 10 -> 11; matrix products, arithmetic and copies ran while one was open for 1% -> 1% of each run, Pallas kernels for 10% -> 9%
where the time goes in v5:
time: 115 us
  starting transfers between devices  52.1 us (45%)
  waiting for transfers between devices  40.2 us (35%)
  Pallas kernels  17.6 us (15%)
  local copies, waits for them, and re-layouts  3.49 us (3%)
    ppermute x7, starting transfers between devices, send_step(): return lax.ppermute(a, ('zh', 'zl'), moves)  16.9 us
    ppermute x7, waiting for transfers between devices, send_step(): return lax.ppermute(a, ('zh', 'zl'), moves)  16.5 us
    ppermute x3, waiting for transfers between devices, shift_y(): return lax.ppermute(a, 'y', [(i, (i + k) % NY) for i in range(NY)])  11.2 us
    ppermute x6, waiting for transfers between devices, shift_x(): return lax.ppermute(a, 'x', [(i, (i + k) % NX) for i in range(NX)])  10.3 us
    ppermute x7, starting transfers between devices, flip_core(): return lax.ppermute(a, 'core', [(0, 1), (1, 0)])  7.54 us
    ppermute x6, starting transfers between devices, shift_x(): return lax.ppermute(a, 'x', [(i, (i + k) % NX) for i in range(NX)])  6.82 us
    all_to_all x1, starting transfers between devices, per_device(): lax.all_to_all(y_out[NC], ('y', 'zl', 'x'), split_axis=0, concat_axis=0,...  6.74 us
    pallas_call x1, Pallas kernels, per_device(): pl.pallas_call(first_kernel, out_shape=[total, jax.ShapeDtypeStruct((8, 1...  6.24 us
  transfers between devices with their start and end apart: 27, of which 11 were waited for; matrix products, arithmetic and copies ran while one was open for 1% of the time, Pallas kernels for 9%

profile of v5, /device:TPU:1, one launch (start us, length us, event | category | flops | bytes accessed | tf_op | source)
XLA Modules:
  0.0 114.7 jit_solution(7908936375965602354)
XLA Ops:
  0.0 2.6 %collective-permute-start = (bf16[192,768]{1,0:T(8,128)(2,1)}, bf16[192,768]{1,0:T(8,128)(2,1)S(1)}, u32[]{:S(2)}, u32[]{:S(2)}) collective-permute-start(bf16[192,768]{1,0:T(8,128)(2,1)} %bitcast.17), channel_id=1, source_target_pairs={{0,4},{4,0},{1,5},{5,1},{2,6},{6,2},{3,7},{7,3},{8,12},{12,8},{9,1... | collective-permute-start | bytes 884744 | tf_op jit(solution)/shard_map/ppermute | solution.py:30
  2.6 1.2 %collective-permute-start.4 = (bf16[192,768]{1,0:T(8,128)(2,1)}, bf16[192,768]{1,0:T(8,128)(2,1)S(1)}, u32[]{:S(2)}, u32[]{:S(2)}) collective-permute-start(bf16[192,768]{1,0:T(8,128)(2,1)} %bitcast.18), channel_id=1, source_target_pairs={{0,1},{1,2},{2,3},{3,0},{4,5},{5,6},{6,7},{7,4},{8,9},{9,10},{10,1... | collective-permute-start | bytes 884744 | tf_op jit(solution)/shard_map/ppermute | solution.py:26
  3.8 1.5 %collective-permute-start.6 = (bf16[192,768]{1,0:T(8,128)(2,1)}, bf16[192,768]{1,0:T(8,128)(2,1)S(1)}, u32[]{:S(2)}, u32[]{:S(2)}) collective-permute-start(bf16[192,768]{1,0:T(8,128)(2,1)} %bitcast.19), channel_id=1, source_target_pairs={{0,3},{1,0},{2,1},{3,2},{4,7},{5,4},{6,5},{7,6},{8,11},{9,8},{10,9... | collective-permute-start | bytes 884744 | tf_op jit(solution)/shard_map/ppermute | solution.py:26
  5.2 1.3 %copy-done = bf16[1,8,1,32,24,24]{3,5,4,2,1,0:T(8,128)(2,1)S(1)} copy-done((bf16[1,8,1,32,24,24]{3,5,4,2,1,0:T(8,128)(2,1)S(1)}, bf16[1,8,1,32,24,24]{3,5,4,2,1,0:T(8,128)(2,1)}, u32[]{:S(2)}) %copy-start) | copy-done | bytes 294936
  6.5 1.3 %copy-done.2 = bf16[768,768]{1,0:T(8,128)(2,1)S(1)} copy-done((bf16[768,768]{1,0:T(8,128)(2,1)S(1)}, bf16[768,768]{1,0:T(8,128)(2,1)}, u32[]{:S(2)}) %copy-start.2) | copy-done | bytes 1179672
  7.8 0.7 copy-done.4
  8.5 0.7 arrange_tiles.1.refs_0_
  9.2 4.7 %collective-permute-start.9 = (bf16[200,768]{1,0:T(8,128)(2,1)S(1)}, bf16[200,768]{1,0:T(8,128)(2,1)S(1)}, u32[]{:S(2)}, u32[]{:S(2)}) collective-permute-start(bf16[200,768]{1,0:T(8,128)(2,1)S(1)} %arrange_tiles.1.refs_0_), channel_id=1, source_target_pairs={{0,52},{4,16},{16,4},{20,32},{32,20},{36,48},{48,36},{52,0},{1,53}... | collective-permute-start | bytes 921608 | tf_op jit(solution)/shard_map/ppermute | solution.py:46
  14.0 1.2 %collective-permute-start.10 = (bf16[200,768]{1,0:T(8,128)(2,1)S(1)}, bf16[200,768]{1,0:T(8,128)(2,1)S(1)}, u32[]{:S(2)}, u32[]{:S(2)}) collective-permute-start(bf16[200,768]{1,0:T(8,128)(2,1)S(1)} %arrange_tiles.1.refs_0_), channel_id=1, source_target_pairs={{0,48},{4,20},{16,0},{20,36},{32,16},{36,52},{48,32},{52,4},{1,49}... | collective-permute-start | bytes 921608 | tf_op jit(solution)/shard_map/ppermute | solution.py:55
  15.2 0.1 rem.118
  15.3 0.1 div.33
  15.4 0.1 ne.108
  15.5 0.0 collective-permute-done.refs_0_
  15.5 1.3 %collective-permute-start.1 = (bf16[192,768]{1,0:T(8,128)(2,1)S(1)}, bf16[192,768]{1,0:T(8,128)(2,1)S(1)}, u32[]{:S(2)}, u32[]{:S(2)}) collective-permute-start(bf16[192,768]{1,0:T(8,128)(2,1)S(1)} %collective-permute-done.refs_0_), channel_id=1, source_target_pairs={{0,3},{1,0},{2,1},{3,2},{4,7},{5,4},{6,5},{7,6},{8,11},{9,8},{10,9... | collective-permute-start | bytes 884744 | tf_op jit(solution)/shard_map/ppermute | solution.py:26
  16.9 0.1 broadcast_add_fusion
  16.9 0.0 collective-permute-done.4.refs_4_
  16.9 0.2 collective-permute-start.3
  17.2 0.0 collective-permute-done.6.refs_6_
  17.2 0.1 collective-permute-start.5
  17.3 4.7 %collective-permute-done.1.refs_2_ = bf16[192,768]{1,0:T(8,128)(2,1)S(1)} collective-permute-done((bf16[192,768]{1,0:T(8,128)(2,1)S(1)}, bf16[192,768]{1,0:T(8,128)(2,1)S(1)}, u32[]{:S(2)}, u32[]{:S(2)}) %collective-permute-start.1) | collective-permute-done | bytes 294944 | tf_op jit(solution)/shard_map/ppermute | solution.py:26
  22.0 2.5 %collective-permute-start.2 = (bf16[192,768]{1,0:T(8,128)(2,1)S(1)}, bf16[192,768]{1,0:T(8,128)(2,1)S(1)}, u32[]{:S(2)}, u32[]{:S(2)}) collective-permute-start(bf16[192,768]{1,0:T(8,128)(2,1)S(1)} %collective-permute-done.1.refs_2_), channel_id=1, source_target_pairs={{0,3},{1,0},{2,1},{3,2},{4,7},{5,4},{6,5},{7,6},{8,11},{9,8},{10,9... | collective-permute-start | bytes 884744 | tf_op jit(solution)/shard_map/ppermute | solution.py:26
  24.5 0.6 fusion.refs_9_
  25.1 5.5 %collective-permute-done.5.refs_5_ = bf16[192,768]{1,0:T(8,128)(2,1)S(1)} collective-permute-done((bf16[192,768]{1,0:T(8,128)(2,1)S(1)}, bf16[192,768]{1,0:T(8,128)(2,1)S(1)}, u32[]{:S(2)}, u32[]{:S(2)}) %collective-permute-start.5) | collective-permute-done | bytes 294944 | tf_op jit(solution)/shard_map/ppermute | solution.py:26
  30.6 0.0 collective-permute-done.2.refs_1_
  30.6 3.4 %beta_product.1 = (bf16[2,48,384]{2,1,0:T(8,128)(2,1)S(1)}, bf16[2,48,384]{2,1,0:T(8,128)(2,1)S(1)}, bf16[2,48,384]{2,1,0:T(8,128)(2,1)S(1)}, bf16[2,48,384]{2,1,0:T(8,128)(2,1)S(1)}) custom-call(s32[36]{0:T(128)S(1)} %fusion.5.slots, bf16[192,768]{1,0:T(8,128)(2,1)S(1)} %collective-permute-done.refs_0_, ...), custom_call_target="tpu_custom_call" | custom-call | tf_op jit(solution)/shard_map/beta_product/pallas_call | solution.py:352
  34.0 0.0 collective-permute-done.9.refs_1_
  34.1 0.0 collective-permute-done.10.refs_2_
  34.1 0.3 stack_tiles.1.refs_0_
  34.3 3.4 %collective-permute-start.11 = (bf16[3,200,768]{2,1,0:T(8,128)(2,1)S(1)}, bf16[3,200,768]{2,1,0:T(8,128)(2,1)S(1)}, u32[]{:S(2)}, u32[]{:S(2)}) collective-permute-start(bf16[3,200,768]{2,1,0:T(8,128)(2,1)S(1)} %stack_tiles.1.refs_0_), channel_id=1, source_target_pairs={{0,8},{8,0},{1,9},{9,1},{2,10},{10,2},{3,11},{11,3},{4,12},{12,4},... | collective-permute-start | bytes 2764808 | tf_op jit(solution)/shard_map/ppermute | solution.py:34
  37.7 1.1 collective-permute-start.8
  38.8 1.2 %collective-permute-start.13 = (bf16[2,48,384]{2,1,0:T(8,128)(2,1)S(1)}, bf16[2,48,384]{2,1,0:T(8,128)(2,1)S(1)}, u32[]{:S(2)}, u32[]{:S(2)}) collective-permute-start(bf16[2,48,384]{2,1,0:T(8,128)(2,1)S(1)} %get-tuple-element.27), channel_id=1, source_target_pairs={{0,16},{4,52},{16,32},{20,4},{32,48},{36,20},{48,0},{52,36},{1,17}... | collective-permute-start | bytes 221192 | tf_op jit(solution)/shard_map/ppermute | solution.py:55
  40.0 2.4 %collective-permute-start.15 = (bf16[2,48,384]{2,1,0:T(8,128)(2,1)S(1)}, bf16[2,48,384]{2,1,0:T(8,128)(2,1)S(1)}, u32[]{:S(2)}, u32[]{:S(2)}) collective-permute-start(bf16[2,48,384]{2,1,0:T(8,128)(2,1)S(1)} %get-tuple-element.28), channel_id=1, source_target_pairs={{0,48},{4,20},{16,0},{20,36},{32,16},{36,52},{48,32},{52,4},{1,49}... | collective-permute-start | bytes 221192 | tf_op jit(solution)/shard_map/ppermute | solution.py:55
  42.4 0.9 collective-permute-start.12
  43.3 1.9 %collective-permute-done.13.refs_4_ = bf16[2,48,384]{2,1,0:T(8,128)(2,1)S(1)} collective-permute-done((bf16[2,48,384]{2,1,0:T(8,128)(2,1)S(1)}, bf16[2,48,384]{2,1,0:T(8,128)(2,1)S(1)}, u32[]{:S(2)}, u32[]{:S(2)}) %collective-permute-start.13) | collective-permute-done | bytes 73760 | tf_op jit(solution)/shard_map/ppermute | solution.py:55
  45.2 0.9 collective-permute-start.14
  46.2 9.0 %collective-permute-done.15.refs_6_ = bf16[2,48,384]{2,1,0:T(8,128)(2,1)S(1)} collective-permute-done((bf16[2,48,384]{2,1,0:T(8,128)(2,1)S(1)}, bf16[2,48,384]{2,1,0:T(8,128)(2,1)S(1)}, u32[]{:S(2)}, u32[]{:S(2)}) %collective-permute-start.15) | collective-permute-done | bytes 73760 | tf_op jit(solution)/shard_map/ppermute | solution.py:55
  55.2 0.9 collective-permute-start.16
  56.1 5.7 %collective-permute-start.7 = (bf16[2,48,384]{2,1,0:T(8,128)(2,1)S(1)}, bf16[2,48,384]{2,1,0:T(8,128)(2,1)S(1)}, u32[]{:S(2)}, u32[]{:S(2)}) collective-permute-start(bf16[2,48,384]{2,1,0:T(8,128)(2,1)S(1)} %get-tuple-element.25), channel_id=1, source_target_pairs={{0,32},{4,36},{16,48},{20,52},{32,0},{36,4},{48,16},{52,20},{1,33}... | collective-permute-start | bytes 221192 | tf_op jit(solution)/shard_map/ppermute | solution.py:55
  61.8 0.0 collective-permute-done.12.refs_3_
  61.8 0.0 collective-permute-done.14.refs_5_
  61.8 0.0 collective-permute-done.16.refs_7_
  61.8 6.2 %alpha_product_first.1 = (f32[6144,128]{1,0:T(8,128)S(1)}, f32[8,128]{1,0:T(8,128)S(1)}) custom-call(s32[1]{0:T(128)} %bitcast.place, bf16[3,200,768]{2,1,0:T(8,128)(2,1)S(1)} %stack_tiles.1.refs_0_, bf16[3,200,768]{2,1,0:T(8,128)(2,1)S(1)} %collective-permute-done.11.refs_1_, bf16[2,48,384]{2,1,0:T(8,128)(2,1)S(1)} %get-tuple-element.26.after.refs_2_, ...), custom_call_target="tpu_custom_call" | custom-call | flops 6899999744 | bytes 1048576 | tf_op jit(solution)/shard_map/alpha_product_first/pallas_call | solution.py:382
  68.1 0.4 collective-permute-start.17
  68.5 0.2 collective-permute-start.18
  68.7 1.2 %collective-permute-done.18.refs_3_ = bf16[2,48,384]{2,1,0:T(8,128)(2,1)S(1)} collective-permute-done((bf16[2,48,384]{2,1,0:T(8,128)(2,1)S(1)}, bf16[2,48,384]{2,1,0:T(8,128)(2,1)S(1)}, u32[]{:S(2)}, u32[]{:S(2)}) %collective-permute-start.18) | collective-permute-done | bytes 73760 | tf_op jit(solution)/shard_map/ppermute | solution.py:34
  69.9 2.7 %alpha_product_last.1 = (f32[6144,128]{1,0:T(8,128)S(1)}, f32[1536,128]{1,0:T(8,128)S(1)}, bf16[384,384]{1,0:T(8,128)(2,1)S(1)}, bf16[384,384]{1,0:T(8,128)(2,1)S(1)}, bf16[384,384]{1,0:T(8,128)(2,1)S(1)}) custom-call(s32[1]{0:T(128)} %bitcast.place, bf16[200,768]{1,0:T(8,128)(2,1)S(1)} %collective-permute-done.8.refs_8_.refs_0_, ...), custom_call_target="tpu_custom_call", output_to_operand_aliasing={{0}: (5, {})} | custom-call | tf_op jit(solution)/shard_map/alpha_product_last/pallas_call | solution.py:393
  72.6 3.0 %collective-permute-start.19 = (bf16[384,384]{1,0:T(8,128)(2,1)S(1)}, bf16[384,384]{1,0:T(8,128)(2,1)S(1)}, u32[]{:S(2)}, u32[]{:S(2)}) collective-permute-start(bf16[384,384]{1,0:T(8,128)(2,1)S(1)} %get-tuple-element.34), channel_id=1, source_target_pairs={{0,128},{64,192},{128,0},{192,64},{1,129},{65,193},{129,1},{193,65... | collective-permute-start | bytes 884744 | tf_op jit(solution)/shard_map/ppermute | solution.py:38
  75.6 0.4 collective-permute-start.20
  76.0 2.3 %collective-permute-start.21 = (bf16[384,384]{1,0:T(8,128)(2,1)S(1)}, bf16[384,384]{1,0:T(8,128)(2,1)S(1)}, u32[]{:S(2)}, u32[]{:S(2)}) collective-permute-start(bf16[384,384]{1,0:T(8,128)(2,1)S(1)} %get-tuple-element.37), channel_id=1, source_target_pairs={{0,192},{64,0},{128,64},{192,128},{1,193},{65,1},{129,65},{193,129... | collective-permute-start | bytes 884744 | tf_op jit(solution)/shard_map/ppermute | solution.py:38
  78.3 4.3 %collective-permute-done.19.r2 = bf16[384,384]{1,0:T(8,128)(2,1)S(1)} collective-permute-done((bf16[384,384]{1,0:T(8,128)(2,1)S(1)}, bf16[384,384]{1,0:T(8,128)(2,1)S(1)}, u32[]{:S(2)}, u32[]{:S(2)}) %collective-permute-start.19) | collective-permute-done | bytes 294944 | tf_op jit(solution)/shard_map/ppermute | solution.py:38
  82.6 6.9 %collective-permute-done.20.r1 = bf16[384,384]{1,0:T(8,128)(2,1)S(1)} collective-permute-done((bf16[384,384]{1,0:T(8,128)(2,1)S(1)}, bf16[384,384]{1,0:T(8,128)(2,1)S(1)}, u32[]{:S(2)}, u32[]{:S(2)}) %collective-permute-start.20) | collective-permute-done | bytes 294944 | tf_op jit(solution)/shard_map/ppermute | solution.py:38
  89.5 1.9 %y_sum.1 = (bf16[4,48,384]{2,1,0:T(8,128)(2,1)S(1)}, bf16[4,48,384]{2,1,0:T(8,128)(2,1)S(1)}, bf16[32,24,192]{2,1,0:T(8,128)(2,1)}) custom-call(s32[8]{0:T(128)S(1)} %get-tuple-element.48.dests, bf16[384,384]{1,0:T(8,128)(2,1)S(1)} %collective-permute-done.19.r2, f32[1536,128]{1,0:T(8,128)S(1)} %get-tuple-element.35.own, ...), custom_call_target="tpu_custom_call" | custom-call | tf_op jit(solution)/shard_map/y_sum/pallas_call | solution.py:405
  91.4 6.7 %all-to-all-start = ((bf16[32,24,192]{2,1,0:T(8,128)(2,1)}), bf16[32,24,192]{2,1,0:T(8,128)(2,1)S(1)}, u32[]{:S(2)}, u32[]{:S(2)}) async-start(bf16[32,24,192]{2,1,0:T(8,128)(2,1)} %get-tuple-element.44), calls=%async_computation | async-start | bytes 786432 | tf_op jit(solution)/shard_map/all_to_all | solution.py:416
  98.1 0.9 collective-permute-start.22
  99.0 1.0 collective-permute-done.22.came
  100.0 0.4 pair_pieces.1
  100.4 2.8 %collective-permute-start.23 = (bf16[2,48,384]{2,1,0:T(8,128)(2,1)S(1)}, bf16[2,48,384]{2,1,0:T(8,128)(2,1)S(1)}, u32[]{:S(2)}, u32[]{:S(2)}) collective-permute-start(bf16[2,48,384]{2,1,0:T(8,128)(2,1)S(1)} %get-tuple-element.40), channel_id=1, source_target_pairs={{0,32},{4,36},{16,48},{20,52},{32,0},{36,4},{48,16},{52,20},{1,33}... | collective-permute-start | bytes 221192 | tf_op jit(solution)/shard_map/ppermute | solution.py:55
  103.3 0.7 collective-permute-start.24
  104.0 2.9 %collective-permute-start.25 = (bf16[2,48,384]{2,1,0:T(8,128)(2,1)S(1)}, bf16[2,48,384]{2,1,0:T(8,128)(2,1)S(1)}, u32[]{:S(2)}, u32[]{:S(2)}) collective-permute-start(bf16[2,48,384]{2,1,0:T(8,128)(2,1)S(1)} %get-tuple-element.43), channel_id=1, source_target_pairs={{0,48},{4,20},{16,0},{20,36},{32,16},{36,52},{48,32},{52,4},{1,49}... | collective-permute-start | bytes 221192 | tf_op jit(solution)/shard_map/ppermute | solution.py:55
  106.8 0.3 fusion.1.refs_5_
  107.2 0.8 collective-permute-done.23.refs_0_
  107.9 1.3 %collective-permute-done.24.refs_2_ = bf16[2,48,384]{2,1,0:T(8,128)(2,1)S(1)} collective-permute-done((bf16[2,48,384]{2,1,0:T(8,128)(2,1)S(1)}, bf16[2,48,384]{2,1,0:T(8,128)(2,1)S(1)}, u32[]{:S(2)}, u32[]{:S(2)}) %collective-permute-start.24) | collective-permute-done | bytes 73760 | tf_op jit(solution)/shard_map/ppermute | solution.py:55
  109.2 3.5 %collective-permute-done.25.refs_3_ = bf16[2,48,384]{2,1,0:T(8,128)(2,1)S(1)} collective-permute-done((bf16[2,48,384]{2,1,0:T(8,128)(2,1)S(1)}, bf16[2,48,384]{2,1,0:T(8,128)(2,1)S(1)}, u32[]{:S(2)}, u32[]{:S(2)}) %collective-permute-start.25) | collective-permute-done | bytes 73760 | tf_op jit(solution)/shard_map/ppermute | solution.py:55
  112.7 1.9 %combine.1 = f32[192,768]{1,0:T(8,128)} custom-call(bf16[2,48,384]{2,1,0:T(8,128)(2,1)S(1)} %collective-permute-done.23.refs_0_, bf16[2,48,384]{2,1,0:T(8,128)(2,1)S(1)} %get-tuple-element.41.refs_1_, bf16[2,48,384]{2,1,0:T(8,128)(2,1)S(1)} %collective-permute-done.24.refs_2_, bf16[2,48,384]{2,1,0:T(8,128)(2,1)S(1)} %collective-permute-done.25.refs_3_, ...), custom_call_target="tpu_custom_call" | custom-call | tf_op jit(solution)/shard_map/combine/pallas_call | solution.py:427
  (26 shorter events, 0.2 us)
Async XLA Ops:
  0.0 15.5 %copy-start.6 = (s32[8]{0:T(128)S(1)}, s32[8]{0:T(128)}, u32[]{:S(2)}) copy-start(s32[8]{0:T(128)} %constant.114.clone) | copy-start | bytes 100
  0.0 15.5 %copy-start.7 = (s32[8]{0:T(128)S(1)}, s32[8]{0:T(128)}, u32[]{:S(2)}) copy-start(s32[8]{0:T(128)} %constant.113.clone) | copy-start | bytes 100
  0.0 15.2 %copy-start.5 = (s32[1,6,6]{2,0,1:T(1,128)S(1)}, s32[1,6,6]{2,0,1:T(1,128)}, u32[]{:S(2)}) copy-start(s32[1,6,6]{2,0,1:T(1,128)} %param.11) | copy-start | bytes 436
  0.0 15.5 %collective-permute-start = (bf16[192,768]{1,0:T(8,128)(2,1)}, bf16[192,768]{1,0:T(8,128)(2,1)S(1)}, u32[]{:S(2)}, u32[]{:S(2)}) collective-permute-start(bf16[192,768]{1,0:T(8,128)(2,1)} %bitcast.17), channel_id=1, source_target_pairs={{0,4},{4,0},{1,5},{5,1},{2,6},{6,2},{3,7},{7,3},{8,12},{12,8},{9,1... | collective-permute-start | bytes 884744 | tf_op jit(solution)/shard_map/ppermute | solution.py:30
  2.6 14.4 %collective-permute-start.4 = (bf16[192,768]{1,0:T(8,128)(2,1)}, bf16[192,768]{1,0:T(8,128)(2,1)S(1)}, u32[]{:S(2)}, u32[]{:S(2)}) collective-permute-start(bf16[192,768]{1,0:T(8,128)(2,1)} %bitcast.18), channel_id=1, source_target_pairs={{0,1},{1,2},{2,3},{3,0},{4,5},{5,6},{6,7},{7,4},{8,9},{9,10},{10,1... | collective-permute-start | bytes 884744 | tf_op jit(solution)/shard_map/ppermute | solution.py:26
  3.8 13.4 %collective-permute-start.6 = (bf16[192,768]{1,0:T(8,128)(2,1)}, bf16[192,768]{1,0:T(8,128)(2,1)S(1)}, u32[]{:S(2)}, u32[]{:S(2)}) collective-permute-start(bf16[192,768]{1,0:T(8,128)(2,1)} %bitcast.19), channel_id=1, source_target_pairs={{0,3},{1,0},{2,1},{3,2},{4,7},{5,4},{6,5},{7,6},{8,11},{9,8},{10,9... | collective-permute-start | bytes 884744 | tf_op jit(solution)/shard_map/ppermute | solution.py:26
  5.2 1.3 %copy-start = (bf16[1,8,1,32,24,24]{3,5,4,2,1,0:T(8,128)(2,1)S(1)}, bf16[1,8,1,32,24,24]{3,5,4,2,1,0:T(8,128)(2,1)}, u32[]{:S(2)}) copy-start(bf16[1,8,1,32,24,24]{3,5,4,2,1,0:T(8,128)(2,1)} %param.12) | copy-start | bytes 884740
  6.5 1.3 %copy-start.2 = (bf16[768,768]{1,0:T(8,128)(2,1)S(1)}, bf16[768,768]{1,0:T(8,128)(2,1)}, u32[]{:S(2)}) copy-start(bf16[768,768]{1,0:T(8,128)(2,1)} %constant.115.clone.turn) | copy-start | bytes 3538948
  7.8 0.7 copy-start.4
  8.5 22.2 %copy-start.1 = (bf16[1,6,6,128,128]{4,3,2,1,0:T(8,128)(2,1)S(1)}, bf16[1,6,6,128,128]{4,3,2,1,0:T(8,128)(2,1)}, u32[]{:S(2)}) copy-start(bf16[1,6,6,128,128]{4,3,2,1,0:T(8,128)(2,1)} %param.10) | copy-start | bytes 3538948
  9.2 24.8 %collective-permute-start.9 = (bf16[200,768]{1,0:T(8,128)(2,1)S(1)}, bf16[200,768]{1,0:T(8,128)(2,1)S(1)}, u32[]{:S(2)}, u32[]{:S(2)}) collective-permute-start(bf16[200,768]{1,0:T(8,128)(2,1)S(1)} %arrange_tiles.1.refs_0_), channel_id=1, source_target_pairs={{0,52},{4,16},{16,4},{20,32},{32,20},{36,48},{48,36},{52,0},{1,53}... | collective-permute-start | bytes 921608 | tf_op jit(solution)/shard_map/ppermute | solution.py:46
  14.0 20.1 %collective-permute-start.10 = (bf16[200,768]{1,0:T(8,128)(2,1)S(1)}, bf16[200,768]{1,0:T(8,128)(2,1)S(1)}, u32[]{:S(2)}, u32[]{:S(2)}) collective-permute-start(bf16[200,768]{1,0:T(8,128)(2,1)S(1)} %arrange_tiles.1.refs_0_), channel_id=1, source_target_pairs={{0,48},{4,20},{16,0},{20,36},{32,16},{36,52},{48,32},{52,4},{1,49}... | collective-permute-start | bytes 921608 | tf_op jit(solution)/shard_map/ppermute | solution.py:55
  15.5 6.5 %collective-permute-start.1 = (bf16[192,768]{1,0:T(8,128)(2,1)S(1)}, bf16[192,768]{1,0:T(8,128)(2,1)S(1)}, u32[]{:S(2)}, u32[]{:S(2)}) collective-permute-start(bf16[192,768]{1,0:T(8,128)(2,1)S(1)} %collective-permute-done.refs_0_), channel_id=1, source_target_pairs={{0,3},{1,0},{2,1},{3,2},{4,7},{5,4},{6,5},{7,6},{8,11},{9,8},{10,9... | collective-permute-start | bytes 884744 | tf_op jit(solution)/shard_map/ppermute | solution.py:26
  16.9 8.2 %collective-permute-start.3 = (bf16[192,768]{1,0:T(8,128)(2,1)S(1)}, bf16[192,768]{1,0:T(8,128)(2,1)S(1)}, u32[]{:S(2)}, u32[]{:S(2)}) collective-permute-start(bf16[192,768]{1,0:T(8,128)(2,1)S(1)} %collective-permute-done.refs_0_), channel_id=1, source_target_pairs={{0,1},{1,2},{2,3},{3,0},{4,5},{5,6},{6,7},{7,4},{8,9},{9,10},{10,1... | collective-permute-start | bytes 884744 | tf_op jit(solution)/shard_map/ppermute | solution.py:26
  17.2 13.5 %collective-permute-start.5 = (bf16[192,768]{1,0:T(8,128)(2,1)S(1)}, bf16[192,768]{1,0:T(8,128)(2,1)S(1)}, u32[]{:S(2)}, u32[]{:S(2)}) collective-permute-start(bf16[192,768]{1,0:T(8,128)(2,1)S(1)} %collective-permute-done.4.refs_4_), channel_id=1, source_target_pairs={{0,1},{1,2},{2,3},{3,0},{4,5},{5,6},{6,7},{7,4},{8,9},{9,10},{10,1... | collective-permute-start | bytes 884744 | tf_op jit(solution)/shard_map/ppermute | solution.py:26
  22.0 8.6 %collective-permute-start.2 = (bf16[192,768]{1,0:T(8,128)(2,1)S(1)}, bf16[192,768]{1,0:T(8,128)(2,1)S(1)}, u32[]{:S(2)}, u32[]{:S(2)}) collective-permute-start(bf16[192,768]{1,0:T(8,128)(2,1)S(1)} %collective-permute-done.1.refs_2_), channel_id=1, source_target_pairs={{0,3},{1,0},{2,1},{3,2},{4,7},{5,4},{6,5},{7,6},{8,11},{9,8},{10,9... | collective-permute-start | bytes 884744 | tf_op jit(solution)/shard_map/ppermute | solution.py:26
  34.3 27.5 %collective-permute-start.11 = (bf16[3,200,768]{2,1,0:T(8,128)(2,1)S(1)}, bf16[3,200,768]{2,1,0:T(8,128)(2,1)S(1)}, u32[]{:S(2)}, u32[]{:S(2)}) collective-permute-start(bf16[3,200,768]{2,1,0:T(8,128)(2,1)S(1)} %stack_tiles.1.refs_0_), channel_id=1, source_target_pairs={{0,8},{8,0},{1,9},{9,1},{2,10},{10,2},{3,11},{11,3},{4,12},{12,4},... | collective-permute-start | bytes 2764808 | tf_op jit(solution)/shard_map/ppermute | solution.py:34
  37.7 18.4 %collective-permute-start.8 = (bf16[200,768]{1,0:T(8,128)(2,1)S(1)}, bf16[200,768]{1,0:T(8,128)(2,1)S(1)}, u32[]{:S(2)}, u32[]{:S(2)}) collective-permute-start(bf16[200,768]{1,0:T(8,128)(2,1)S(1)} %arrange_tiles.1.refs_0_), channel_id=1, source_target_pairs={{0,36},{4,32},{16,52},{20,48},{32,4},{36,0},{48,20},{52,16},{1,37}... | collective-permute-start | bytes 921608 | tf_op jit(solution)/shard_map/ppermute | solution.py:46
  38.8 6.4 %collective-permute-start.13 = (bf16[2,48,384]{2,1,0:T(8,128)(2,1)S(1)}, bf16[2,48,384]{2,1,0:T(8,128)(2,1)S(1)}, u32[]{:S(2)}, u32[]{:S(2)}) collective-permute-start(bf16[2,48,384]{2,1,0:T(8,128)(2,1)S(1)} %get-tuple-element.27), channel_id=1, source_target_pairs={{0,16},{4,52},{16,32},{20,4},{32,48},{36,20},{48,0},{52,36},{1,17}... | collective-permute-start | bytes 221192 | tf_op jit(solution)/shard_map/ppermute | solution.py:55
  40.0 15.2 %collective-permute-start.15 = (bf16[2,48,384]{2,1,0:T(8,128)(2,1)S(1)}, bf16[2,48,384]{2,1,0:T(8,128)(2,1)S(1)}, u32[]{:S(2)}, u32[]{:S(2)}) collective-permute-start(bf16[2,48,384]{2,1,0:T(8,128)(2,1)S(1)} %get-tuple-element.28), channel_id=1, source_target_pairs={{0,48},{4,20},{16,0},{20,36},{32,16},{36,52},{48,32},{52,4},{1,49}... | collective-permute-start | bytes 221192 | tf_op jit(solution)/shard_map/ppermute | solution.py:55
  42.4 19.4 %collective-permute-start.12 = (bf16[2,48,384]{2,1,0:T(8,128)(2,1)S(1)}, bf16[2,48,384]{2,1,0:T(8,128)(2,1)S(1)}, u32[]{:S(2)}, u32[]{:S(2)}) collective-permute-start(bf16[2,48,384]{2,1,0:T(8,128)(2,1)S(1)} %get-tuple-element.26.after.refs_2_), channel_id=1, source_target_pairs={{0,8},{8,0},{1,9},{9,1},{2,10},{10,2},{3,11},{11,3},{4,12},{12,4},... | collective-permute-start | bytes 221192 | tf_op jit(solution)/shard_map/ppermute | solution.py:34
  45.2 16.6 %collective-permute-start.14 = (bf16[2,48,384]{2,1,0:T(8,128)(2,1)S(1)}, bf16[2,48,384]{2,1,0:T(8,128)(2,1)S(1)}, u32[]{:S(2)}, u32[]{:S(2)}) collective-permute-start(bf16[2,48,384]{2,1,0:T(8,128)(2,1)S(1)} %collective-permute-done.13.refs_4_), channel_id=1, source_target_pairs={{0,8},{8,0},{1,9},{9,1},{2,10},{10,2},{3,11},{11,3},{4,12},{12,4},... | collective-permute-start | bytes 221192 | tf_op jit(solution)/shard_map/ppermute | solution.py:34
  55.2 6.6 %collective-permute-start.16 = (bf16[2,48,384]{2,1,0:T(8,128)(2,1)S(1)}, bf16[2,48,384]{2,1,0:T(8,128)(2,1)S(1)}, u32[]{:S(2)}, u32[]{:S(2)}) collective-permute-start(bf16[2,48,384]{2,1,0:T(8,128)(2,1)S(1)} %collective-permute-done.15.refs_6_), channel_id=1, source_target_pairs={{0,8},{8,0},{1,9},{9,1},{2,10},{10,2},{3,11},{11,3},{4,12},{12,4},... | collective-permute-start | bytes 221192 | tf_op jit(solution)/shard_map/ppermute | solution.py:34
  56.1 12.0 %collective-permute-start.7 = (bf16[2,48,384]{2,1,0:T(8,128)(2,1)S(1)}, bf16[2,48,384]{2,1,0:T(8,128)(2,1)S(1)}, u32[]{:S(2)}, u32[]{:S(2)}) collective-permute-start(bf16[2,48,384]{2,1,0:T(8,128)(2,1)S(1)} %get-tuple-element.25), channel_id=1, source_target_pairs={{0,32},{4,36},{16,48},{20,52},{32,0},{36,4},{48,16},{52,20},{1,33}... | collective-permute-start | bytes 221192 | tf_op jit(solution)/shard_map/ppermute | solution.py:55
  68.1 1.8 %collective-permute-start.17 = (bf16[200,768]{1,0:T(8,128)(2,1)S(1)}, bf16[200,768]{1,0:T(8,128)(2,1)S(1)}, u32[]{:S(2)}, u32[]{:S(2)}) collective-permute-start(bf16[200,768]{1,0:T(8,128)(2,1)S(1)} %collective-permute-done.8.refs_8_.refs_0_), channel_id=1, source_target_pairs={{0,8},{8,0},{1,9},{9,1},{2,10},{10,2},{3,11},{11,3},{4,12},{12,4},... | collective-permute-start | bytes 921608 | tf_op jit(solution)/shard_map/ppermute | solution.py:34
  68.5 1.4 %collective-permute-start.18 = (bf16[2,48,384]{2,1,0:T(8,128)(2,1)S(1)}, bf16[2,48,384]{2,1,0:T(8,128)(2,1)S(1)}, u32[]{:S(2)}, u32[]{:S(2)}) collective-permute-start(bf16[2,48,384]{2,1,0:T(8,128)(2,1)S(1)} %collective-permute-done.7.refs_2_), channel_id=1, source_target_pairs={{0,8},{8,0},{1,9},{9,1},{2,10},{10,2},{3,11},{11,3},{4,12},{12,4},... | collective-permute-start | bytes 221192 | tf_op jit(solution)/shard_map/ppermute | solution.py:34
  72.6 10.0 %collective-permute-start.19 = (bf16[384,384]{1,0:T(8,128)(2,1)S(1)}, bf16[384,384]{1,0:T(8,128)(2,1)S(1)}, u32[]{:S(2)}, u32[]{:S(2)}) collective-permute-start(bf16[384,384]{1,0:T(8,128)(2,1)S(1)} %get-tuple-element.34), channel_id=1, source_target_pairs={{0,128},{64,192},{128,0},{192,64},{1,129},{65,193},{129,1},{193,65... | collective-permute-start | bytes 884744 | tf_op jit(solution)/shard_map/ppermute | solution.py:38
  75.6 13.8 %collective-permute-start.20 = (bf16[384,384]{1,0:T(8,128)(2,1)S(1)}, bf16[384,384]{1,0:T(8,128)(2,1)S(1)}, u32[]{:S(2)}, u32[]{:S(2)}) collective-permute-start(bf16[384,384]{1,0:T(8,128)(2,1)S(1)} %get-tuple-element.36), channel_id=1, source_target_pairs={{0,64},{64,128},{128,192},{192,0},{1,65},{65,129},{129,193},{193,1... | collective-permute-start | bytes 884744 | tf_op jit(solution)/shard_map/ppermute | solution.py:38
  76.0 13.5 %collective-permute-start.21 = (bf16[384,384]{1,0:T(8,128)(2,1)S(1)}, bf16[384,384]{1,0:T(8,128)(2,1)S(1)}, u32[]{:S(2)}, u32[]{:S(2)}) collective-permute-start(bf16[384,384]{1,0:T(8,128)(2,1)S(1)} %get-tuple-element.37), channel_id=1, source_target_pairs={{0,192},{64,0},{128,64},{192,128},{1,193},{65,1},{129,65},{193,129... | collective-permute-start | bytes 884744 | tf_op jit(solution)/shard_map/ppermute | solution.py:38
  91.4 21.3 %copy-start.3 = (f32[8,24,768]{2,1,0:T(8,128)S(1)}, f32[8,24,768]{2,1,0:T(8,128)}, u32[]{:S(2)}) copy-start(f32[8,24,768]{2,1,0:T(8,128)} %param.14) | copy-start | bytes 1769476
  91.4 21.3 %all-to-all-start = ((bf16[32,24,192]{2,1,0:T(8,128)(2,1)}), bf16[32,24,192]{2,1,0:T(8,128)(2,1)S(1)}, u32[]{:S(2)}, u32[]{:S(2)}) async-start(bf16[32,24,192]{2,1,0:T(8,128)(2,1)} %get-tuple-element.44), calls=%async_computation | async-start | bytes 786432 | tf_op jit(solution)/shard_map/all_to_all | solution.py:416
  98.1 1.9 %collective-permute-start.22 = (bf16[4,48,384]{2,1,0:T(8,128)(2,1)S(1)}, bf16[4,48,384]{2,1,0:T(8,128)(2,1)S(1)}, u32[]{:S(2)}, u32[]{:S(2)}) collective-permute-start(bf16[4,48,384]{2,1,0:T(8,128)(2,1)S(1)} %get-tuple-element.39), channel_id=1, source_target_pairs={{0,8},{8,0},{1,9},{9,1},{2,10},{10,2},{3,11},{11,3},{4,12},{12,4},... | collective-permute-start | bytes 442376 | tf_op jit(solution)/shard_map/ppermute | solution.py:34
  100.4 7.5 %collective-permute-start.23 = (bf16[2,48,384]{2,1,0:T(8,128)(2,1)S(1)}, bf16[2,48,384]{2,1,0:T(8,128)(2,1)S(1)}, u32[]{:S(2)}, u32[]{:S(2)}) collective-permute-start(bf16[2,48,384]{2,1,0:T(8,128)(2,1)S(1)} %get-tuple-element.40), channel_id=1, source_target_pairs={{0,32},{4,36},{16,48},{20,52},{32,0},{36,4},{48,16},{52,20},{1,33}... | collective-permute-start | bytes 221192 | tf_op jit(solution)/shard_map/ppermute | solution.py:55
  103.3 5.9 %collective-permute-start.24 = (bf16[2,48,384]{2,1,0:T(8,128)(2,1)S(1)}, bf16[2,48,384]{2,1,0:T(8,128)(2,1)S(1)}, u32[]{:S(2)}, u32[]{:S(2)}) collective-permute-start(bf16[2,48,384]{2,1,0:T(8,128)(2,1)S(1)} %get-tuple-element.42), channel_id=1, source_target_pairs={{0,16},{4,52},{16,32},{20,4},{32,48},{36,20},{48,0},{52,36},{1,17}... | collective-permute-start | bytes 221192 | tf_op jit(solution)/shard_map/ppermute | solution.py:55
  104.0 8.7 %collective-permute-start.25 = (bf16[2,48,384]{2,1,0:T(8,128)(2,1)S(1)}, bf16[2,48,384]{2,1,0:T(8,128)(2,1)S(1)}, u32[]{:S(2)}, u32[]{:S(2)}) collective-permute-start(bf16[2,48,384]{2,1,0:T(8,128)(2,1)S(1)} %get-tuple-element.43), channel_id=1, source_target_pairs={{0,48},{4,20},{16,0},{20,36},{32,16},{36,52},{48,32},{52,4},{1,49}... | collective-permute-start | bytes 221192 | tf_op jit(solution)/shard_map/ppermute | solution.py:55
